TPU v7x, 32 devices: a whole 2x2x4 slice. The times are simulated.
32 devices in a mesh: area: 8 (over z, x), scen: 4 (over y, core).
Axes of the slice: x: 2, y: 2, z: 4, core: 2. Of those that a mesh axis runs over, the one named last changes fastest.
Arguments:
- injection: float32 [8, 128, 4096], P('area', 'scen'), may hold values from -6 to 6
- kkt_factor: bfloat16 [8, 4096, 4096], P('area', 'scen'), may hold values from -0.09375 to 0.09375
- dual_price: float32 [8, 128, 512], P('area', 'scen'), may hold values from -6 to 6
- area_size: int32 [8], replicated, may hold values from 1024 to 4096, as said below
- bnd_bus: int32 [8, 512], replicated, may hold values from 0 to 4095, as said below
- peer_end: int32 [8, 512], replicated, may hold values from 0 to 4095, as said below
Outputs:
- angles: float32 [8, 128, 4096], P('area', 'scen')
- dual_out: float32 [8, 128, 512], P('area', 'scen')
- consensus: float32 [8, 128, 512], P('area', 'scen')
Inputs may be any that keep to these rules, and one draw needn't show every extreme that they name: `area_size`: one area has exactly 4096 live buses and another exactly 1024. `bnd_bus`: the buses of one area's ends are distinct and lie below that area's size; they include bus 0 and the area's last live bus. peer_end is a pairing: the peer of an end's peer is the end itself, and the two ends lie in different areas. The ends of area a form 4 tie sets of 128 consecutive ends; tie set g of area a is paired whole with tie set g of area a XOR s_g, where s_g is nonzero, the same for all areas, and the 4 values s_g differ.
All inputs are finite; a program needn't handle non-finite values.
Results may differ from a plain program's by a relative error of at most 0.0043.
Values may be sent and summed in bfloat16 or wider, within the bound.
No kernel may reach another device: no remote copies, remote signals or barrier semaphores. Data moves between devices by JAX's collectives and lax.ppermute only.
A program may use at most 128 MiB of HBM per device.

v0:
```python
import jax
import jax.numpy as jnp
from jax import lax
from jax.experimental import pallas as pl
from jax.experimental.pallas import tpu as pltpu
from jax.sharding import PartitionSpec as P


CAP = 128
PENALTY = 1.5
PROXIMAL = 0.5
DENOM = 2.0 * PENALTY + PROXIMAL
SUBLANES = 16

F32 = jnp.float32
BF16 = jnp.bfloat16

WHOLE = pl.BlockSpec(memory_space=pltpu.VMEM)
SCALARS = pl.BlockSpec(memory_space=pltpu.SMEM)


def dot_nt(a, b):
    return lax.dot_general(a, b, (((1,), (1,)), ((), ())), preferred_element_type=F32)


def dot_tn(a, b):
    return lax.dot_general(a, b, (((0,), (0,)), ((), ())), preferred_element_type=F32)


def dot_nn(a, b):
    return jnp.dot(a, b, preferred_element_type=F32)


def swap(x, axis, bit):
    n = lax.axis_size(axis)
    return lax.ppermute(x, axis, [(i, i ^ bit) for i in range(n)])


def halves(x):
    high = x.astype(BF16)
    return high, (x - high.astype(F32)).astype(BF16)


def out(shape, dtype):
    return jax.ShapeDtypeStruct(shape, dtype)


def live_rows(area_size, band_rows, shape, axis):
    start = lax.axis_index("scen") * band_rows
    return start + lax.broadcasted_iota(jnp.int32, shape, axis) < area_size[lax.axis_index("area")]


def plain_kernel(area_size, injection, plain):
    live = lax.broadcasted_iota(jnp.int32, injection.shape, 1) < area_size[lax.axis_index("area")]
    plain[...] = jnp.where(live, injection[...], 0.0).astype(BF16)


def plain_side(area_size, injection):
    return pl.pallas_call(
        plain_kernel,
        out_shape=out(injection.shape, BF16),
        in_specs=[SCALARS, WHOLE],
        out_specs=WHOLE,
    )(area_size, injection)


def ends_kernel(area_size, bnd_bus, factor, factor_ends, gram, squares, total):
    step = pl.program_id(0)
    rows, depth = factor.shape
    ends_total = bnd_bus.shape[1]

    @pl.when(step == 0)
    def _():
        total[...] = jnp.zeros_like(total)

    buses = bnd_bus[pl.ds(lax.axis_index("area"), 1), :] - step * depth
    pick = lax.broadcasted_iota(jnp.int32, (depth, ends_total), 0) == buses
    total[...] += dot_nn(factor[...], jnp.where(pick, 1.0, 0.0).astype(BF16))

    @pl.when(step == pl.num_programs(0) - 1)
    def _():
        live = live_rows(area_size, rows, total.shape, 0)
        columns = jnp.where(live, total[...], 0.0).astype(BF16)
        factor_ends[...] = columns
        product = dot_tn(columns, columns)
        square = (ends_total, ends_total)
        diag = lax.broadcasted_iota(jnp.int32, square, 0) == lax.broadcasted_iota(
            jnp.int32, square, 1
        )
        squares[...] = jnp.sum(jnp.where(diag, product, 0.0), axis=0, keepdims=True)
        gram[...] = jnp.where(diag, 0.0, product)


def ends_columns(area_size, bnd_bus, factor):
    rows, width = factor.shape
    ends_total = bnd_bus.shape[1]
    depth = 512
    return pl.pallas_call(
        ends_kernel,
        grid=(width // depth,),
        out_shape=(
            out((rows, ends_total), BF16),
            out((ends_total, ends_total), F32),
            out((1, ends_total), F32),
        ),
        in_specs=[SCALARS, WHOLE, pl.BlockSpec((rows, depth), lambda i: (0, i))],
        out_specs=(
            pl.BlockSpec((rows, ends_total), lambda i: (0, 0)),
            pl.BlockSpec((ends_total, ends_total), lambda i: (0, 0)),
            pl.BlockSpec((1, ends_total), lambda i: (0, 0)),
        ),
        scratch_shapes=[pltpu.VMEM((rows, ends_total), F32)],
    )(area_size, bnd_bus, factor)


def base_kernel(
    area_size, near, far, small_near, small_far, factor, factor_ends, base, partial, side, small
):
    step = pl.program_id(0)
    half = near.shape[0]
    ends_total = small.shape[1] // 2

    @pl.when(step == 0)
    def _():
        side[:half] = near[...]
        side[half:] = far[...]
        small[:half] = small_near[...]
        small[half:] = small_far[...]
        partial[...] = jnp.zeros_like(partial)

    here = factor_ends[...]
    value = dot_nt(side[...], factor[...]) - dot_nt(small[:, ends_total:], here)
    start = lax.axis_index("scen") * (pl.num_programs(0) * here.shape[0]) + step * here.shape[0]
    live = start + lax.broadcasted_iota(jnp.int32, value.shape, 1) < area_size[lax.axis_index("area")]
    value = jnp.where(live, value, 0.0)
    base[...] = value
    first = (value + dot_nt(small[:, :ends_total], here)).astype(BF16)
    partial[...] += PENALTY * dot_nn(first, here)


def base_product(area_size, near, far, small_near, small_far, factor, factor_ends):
    rows, width = factor.shape
    ends_total = factor_ends.shape[1]
    count = 2 * near.shape[0]
    block = 256
    return pl.pallas_call(
        base_kernel,
        grid=(rows // block,),
        out_shape=(out((count, rows), F32), out((count, ends_total), F32)),
        in_specs=[
            SCALARS,
            WHOLE,
            WHOLE,
            WHOLE,
            WHOLE,
            pl.BlockSpec((block, width), lambda i: (i, 0)),
            pl.BlockSpec((block, ends_total), lambda i: (i, 0)),
        ],
        out_specs=(
            pl.BlockSpec((count, block), lambda i: (0, i)),
            pl.BlockSpec((count, ends_total), lambda i: (0, 0)),
        ),
        scratch_shapes=[
            pltpu.VMEM((count, width), BF16),
            pltpu.VMEM((count, 2 * ends_total), BF16),
        ],
    )(area_size, near, far, small_near, small_far, factor, factor_ends)


def second_kernel(base, near, far, factor_ends, factor, second, keep, send, right):
    half = near.shape[0]

    @pl.when(pl.program_id(0) == 0)
    def _():
        right[:half] = near[...]
        right[half:] = far[...]
        second[...] = (base[...] + dot_nt(right[...], factor_ends[...])).astype(BF16)

    value = dot_nn(second[...], factor[...])
    keep[...] = value[:half]
    send[...] = value[half:].astype(BF16)


def angles_specs(half, depth, rows, width, parts, part):
    steps = width // parts // depth
    spec = pl.BlockSpec((half, depth), lambda i: (0, i))
    shapes = (out((half, width // parts), F32), out((half, width // parts), BF16))
    return steps, pl.BlockSpec((rows, depth), lambda i: (0, part * steps + i)), spec, shapes


def second_product(base, near, far, factor_ends, factor, parts):
    rows, width = factor.shape
    half = near.shape[0]
    steps, factor_spec, spec, shapes = angles_specs(half, 512, rows, width, parts, 0)
    return pl.pallas_call(
        second_kernel,
        grid=(steps,),
        out_shape=(out((2 * half, rows), BF16),) + shapes,
        in_specs=[WHOLE, WHOLE, WHOLE, WHOLE, factor_spec],
        out_specs=(pl.BlockSpec((2 * half, rows), lambda i: (0, 0)), spec, spec),
        scratch_shapes=[pltpu.VMEM((2 * half, near.shape[1]), BF16)],
    )(base, near, far, factor_ends, factor)


def angles_kernel(second, factor, keep, send):
    half = keep.shape[0]
    value = dot_nn(second[...], factor[...])
    keep[...] = value[:half]
    send[...] = value[half:].astype(BF16)


def angles_product(second, factor, parts, part):
    rows, width = factor.shape
    half = second.shape[0] // 2
    steps, factor_spec, spec, shapes = angles_specs(half, 512, rows, width, parts, part)
    return pl.pallas_call(
        angles_kernel,
        grid=(steps,),
        out_shape=shapes,
        in_specs=[WHOLE, factor_spec],
        out_specs=(spec, spec),
    )(second, factor)


def shards(injection, kkt_factor, dual_price, area_size, bnd_bus, peer_end):
    area_id = lax.axis_index("area")
    band_index = lax.axis_index("scen")
    areas_all = lax.axis_size("area")
    factor = kkt_factor[0]
    _, width = factor.shape
    injection_here = injection[0]
    dual_here = dual_price[0]
    columns, ends_total = dual_here.shape
    buses = bnd_bus[area_id]
    peers = peer_end[area_id]
    offset = (peers // ends_total) ^ area_id

    plain = plain_side(area_size, injection_here)
    other = swap(plain, "scen", 2)
    pair = jnp.concatenate([plain, other], axis=0)
    pair_far = swap(pair, "scen", 1)
    at_ends = injection_here[:, buses]
    at_ends_high, at_ends_low = halves(at_ends)
    first_here = (at_ends - dual_here).astype(BF16)
    small = jnp.concatenate([first_here, at_ends_high, at_ends_low], axis=1)
    small_pair = jnp.concatenate([small, swap(small, "scen", 2)], axis=0)
    small_send = small_pair[:, : 2 * ends_total]
    small_far = swap(small_send, "scen", 1)
    at_ends_pair = small_pair[:, ends_total : 2 * ends_total].astype(F32)
    at_ends_pair = at_ends_pair + small_pair[:, 2 * ends_total :].astype(F32)

    factor_ends, gram, squares = ends_columns(area_size, bnd_bus, factor)
    slots = jnp.arange(ends_total)
    half = ends_total // 2
    side = band_index % 2

    def with_squares(rows, squares):
        high, low = halves(squares)
        blank = jnp.zeros((SUBLANES - 2, ends_total), BF16)
        return jnp.concatenate([rows.astype(BF16), high, low, blank], axis=0)

    def add_gram(rows, squares, incoming):
        incoming = incoming.astype(F32)
        return rows + incoming[:half], squares + incoming[half : half + 1] + incoming[half + 1 : half + 2]

    gram_keep = lax.dynamic_slice_in_dim(gram, side * half, half, 0)
    gram_send = lax.dynamic_slice_in_dim(gram, (1 - side) * half, half, 0)
    gram_keep, squares = add_gram(
        gram_keep, squares, swap(with_squares(gram_send, squares), "scen", 1)
    )
    gram_keep, squares = add_gram(
        gram_keep, squares, swap(with_squares(gram_keep, squares), "scen", 2)
    )
    gram_keep = gram_keep.astype(BF16)
    gram_other = swap(gram_keep, "scen", 1)
    gram_all = jnp.where(
        side == 0,
        jnp.concatenate([gram_keep, gram_other], axis=0),
        jnp.concatenate([gram_other, gram_keep], axis=0),
    )
    mate = ((slots // CAP * CAP + peers % CAP)[None, :] == slots[:, None]).astype(BF16)

    base, partial = base_product(
        area_size, pair, pair_far, small_send, small_far, factor, factor_ends
    )

    def exchange(q):
        moved = q
        bit = 1
        while bit < areas_all:
            moved = jnp.where((offset & bit)[None, :] != 0, swap(moved, "area", bit), moved)
            bit *= 2
        return dot_nn(moved, mate)

    def with_low(x, low_rows):
        high, low = halves(x)
        return jnp.concatenate([high, low[low_rows]], axis=0)

    pair_rows = 2 * columns
    keep = partial[:pair_rows] + swap(partial[pair_rows:], "scen", 1)
    keep = keep + jnp.concatenate([dual_here, jnp.zeros_like(dual_here)], axis=0)
    first_rows, last_rows = slice(0, columns), slice(columns, pair_rows)
    other = swap(with_low(keep, last_rows), "scen", 2).astype(F32)
    q = keep + jnp.concatenate([other[last_rows] + other[pair_rows:], other[first_rows]], axis=0)
    moved = exchange(with_low(q, first_rows))
    moved = jnp.concatenate([moved[first_rows] + moved[pair_rows:], moved[last_rows]], axis=0)
    consensus = (q + moved) / DENOM
    spread = q - 2.0 * PENALTY * consensus
    second_pair = (at_ends_pair - spread).astype(BF16)
    second_far = swap(second_pair, "scen", 1)

    q_own, consensus_own = q[:columns], consensus[:columns]
    change = second_pair[:columns].astype(F32) - first_here.astype(F32)
    change_high, change_low = halves(change)
    ends_scaled = (q_own - dual_here) + PENALTY * (
        change * squares + dot_nn(change_high, gram_all) + dot_nn(change_low, gram_all)
    )
    q_last = ends_scaled + (q_own - PENALTY * consensus_own)
    moved = exchange(with_low(q_last, first_rows))
    moved = moved[first_rows] + moved[last_rows]
    consensus_last = (q_last + moved + PROXIMAL * consensus_own) / DENOM
    dual_last = q_last - PENALTY * consensus_last

    parts = 2
    second, keep, send = second_product(base, second_pair, second_far, factor_ends, factor, parts)
    pieces = []
    for part in range(parts):
        if part:
            keep, send = angles_product(second, factor, parts, part)
        keep = keep + swap(send, "scen", 1).astype(F32)
        pieces.append(keep[:columns] + swap(keep[columns:].astype(BF16), "scen", 2).astype(F32))
    live_mask = jnp.arange(width) < area_size[area_id]
    angles_here = jnp.where(live_mask, jnp.concatenate(pieces, axis=1), 0.0)
    return (angles_here[None], dual_last[None], consensus_last[None])


def solution(mesh):
    spec = P("area", "scen", None)
    return jax.shard_map(
        shards,
        mesh=mesh,
        in_specs=(spec, spec, spec, P(), P(), P()),
        out_specs=(spec, spec, spec),
        check_vma=False,
    )
```

profile of v0, /device:TPU:0, one launch (start us, length us, event | category | flops | bytes accessed | tf_op | source)
XLA Modules:
  0.0 99.1 jit_solution(10323830517261246866)
XLA Ops:
  0.6 11.2 %shard_map.86 = (bf16[1024,512]{1,0:T(8,128)(2,1)}, f32[512,512]{1,0:T(8,128)}, f32[1,512]{1,0:T(1,128)}) custom-call(s32[8]{0:T(128)} %area_size.5, s32[8,512]{1,0:T(8,128)} %bnd_bus.1, bf16[1024,4096]{1,0:T(8,128)(2,1)} %bitcast.28), custom_call_target="tpu_custom_call" | custom-call | tf_op jit(solution)/shard_map/pallas_call | solution.py:98
  11.8 0.8 fusion.33
  12.6 1.1 %dynamic-slice_convert_fusion = bf16[256,512]{1,0:T(8,128)(2,1)S(1)} fusion(f32[512,512]{1,0:T(8,128)} %get-tuple-element.22, s32[]{:T(128)S(6)} %select_n.102), kind=kLoop, calls=%fused_computation.13 | loop fusion | bytes 524292 | tf_op jit(solution)/shard_map/convert_element_type | solution.py:260
  13.7 0.1 pad.14.clone
  13.7 0.8 maximum_maximum_fusion
  14.6 0.5 collective-permute-start.14
  15.1 1.8 %shard_map.85 = bf16[32,4096]{1,0:T(8,128)(2,1)} custom-call(s32[8]{0:T(128)} %area_size.5, f32[32,4096]{1,0:T(8,128)} %bitcast.32), custom_call_target="tpu_custom_call" | custom-call | tf_op jit(solution)/shard_map/pallas_call | solution.py:59
  16.9 2.5 %collective-permute-start = (bf16[32,4096]{1,0:T(8,128)(2,1)}, bf16[32,4096]{1,0:T(8,128)(2,1)}, u32[]{:S(2)}, u32[]{:S(2)}) collective-permute-start(bf16[32,4096]{1,0:T(8,128)(2,1)} %shard_map.85), channel_id=1, source_target_pairs={{0,2},{1,3},{2,0},{3,1},{4,6},{5,7},{6,4},{7,5},{8,10},{9,11},{10,... | collective-permute-start | bytes 786440 | tf_op jit(solution)/shard_map/ppermute | solution.py:36
  19.4 0.6 copy.11
  20.0 0.8 compare_select_fusion
  20.9 1.7 %gather_fusion = f32[512,32]{1,0:T(8,128)} fusion(f32[32,4096]{0,1:T(8,128)S(1)} %copy.11, s32[1024]{0:T(1024)S(1)} %pad_clamp_fusion), kind=kCustom, calls=%fused_computation | custom fusion | bytes 133120 | tf_op jit(solution)/shard_map/gather | solution.py:242
  22.5 1.0 %copy.12 = f32[512,32]{0,1:T(8,128)S(1)} copy(f32[512,32]{1,0:T(8,128)} %gather_fusion) | data formatting | bytes 131072 | tf_op jit(solution)/shard_map/gather | solution.py:242
  23.6 0.0 copy-start.12
  23.6 0.1 collective-permute-start.2
  23.7 0.7 fusion.26
  24.5 2.5 %collective-permute-done = bf16[32,4096]{1,0:T(8,128)(2,1)} collective-permute-done((bf16[32,4096]{1,0:T(8,128)(2,1)}, bf16[32,4096]{1,0:T(8,128)(2,1)}, u32[]{:S(2)}, u32[]{:S(2)}) %collective-permute-start) | collective-permute-done | bytes 262176 | tf_op jit(solution)/shard_map/ppermute | solution.py:36
  27.0 1.0 pad_maximum_fusion.near
  28.0 0.1 collective-permute-start.1
  28.0 0.8 collective-permute-done.2
  28.8 0.1 collective-permute-start.3
  28.9 1.0 %convert_element_type.138 = f32[272,512]{1,0:T(8,128)S(1)} convert(bf16[272,512]{1,0:T(8,128)(2,1)} %collective-permute-done.14) | non-fusion elementwise | flops 139264 | bytes 835584 | tf_op jit(solution)/shard_map/convert_element_type | solution.py:263
  30.0 0.1 fusion.9
  30.1 0.2 collective-permute-done.3.small_far
  30.3 0.6 copy-done.10
  30.9 0.2 copy-done.7
  31.1 8.0 %shard_map.87 = (f32[128,1024]{1,0:T(8,128)}, f32[128,512]{1,0:T(8,128)}) custom-call(s32[8]{0:T(128)} %area_size.5, bf16[64,4096]{1,0:T(8,128)(2,1)} %copy-done.1, bf16[64,4096]{1,0:T(8,128)(2,1)} %copy-done.7, bf16[64,1024]{1,0:T(8,128)(2,1)} %copy-done.4, bf16[64,1024]{1,0:T(8,128)(2,1)} %copy-done.10, bf16[1024,4096]{1,0:T(8,128)(2,1)} %bitcast.29, ...), custom_call_target="tpu_custom_call" | custom-call | tf_op jit(solution)/shard_map/pallas_call | solution.py:146
  39.1 0.9 slice.90
  40.0 0.4 collective-permute-start.4
  40.4 1.0 %collective-permute-done.4 = f32[64,512]{1,0:T(8,128)S(1)} collective-permute-done((f32[64,512]{1,0:T(8,128)S(1)}, f32[64,512]{1,0:T(8,128)S(1)}, u32[]{:S(2)}, u32[]{:S(2)}) %collective-permute-start.4) | collective-permute-done | bytes 131104 | tf_op jit(solution)/shard_map/ppermute | solution.py:36
  41.5 0.9 fusion.31
  42.4 1.9 %collective-permute-start.5 = (bf16[96,512]{1,0:T(8,128)(2,1)S(1)}, bf16[96,512]{1,0:T(8,128)(2,1)S(1)}, u32[]{:S(2)}, u32[]{:S(2)}) collective-permute-start(bf16[96,512]{1,0:T(8,128)(2,1)S(1)} %pad_maximum_fusion.3), channel_id=1, source_target_pairs={{0,2},{1,3},{2,0},{3,1},{4,6},{5,7},{6,4},{7,5},{8,10},{9,11},{10,... | collective-permute-start | bytes 294920 | tf_op jit(solution)/shard_map/ppermute | solution.py:36
  44.3 0.1 maximum_maximum_fusion.1
  44.5 0.3 collective-permute-start.15
  44.7 3.3 %collective-permute-done.5 = bf16[96,512]{1,0:T(8,128)(2,1)S(1)} collective-permute-done((bf16[96,512]{1,0:T(8,128)(2,1)S(1)}, bf16[96,512]{1,0:T(8,128)(2,1)S(1)}, u32[]{:S(2)}, u32[]{:S(2)}) %collective-permute-start.5) | collective-permute-done | bytes 98336 | tf_op jit(solution)/shard_map/ppermute | solution.py:36
  48.1 1.8 %collective-permute-start.6 = (bf16[96,512]{1,0:T(8,128)(2,1)S(1)}, bf16[96,512]{1,0:T(8,128)(2,1)S(1)}, u32[]{:S(2)}, u32[]{:S(2)}) collective-permute-start(bf16[96,512]{1,0:T(8,128)(2,1)S(1)} %pad_maximum_fusion.4), channel_id=1, source_target_pairs={{0,4},{4,0},{8,12},{12,8},{16,20},{20,16},{24,28},{28,24},{1,5},{5... | collective-permute-start | bytes 294920 | tf_op jit(solution)/shard_map/ppermute | solution.py:36
  50.0 3.5 %collective-permute-done.15 = bf16[272,512]{1,0:T(8,128)(2,1)S(1)} collective-permute-done((bf16[272,512]{1,0:T(8,128)(2,1)S(1)}, bf16[272,512]{1,0:T(8,128)(2,1)S(1)}, u32[]{:S(2)}, u32[]{:S(2)}) %collective-permute-start.15) | collective-permute-done | bytes 278560 | tf_op jit(solution)/shard_map/ppermute | solution.py:36
  53.5 0.1 convert_element_type.143
  53.6 1.8 %collective-permute-start.7 = (bf16[96,512]{1,0:T(8,128)(2,1)S(1)}, bf16[96,512]{1,0:T(8,128)(2,1)S(1)}, u32[]{:S(2)}, u32[]{:S(2)}) collective-permute-start(bf16[96,512]{1,0:T(8,128)(2,1)S(1)} %broadcast_select_fusion), channel_id=1, source_target_pairs={{0,8},{4,12},{8,0},{12,4},{16,24},{20,28},{24,16},{28,20},{1,9},{5... | collective-permute-start | bytes 294920 | tf_op jit(solution)/shard_map/ppermute | solution.py:36
  55.4 0.2 fusion.4
  55.6 2.7 %collective-permute-done.7 = bf16[96,512]{1,0:T(8,128)(2,1)S(1)} collective-permute-done((bf16[96,512]{1,0:T(8,128)(2,1)S(1)}, bf16[96,512]{1,0:T(8,128)(2,1)S(1)}, u32[]{:S(2)}, u32[]{:S(2)}) %collective-permute-start.7) | collective-permute-done | bytes 98336 | tf_op jit(solution)/shard_map/ppermute | solution.py:36
  58.3 2.8 %collective-permute-start.8 = (bf16[96,512]{1,0:T(8,128)(2,1)S(1)}, bf16[96,512]{1,0:T(8,128)(2,1)S(1)}, u32[]{:S(2)}, u32[]{:S(2)}) collective-permute-start(bf16[96,512]{1,0:T(8,128)(2,1)S(1)} %broadcast_select_fusion.1), channel_id=1, source_target_pairs={{0,16},{4,20},{8,24},{12,28},{16,0},{20,4},{24,8},{28,12},{1,17},{... | collective-permute-start | bytes 294920 | tf_op jit(solution)/shard_map/ppermute | solution.py:36
  61.1 2.7 %collective-permute-done.8 = bf16[96,512]{1,0:T(8,128)(2,1)S(1)} collective-permute-done((bf16[96,512]{1,0:T(8,128)(2,1)S(1)}, bf16[96,512]{1,0:T(8,128)(2,1)S(1)}, u32[]{:S(2)}, u32[]{:S(2)}) %collective-permute-start.8) | collective-permute-done | bytes 98336 | tf_op jit(solution)/shard_map/ppermute | solution.py:36
  63.9 0.3 fusion.3
  64.3 0.0 copy-start.8
  64.3 0.2 fusion.12
  64.5 0.3 fusion.32
  64.8 1.7 %collective-permute-start.17 = (bf16[64,512]{1,0:T(8,128)(2,1)S(1)}, bf16[64,512]{1,0:T(8,128)(2,1)S(1)}, u32[]{:S(2)}, u32[]{:S(2)}) collective-permute-start(bf16[64,512]{1,0:T(8,128)(2,1)S(1)} %pad_maximum_fusion.5), channel_id=1, source_target_pairs={{0,4},{4,0},{8,12},{12,8},{16,20},{20,16},{24,28},{28,24},{1,5},{5... | collective-permute-start | bytes 196616 | tf_op jit(solution)/shard_map/ppermute | solution.py:36
  66.6 2.6 %collective-permute-done.17 = bf16[64,512]{1,0:T(8,128)(2,1)S(1)} collective-permute-done((bf16[64,512]{1,0:T(8,128)(2,1)S(1)}, bf16[64,512]{1,0:T(8,128)(2,1)S(1)}, u32[]{:S(2)}, u32[]{:S(2)}) %collective-permute-start.17) | collective-permute-done | bytes 65568 | tf_op jit(solution)/shard_map/ppermute | solution.py:36
  69.2 2.0 %collective-permute-start.18 = (bf16[64,512]{1,0:T(8,128)(2,1)S(1)}, bf16[64,512]{1,0:T(8,128)(2,1)S(1)}, u32[]{:S(2)}, u32[]{:S(2)}) collective-permute-start(bf16[64,512]{1,0:T(8,128)(2,1)S(1)} %broadcast_select_fusion.2), channel_id=1, source_target_pairs={{0,8},{4,12},{8,0},{12,4},{16,24},{20,28},{24,16},{28,20},{1,9},{5... | collective-permute-start | bytes 196616 | tf_op jit(solution)/shard_map/ppermute | solution.py:36
  71.1 0.6 dynamic_slice.15
  71.7 1.8 %collective-permute-done.18 = bf16[64,512]{1,0:T(8,128)(2,1)S(1)} collective-permute-done((bf16[64,512]{1,0:T(8,128)(2,1)S(1)}, bf16[64,512]{1,0:T(8,128)(2,1)S(1)}, u32[]{:S(2)}, u32[]{:S(2)}) %collective-permute-start.18) | collective-permute-done | bytes 65568 | tf_op jit(solution)/shard_map/ppermute | solution.py:36
  73.5 3.5 %collective-permute-start.19 = (bf16[64,512]{1,0:T(8,128)(2,1)S(1)}, bf16[64,512]{1,0:T(8,128)(2,1)S(1)}, u32[]{:S(2)}, u32[]{:S(2)}) collective-permute-start(bf16[64,512]{1,0:T(8,128)(2,1)S(1)} %broadcast_select_fusion.3), channel_id=1, source_target_pairs={{0,16},{4,20},{8,24},{12,28},{16,0},{20,4},{24,8},{28,12},{1,17},{... | collective-permute-start | bytes 196616 | tf_op jit(solution)/shard_map/ppermute | solution.py:36
  77.0 0.7 iota_compare_fusion.3
  77.7 0.6 copy-done.11
  78.3 5.4 %shard_map.88 = (bf16[128,1024]{1,0:T(8,128)(2,1)}, f32[64,2048]{1,0:T(8,128)}, bf16[64,2048]{1,0:T(8,128)(2,1)}) custom-call(f32[128,1024]{1,0:T(8,128)} %get-tuple-element.14.base, bf16[64,512]{1,0:T(8,128)(2,1)} %copy-done.8, bf16[64,512]{1,0:T(8,128)(2,1)} %copy-done.11, bf16[1024,512]{1,0:T(8,128)(2,1)} %get-tuple-element.13.factor_ends, ...), custom_call_target="tpu_custom_call" | custom-call | tf_op jit(solution)/shard_map/pallas_call | solution.py:195
  83.8 4.6 %shard_map.89 = (f32[64,2048]{1,0:T(8,128)}, bf16[64,2048]{1,0:T(8,128)(2,1)}) custom-call(bf16[128,1024]{1,0:T(8,128)(2,1)} %get-tuple-element.18.second, bf16[1024,4096]{1,0:T(8,128)(2,1)} %bitcast.31), custom_call_target="tpu_custom_call" | custom-call | tf_op jit(solution)/shard_map/pallas_call | solution.py:216
  88.4 0.5 collective-permute-start.12
  88.9 0.3 fusion.2
  89.2 0.7 multiply_bitcast_fusion
  90.0 1.6 %collective-permute-start.11 = (bf16[32,2048]{1,0:T(8,128)(2,1)S(1)}, bf16[32,2048]{1,0:T(8,128)(2,1)S(1)}, u32[]{:S(2)}, u32[]{:S(2)}) collective-permute-start(bf16[32,2048]{1,0:T(8,128)(2,1)S(1)} %slice.214), channel_id=1, source_target_pairs={{0,2},{1,3},{2,0},{3,1},{4,6},{5,7},{6,4},{7,5},{8,10},{9,11},{10,... | collective-permute-start | bytes 393224 | tf_op jit(solution)/shard_map/ppermute | solution.py:36
  91.6 0.6 collective-permute-start.13
  92.2 4.2 %collective-permute-done.11 = bf16[32,2048]{1,0:T(8,128)(2,1)S(1)} collective-permute-done((bf16[32,2048]{1,0:T(8,128)(2,1)S(1)}, bf16[32,2048]{1,0:T(8,128)(2,1)S(1)}, u32[]{:S(2)}, u32[]{:S(2)}) %collective-permute-start.11) | collective-permute-done | bytes 131104 | tf_op jit(solution)/shard_map/ppermute | solution.py:36
  96.4 1.8 %collective-permute-done.13 = bf16[32,2048]{1,0:T(8,128)(2,1)S(1)} collective-permute-done((bf16[32,2048]{1,0:T(8,128)(2,1)S(1)}, bf16[32,2048]{1,0:T(8,128)(2,1)S(1)}, u32[]{:S(2)}, u32[]{:S(2)}) %collective-permute-start.13) | collective-permute-done | bytes 131104 | tf_op jit(solution)/shard_map/ppermute | solution.py:36
  98.3 0.8 maximum_select_fusion
  (65 shorter events, 0.6 us)
Async XLA Ops:
  11.8 7.6 %copy-start = (f32[1,32,4096]{2,1,0:T(8,128)S(1)}, f32[1,32,4096]{2,1,0:T(8,128)}, u32[]{:S(2)}) copy-start(f32[1,32,4096]{2,1,0:T(8,128)} %param.6) | copy-start | bytes 1572868
  14.6 14.3 %collective-permute-start.14 = (bf16[272,512]{1,0:T(8,128)(2,1)}, bf16[272,512]{1,0:T(8,128)(2,1)}, u32[]{:S(2)}, u32[]{:S(2)}) collective-permute-start(bf16[272,512]{1,0:T(8,128)(2,1)} %maximum_maximum_fusion), channel_id=1, source_target_pairs={{0,1},{1,0},{2,3},{3,2},{4,5},{5,4},{6,7},{7,6},{8,9},{9,8},{10,11... | collective-permute-start | bytes 835592 | tf_op jit(solution)/shard_map/ppermute | solution.py:36
  15.1 8.5 %copy-start.9 = (f32[1,32,512]{2,1,0:T(8,128)S(1)}, f32[1,32,512]{2,1,0:T(8,128)}, u32[]{:S(2)}) copy-start(f32[1,32,512]{2,1,0:T(8,128)} %param.8) | copy-start | bytes 196612
  16.9 10.0 %copy-start.3 = (bf16[32,4096]{1,0:T(8,128)(2,1)S(1)}, bf16[32,4096]{1,0:T(8,128)(2,1)}, u32[]{:S(2)}) copy-start(bf16[32,4096]{1,0:T(8,128)(2,1)} %shard_map.85) | copy-start | bytes 786436
  16.9 10.0 %collective-permute-start = (bf16[32,4096]{1,0:T(8,128)(2,1)}, bf16[32,4096]{1,0:T(8,128)(2,1)}, u32[]{:S(2)}, u32[]{:S(2)}) collective-permute-start(bf16[32,4096]{1,0:T(8,128)(2,1)} %shard_map.85), channel_id=1, source_target_pairs={{0,2},{1,3},{2,0},{3,1},{4,6},{5,7},{6,4},{7,5},{8,10},{9,11},{10,... | collective-permute-start | bytes 786440 | tf_op jit(solution)/shard_map/ppermute | solution.py:36
  20.0 9.9 %copy-start.2 = (f32[512,512]{1,0:T(8,128)S(1)}, f32[512,512]{1,0:T(8,128)}, u32[]{:S(2)}) copy-start(f32[512,512]{1,0:T(8,128)} %get-tuple-element.22) | copy-start | bytes 3145732
  23.6 6.5 %copy-start.12 = (f32[1,512]{1,0:T(1,128)S(1)}, f32[1,512]{1,0:T(1,128)}, u32[]{:S(2)}) copy-start(f32[1,512]{1,0:T(1,128)} %get-tuple-element.21) | copy-start | bytes 6148
  23.6 5.2 %collective-permute-start.2 = (bf16[32,1536]{1,0:T(8,128)(2,1)S(1)}, bf16[32,1536]{1,0:T(8,128)(2,1)S(1)}, u32[]{:S(2)}, u32[]{:S(2)}) collective-permute-start(bf16[32,1536]{1,0:T(8,128)(2,1)S(1)} %pad_maximum_fusion.2), channel_id=1, source_target_pairs={{0,2},{1,3},{2,0},{3,1},{4,6},{5,7},{6,4},{7,5},{8,10},{9,11},{10,... | collective-permute-start | bytes 294920 | tf_op jit(solution)/shard_map/ppermute | solution.py:36
  27.9 2.3 %copy-start.1 = (bf16[64,4096]{1,0:T(8,128)(2,1)}, bf16[64,4096]{1,0:T(8,128)(2,1)S(1)}, u32[]{:S(2)}) copy-start(bf16[64,4096]{1,0:T(8,128)(2,1)S(1)} %pad_maximum_fusion.near) | copy-start | bytes 1572868
  28.0 2.3 %collective-permute-start.1 = (bf16[64,4096]{1,0:T(8,128)(2,1)S(1)}, bf16[64,4096]{1,0:T(8,128)(2,1)S(1)}, u32[]{:S(2)}, u32[]{:S(2)}) collective-permute-start(bf16[64,4096]{1,0:T(8,128)(2,1)S(1)} %pad_maximum_fusion.near), channel_id=1, source_target_pairs={{0,1},{1,0},{2,3},{3,2},{4,5},{5,4},{6,7},{7,6},{8,9},{9,8},{10,11... | collective-permute-start | bytes 1572872 | tf_op jit(solution)/shard_map/ppermute | solution.py:36
  28.8 1.4 %copy-start.4 = (bf16[64,1024]{1,0:T(8,128)(2,1)}, bf16[64,1024]{1,0:T(8,128)(2,1)S(1)}, u32[]{:S(2)}) copy-start(bf16[64,1024]{1,0:T(8,128)(2,1)S(1)} %slice.116.small_near) | copy-start | bytes 393220
  28.8 1.4 %collective-permute-start.3 = (bf16[64,1024]{1,0:T(8,128)(2,1)S(1)}, bf16[64,1024]{1,0:T(8,128)(2,1)S(1)}, u32[]{:S(2)}, u32[]{:S(2)}) collective-permute-start(bf16[64,1024]{1,0:T(8,128)(2,1)S(1)} %slice.116.small_near), channel_id=1, source_target_pairs={{0,1},{1,0},{2,3},{3,2},{4,5},{5,4},{6,7},{7,6},{8,9},{9,8},{10,11... | collective-permute-start | bytes 393224 | tf_op jit(solution)/shard_map/ppermute | solution.py:36
  30.2 0.7 copy-start.10
  30.3 0.9 copy-start.7
  40.0 1.4 %collective-permute-start.4 = (f32[64,512]{1,0:T(8,128)S(1)}, f32[64,512]{1,0:T(8,128)S(1)}, u32[]{:S(2)}, u32[]{:S(2)}) collective-permute-start(f32[64,512]{1,0:T(8,128)S(1)} %slice.90), channel_id=1, source_target_pairs={{0,1},{1,0},{2,3},{3,2},{4,5},{5,4},{6,7},{7,6},{8,9},{9,8},{10,11... | collective-permute-start | bytes 393224 | tf_op jit(solution)/shard_map/ppermute | solution.py:36
  42.4 5.6 %collective-permute-start.5 = (bf16[96,512]{1,0:T(8,128)(2,1)S(1)}, bf16[96,512]{1,0:T(8,128)(2,1)S(1)}, u32[]{:S(2)}, u32[]{:S(2)}) collective-permute-start(bf16[96,512]{1,0:T(8,128)(2,1)S(1)} %pad_maximum_fusion.3), channel_id=1, source_target_pairs={{0,2},{1,3},{2,0},{3,1},{4,6},{5,7},{6,4},{7,5},{8,10},{9,11},{10,... | collective-permute-start | bytes 294920 | tf_op jit(solution)/shard_map/ppermute | solution.py:36
  44.5 9.0 %collective-permute-start.15 = (bf16[272,512]{1,0:T(8,128)(2,1)S(1)}, bf16[272,512]{1,0:T(8,128)(2,1)S(1)}, u32[]{:S(2)}, u32[]{:S(2)}) collective-permute-start(bf16[272,512]{1,0:T(8,128)(2,1)S(1)} %maximum_maximum_fusion.1), channel_id=1, source_target_pairs={{0,2},{1,3},{2,0},{3,1},{4,6},{5,7},{6,4},{7,5},{8,10},{9,11},{10,... | collective-permute-start | bytes 835592 | tf_op jit(solution)/shard_map/ppermute | solution.py:36
  48.1 5.4 %collective-permute-start.6 = (bf16[96,512]{1,0:T(8,128)(2,1)S(1)}, bf16[96,512]{1,0:T(8,128)(2,1)S(1)}, u32[]{:S(2)}, u32[]{:S(2)}) collective-permute-start(bf16[96,512]{1,0:T(8,128)(2,1)S(1)} %pad_maximum_fusion.4), channel_id=1, source_target_pairs={{0,4},{4,0},{8,12},{12,8},{16,20},{20,16},{24,28},{28,24},{1,5},{5... | collective-permute-start | bytes 294920 | tf_op jit(solution)/shard_map/ppermute | solution.py:36
  53.6 4.7 %collective-permute-start.7 = (bf16[96,512]{1,0:T(8,128)(2,1)S(1)}, bf16[96,512]{1,0:T(8,128)(2,1)S(1)}, u32[]{:S(2)}, u32[]{:S(2)}) collective-permute-start(bf16[96,512]{1,0:T(8,128)(2,1)S(1)} %broadcast_select_fusion), channel_id=1, source_target_pairs={{0,8},{4,12},{8,0},{12,4},{16,24},{20,28},{24,16},{28,20},{1,9},{5... | collective-permute-start | bytes 294920 | tf_op jit(solution)/shard_map/ppermute | solution.py:36
  58.3 5.6 %collective-permute-start.8 = (bf16[96,512]{1,0:T(8,128)(2,1)S(1)}, bf16[96,512]{1,0:T(8,128)(2,1)S(1)}, u32[]{:S(2)}, u32[]{:S(2)}) collective-permute-start(bf16[96,512]{1,0:T(8,128)(2,1)S(1)} %broadcast_select_fusion.1), channel_id=1, source_target_pairs={{0,16},{4,20},{8,24},{12,28},{16,0},{20,4},{24,8},{28,12},{1,17},{... | collective-permute-start | bytes 294920 | tf_op jit(solution)/shard_map/ppermute | solution.py:36
  61.1 3.2 %collective-permute-start.16 = (bf16[256,512]{1,0:T(8,128)(2,1)S(1)}, bf16[256,512]{1,0:T(8,128)(2,1)S(1)}, u32[]{:S(2)}, u32[]{:S(2)}) collective-permute-start(bf16[256,512]{1,0:T(8,128)(2,1)S(1)} %fusion.4), channel_id=1, source_target_pairs={{0,1},{1,0},{2,3},{3,2},{4,5},{5,4},{6,7},{7,6},{8,9},{9,8},{10,11... | collective-permute-start | bytes 786440 | tf_op jit(solution)/shard_map/ppermute | solution.py:36
  64.3 7.5 %copy-start.8 = (bf16[64,512]{1,0:T(8,128)(2,1)}, bf16[64,512]{1,0:T(8,128)(2,1)S(1)}, u32[]{:S(2)}) copy-start(bf16[64,512]{1,0:T(8,128)(2,1)S(1)} %get-tuple-element.37.near) | copy-start | bytes 196612
  64.3 6.9 %copy-start.13 = (s32[8]{0:T(128)S(1)}, s32[8]{0:T(128)}, u32[]{:S(2)}) copy-start(s32[8]{0:T(128)} %area_size.5) | copy-start | bytes 100
  64.8 4.3 %collective-permute-start.17 = (bf16[64,512]{1,0:T(8,128)(2,1)S(1)}, bf16[64,512]{1,0:T(8,128)(2,1)S(1)}, u32[]{:S(2)}, u32[]{:S(2)}) collective-permute-start(bf16[64,512]{1,0:T(8,128)(2,1)S(1)} %pad_maximum_fusion.5), channel_id=1, source_target_pairs={{0,4},{4,0},{8,12},{12,8},{16,20},{20,16},{24,28},{28,24},{1,5},{5... | collective-permute-start | bytes 196616 | tf_op jit(solution)/shard_map/ppermute | solution.py:36
  69.2 4.3 %collective-permute-start.18 = (bf16[64,512]{1,0:T(8,128)(2,1)S(1)}, bf16[64,512]{1,0:T(8,128)(2,1)S(1)}, u32[]{:S(2)}, u32[]{:S(2)}) collective-permute-start(bf16[64,512]{1,0:T(8,128)(2,1)S(1)} %broadcast_select_fusion.2), channel_id=1, source_target_pairs={{0,8},{4,12},{8,0},{12,4},{16,24},{20,28},{24,16},{28,20},{1,9},{5... | collective-permute-start | bytes 196616 | tf_op jit(solution)/shard_map/ppermute | solution.py:36
  71.7 6.0 %collective-permute-start.9 = (bf16[64,512]{1,0:T(8,128)(2,1)S(1)}, bf16[64,512]{1,0:T(8,128)(2,1)S(1)}, u32[]{:S(2)}, u32[]{:S(2)}) collective-permute-start(bf16[64,512]{1,0:T(8,128)(2,1)S(1)} %get-tuple-element.37.near), channel_id=1, source_target_pairs={{0,1},{1,0},{2,3},{3,2},{4,5},{5,4},{6,7},{7,6},{8,9},{9,8},{10,11... | collective-permute-start | bytes 196616 | tf_op jit(solution)/shard_map/ppermute | solution.py:36
  73.5 15.4 %collective-permute-start.19 = (bf16[64,512]{1,0:T(8,128)(2,1)S(1)}, bf16[64,512]{1,0:T(8,128)(2,1)S(1)}, u32[]{:S(2)}, u32[]{:S(2)}) collective-permute-start(bf16[64,512]{1,0:T(8,128)(2,1)S(1)} %broadcast_select_fusion.3), channel_id=1, source_target_pairs={{0,16},{4,20},{8,24},{12,28},{16,0},{20,4},{24,8},{28,12},{1,17},{... | collective-permute-start | bytes 196616 | tf_op jit(solution)/shard_map/ppermute | solution.py:36
  77.7 0.6 copy-start.11
  83.8 6.1 %collective-permute-start.10 = (bf16[64,2048]{1,0:T(8,128)(2,1)}, bf16[64,2048]{1,0:T(8,128)(2,1)S(1)}, u32[]{:S(2)}, u32[]{:S(2)}) collective-permute-start(bf16[64,2048]{1,0:T(8,128)(2,1)} %get-tuple-element.17), channel_id=1, source_target_pairs={{0,1},{1,0},{2,3},{3,2},{4,5},{5,4},{6,7},{7,6},{8,9},{9,8},{10,11... | collective-permute-start | bytes 786440 | tf_op jit(solution)/shard_map/ppermute | solution.py:36
  83.8 6.1 %copy-start.6 = (f32[64,2048]{1,0:T(8,128)S(1)}, f32[64,2048]{1,0:T(8,128)}, u32[]{:S(2)}) copy-start(f32[64,2048]{1,0:T(8,128)} %get-tuple-element.16) | copy-start | bytes 1572868
  88.4 3.1 %copy-start.5 = (f32[64,2048]{1,0:T(8,128)S(1)}, f32[64,2048]{1,0:T(8,128)}, u32[]{:S(2)}) copy-start(f32[64,2048]{1,0:T(8,128)} %get-tuple-element.19) | copy-start | bytes 1572868
  88.4 3.1 %collective-permute-start.12 = (bf16[64,2048]{1,0:T(8,128)(2,1)}, bf16[64,2048]{1,0:T(8,128)(2,1)S(1)}, u32[]{:S(2)}, u32[]{:S(2)}) collective-permute-start(bf16[64,2048]{1,0:T(8,128)(2,1)} %get-tuple-element.20), channel_id=1, source_target_pairs={{0,1},{1,0},{2,3},{3,2},{4,5},{5,4},{6,7},{7,6},{8,9},{9,8},{10,11... | collective-permute-start | bytes 786440 | tf_op jit(solution)/shard_map/ppermute | solution.py:36
  90.0 6.4 %collective-permute-start.11 = (bf16[32,2048]{1,0:T(8,128)(2,1)S(1)}, bf16[32,2048]{1,0:T(8,128)(2,1)S(1)}, u32[]{:S(2)}, u32[]{:S(2)}) collective-permute-start(bf16[32,2048]{1,0:T(8,128)(2,1)S(1)} %slice.214), channel_id=1, source_target_pairs={{0,2},{1,3},{2,0},{3,1},{4,6},{5,7},{6,4},{7,5},{8,10},{9,11},{10,... | collective-permute-start | bytes 393224 | tf_op jit(solution)/shard_map/ppermute | solution.py:36
  91.6 6.6 %collective-permute-start.13 = (bf16[32,2048]{1,0:T(8,128)(2,1)S(1)}, bf16[32,2048]{1,0:T(8,128)(2,1)S(1)}, u32[]{:S(2)}, u32[]{:S(2)}) collective-permute-start(bf16[32,2048]{1,0:T(8,128)(2,1)S(1)} %slice.213), channel_id=1, source_target_pairs={{0,2},{1,3},{2,0},{3,1},{4,6},{5,7},{6,4},{7,5},{8,10},{9,11},{10,... | collective-permute-start | bytes 393224 | tf_op jit(solution)/shard_map/ppermute | solution.py:36
where the time goes:
time: 99.9 us; the launch traced here: 99.1 us
  Pallas kernels  31.1 us (31%)
  waiting for transfers between devices  27.1 us (27%)
  starting transfers between devices  22.1 us (22%)
  other arithmetic  9.18 us (9%)
  local copies, waits for them, and re-layouts  7.52 us (8%)
  matrix products  1.11 us (1%)
  between operations  1.1 us (1%)
    ppermute x20, waiting for transfers between devices, swap(): return lax.ppermute(x, axis, [(i, i ^ bit) for i in range(n)])  27.1 us
    ppermute x20, starting transfers between devices, swap(): return lax.ppermute(x, axis, [(i, i ^ bit) for i in range(n)])  22.1 us
    pallas_call x1, Pallas kernels, ends_columns(): pl.pallas_call(ends_kernel, grid=(width // depth,), out_shape=(out((rows,...  11.2 us
    pallas_call x1, Pallas kernels, base_product(): pl.pallas_call(base_kernel, grid=(rows // block,), out_shape=(out((count,...  8.01 us
    pallas_call x1, Pallas kernels, second_product(): pl.pallas_call(second_kernel, grid=(steps,), out_shape=(out((2 * half, ro...  5.45 us
    pallas_call x1, Pallas kernels, angles_product(): pl.pallas_call(angles_kernel, grid=(steps,), out_shape=shapes, in_specs=[...  4.63 us
    gather x2, local copies, waits for them, and re-layouts, shards(): at_ends = injection_here[:, buses]  2.7 us
  transfers between devices with their start and end apart: 20, of which 12 were waited for; matrix products, arithmetic and copies ran while one was open for 10% of the time, Pallas kernels for 12%

commit v1 on v0

v1 whole, which is shorter than its diff:
```python
import jax
import jax.numpy as jnp
from jax import lax
from jax.experimental import pallas as pl
from jax.experimental.pallas import tpu as pltpu
from jax.sharding import PartitionSpec as P


CAP = 128
PENALTY = 1.5
PROXIMAL = 0.5
DENOM = 2.0 * PENALTY + PROXIMAL
SUBLANES = 16

F32 = jnp.float32
BF16 = jnp.bfloat16

WHOLE = pl.BlockSpec(memory_space=pltpu.VMEM)
SCALARS = pl.BlockSpec(memory_space=pltpu.SMEM)


def dot_nt(a, b):
    return lax.dot_general(a, b, (((1,), (1,)), ((), ())), preferred_element_type=F32)


def dot_tn(a, b):
    return lax.dot_general(a, b, (((0,), (0,)), ((), ())), preferred_element_type=F32)


def dot_nn(a, b):
    return jnp.dot(a, b, preferred_element_type=F32)


def swap(x, axis, bit):
    n = lax.axis_size(axis)
    return lax.ppermute(x, axis, [(i, i ^ bit) for i in range(n)])


def halves(x):
    high = x.astype(BF16)
    return high, (x - high.astype(F32)).astype(BF16)


def out(shape, dtype):
    return jax.ShapeDtypeStruct(shape, dtype)


def plain_kernel(area_size, injection, dual, packed):
    width = injection.shape[1]
    live = lax.broadcasted_iota(jnp.int32, injection.shape, 1) < area_size[lax.axis_index("area")]
    packed[:, :width] = jnp.where(live, injection[...], 0.0).astype(BF16)
    packed[:, width:] = dual[...].astype(BF16)


def packed_side(area_size, injection, dual):
    return pl.pallas_call(
        plain_kernel,
        out_shape=out((injection.shape[0], injection.shape[1] + dual.shape[1]), BF16),
        in_specs=[SCALARS, WHOLE, WHOLE],
        out_specs=WHOLE,
    )(area_size, injection, dual)


def base_kernel(area_size, near, far, dual, factor, factor_ends, base, keep, send, side, partial):
    step = pl.program_id(0)
    half = near.shape[0]
    block, width = factor.shape

    @pl.when(step == 0)
    def _():
        side[:half] = near[...]
        side[half:] = far[...]
        partial[...] = jnp.zeros_like(partial)

    here = factor_ends[...]
    value = dot_nt(side[:, :width], factor[...])
    start = lax.axis_index("scen") * (pl.num_programs(0) * block) + step * block
    live = start + lax.broadcasted_iota(jnp.int32, value.shape, 1) < area_size[lax.axis_index("area")]
    value = jnp.where(live, value, 0.0)
    base[...] = value
    first = (value - dot_nt(side[:, width:], here)).astype(BF16)
    partial[...] += dot_nn(first, here)

    @pl.when(step == pl.num_programs(0) - 1)
    def _():
        count = dual.shape[0]
        keep[:count] = PENALTY * partial[:count] + dual[...]
        keep[count:] = PENALTY * partial[count:half]
        send[...] = PENALTY * partial[half:]


def base_product(area_size, near, far, dual, factor, factor_ends):
    rows, width = factor.shape
    half, packed_width = near.shape
    ends_total = factor_ends.shape[1]
    block = 512
    fixed = pl.BlockSpec((half, ends_total), lambda i: (0, 0))
    return pl.pallas_call(
        base_kernel,
        grid=(rows // block,),
        out_shape=(
            out((2 * half, rows), F32),
            out((half, ends_total), F32),
            out((half, ends_total), F32),
        ),
        in_specs=[
            SCALARS,
            WHOLE,
            WHOLE,
            WHOLE,
            pl.BlockSpec((block, width), lambda i: (i, 0)),
            pl.BlockSpec((block, ends_total), lambda i: (i, 0)),
        ],
        out_specs=(pl.BlockSpec((2 * half, block), lambda i: (0, i)), fixed, fixed),
        scratch_shapes=[
            pltpu.VMEM((2 * half, packed_width), BF16),
            pltpu.VMEM((2 * half, ends_total), F32),
        ],
    )(area_size, near, far, dual, factor, factor_ends)


def second_kernel(base, near, far, factor_ends, factor, second, keep, send, right):
    half = near.shape[0]

    @pl.when(pl.program_id(0) == 0)
    def _():
        right[:half] = near[...]
        right[half:] = far[...]
        second[...] = (base[...] - dot_nt(right[...], factor_ends[...])).astype(BF16)

    value = dot_nn(second[...], factor[...])
    keep[...] = value[:half]
    send[...] = value[half:].astype(BF16)


def angles_specs(half, depth, rows, width, parts, part):
    steps = width // parts // depth
    spec = pl.BlockSpec((half, depth), lambda i: (0, i))
    shapes = (out((half, width // parts), F32), out((half, width // parts), BF16))
    return steps, pl.BlockSpec((rows, depth), lambda i: (0, part * steps + i)), spec, shapes


def second_product(base, near, far, factor_ends, factor, parts):
    rows, width = factor.shape
    half = near.shape[0]
    steps, factor_spec, spec, shapes = angles_specs(half, 1024, rows, width, parts, 0)
    return pl.pallas_call(
        second_kernel,
        grid=(steps,),
        out_shape=(out((2 * half, rows), BF16),) + shapes,
        in_specs=[WHOLE, WHOLE, WHOLE, WHOLE, factor_spec],
        out_specs=(pl.BlockSpec((2 * half, rows), lambda i: (0, 0)), spec, spec),
        scratch_shapes=[pltpu.VMEM((2 * half, near.shape[1]), BF16)],
    )(base, near, far, factor_ends, factor)


def angles_kernel(second, factor, keep, send):
    half = keep.shape[0]
    value = dot_nn(second[...], factor[...])
    keep[...] = value[:half]
    send[...] = value[half:].astype(BF16)


def angles_product(second, factor, parts, part):
    rows, width = factor.shape
    half = second.shape[0] // 2
    steps, factor_spec, spec, shapes = angles_specs(half, 1024, rows, width, parts, part)
    return pl.pallas_call(
        angles_kernel,
        grid=(steps,),
        out_shape=shapes,
        in_specs=[WHOLE, factor_spec],
        out_specs=(spec, spec),
    )(second, factor)


def shards(injection, kkt_factor, dual_price, area_size, bnd_bus, peer_end):
    area_id = lax.axis_index("area")
    band_index = lax.axis_index("scen")
    areas_all = lax.axis_size("area")
    factor = kkt_factor[0]
    band_rows, width = factor.shape
    injection_here = injection[0]
    dual_here = dual_price[0]
    columns, ends_total = dual_here.shape
    size_here = area_size[area_id]
    buses = bnd_bus[area_id]
    peers = peer_end[area_id]
    offset = (peers // ends_total) ^ area_id

    packed = packed_side(area_size, injection_here, dual_here)
    other = swap(packed, "scen", 2)
    pair = jnp.concatenate([packed, other], axis=0)
    pair_far = swap(pair, "scen", 1)

    live_band = (band_index * band_rows + jnp.arange(band_rows))[:, None] < size_here
    pick = (jnp.arange(width)[:, None] == buses[None, :]).astype(BF16)
    factor_ends = jnp.where(live_band, dot_nn(factor, pick), 0.0).astype(BF16)
    gram = dot_tn(factor_ends, factor_ends)
    slots = jnp.arange(ends_total)
    on_diag = slots[:, None] == slots[None, :]
    squares = jnp.sum(jnp.where(on_diag, gram, 0.0), axis=0, keepdims=True)
    gram = jnp.where(on_diag, 0.0, gram)
    half = ends_total // 2
    side = band_index % 2

    def with_squares(rows, squares):
        high, low = halves(squares)
        blank = jnp.zeros((SUBLANES - 2, ends_total), BF16)
        return jnp.concatenate([rows.astype(BF16), high, low, blank], axis=0)

    def add_gram(rows, squares, incoming):
        incoming = incoming.astype(F32)
        return rows + incoming[:half], squares + incoming[half : half + 1] + incoming[half + 1 : half + 2]

    gram_keep = lax.dynamic_slice_in_dim(gram, side * half, half, 0)
    gram_send = lax.dynamic_slice_in_dim(gram, (1 - side) * half, half, 0)
    gram_keep, squares = add_gram(
        gram_keep, squares, swap(with_squares(gram_send, squares), "scen", 1)
    )
    gram_keep, squares = add_gram(
        gram_keep, squares, swap(with_squares(gram_keep, squares), "scen", 2)
    )
    gram_keep = gram_keep.astype(BF16)
    gram_other = swap(gram_keep, "scen", 1)
    gram_all = jnp.where(
        side == 0,
        jnp.concatenate([gram_keep, gram_other], axis=0),
        jnp.concatenate([gram_other, gram_keep], axis=0),
    )
    mate = ((slots // CAP * CAP + peers % CAP)[None, :] == slots[:, None]).astype(BF16)

    base, keep, send = base_product(
        area_size, pair, pair_far, dual_here, factor, factor_ends
    )

    def exchange(q):
        moved = q
        bit = 1
        while bit < areas_all:
            moved = jnp.where((offset & bit)[None, :] != 0, swap(moved, "area", bit), moved)
            bit *= 2
        return dot_nn(moved, mate)

    def with_low(x, low_rows):
        high, low = halves(x)
        return jnp.concatenate([high, low[low_rows]], axis=0)

    pair_rows = 2 * columns
    keep = keep + swap(send, "scen", 1)
    pair_rows = 2 * columns
    first_rows, last_rows = slice(0, columns), slice(columns, pair_rows)
    other = swap(with_low(keep, last_rows), "scen", 2).astype(F32)
    q = keep + jnp.concatenate([other[last_rows] + other[pair_rows:], other[first_rows]], axis=0)
    moved = exchange(with_low(q, first_rows))
    moved = jnp.concatenate([moved[first_rows] + moved[pair_rows:], moved[last_rows]], axis=0)
    consensus = (q + moved) / DENOM
    spread = q - 2.0 * PENALTY * consensus
    spread_pair = spread.astype(BF16)
    spread_far = swap(spread_pair, "scen", 1)

    q_own, consensus_own = q[:columns], consensus[:columns]
    change = spread_pair[:columns].astype(F32) - dual_here.astype(BF16).astype(F32)
    change_high, change_low = halves(change)
    ends_scaled = (q_own - dual_here) - PENALTY * (
        change * squares + dot_nn(change_high, gram_all) + dot_nn(change_low, gram_all)
    )
    q_last = ends_scaled + (q_own - PENALTY * consensus_own)
    moved = exchange(with_low(q_last, first_rows))
    moved = moved[first_rows] + moved[last_rows]
    consensus_last = (q_last + moved + PROXIMAL * consensus_own) / DENOM
    dual_last = q_last - PENALTY * consensus_last

    parts = 2
    second, keep, send = second_product(base, spread_pair, spread_far, factor_ends, factor, parts)
    pieces = []
    for part in range(parts):
        if part:
            keep, send = angles_product(second, factor, parts, part)
        keep = keep + swap(send, "scen", 1).astype(F32)
        pieces.append(keep[:columns] + swap(keep[columns:].astype(BF16), "scen", 2).astype(F32))
    live_mask = jnp.arange(width) < size_here
    angles_here = jnp.where(live_mask, jnp.concatenate(pieces, axis=1), 0.0)
    return (angles_here[None], dual_last[None], consensus_last[None])


def solution(mesh):
    spec = P("area", "scen", None)
    return jax.shard_map(
        shards,
        mesh=mesh,
        in_specs=(spec, spec, spec, P(), P(), P()),
        out_specs=(spec, spec, spec),
        check_vma=False,
    )
```

time: 99.9 us -> 85.9 us (0.86)
  Pallas kernels: 31.1 us -> 16.9 us
  matrix products: 1.11 us -> 9.78 us
  local copies, waits for them, and re-layouts: 7.52 us -> 3.08 us
  other arithmetic: 9.18 us -> 6.53 us
    pallas_call x3 -> x2, Pallas kernels: 21 us -> 9.1 us  [the longest x1 7.27 us: base_product(): pl.pallas_call(base_kernel, grid=(rows // block,), out_shape=(out((2 * ha...]
    dot_general x4 -> x5, matrix products: 1.11 us -> 9.03 us  [dot_nn(): return jnp.dot(a, b, preferred_element_type=F32)]
    gather x2 -> x0, local copies, waits for them, and re-layouts: 2.7 us -> none  [shards(): at_ends = injection_here[:, buses]]
    pallas_call x1, Pallas kernels: 5.45 us -> 4.25 us  [second_product(): pl.pallas_call(second_kernel, grid=(steps,), out_shape=(out((2 * half, ro...]
    pallas_call x1, Pallas kernels: 4.63 us -> 3.56 us  [angles_product(): pl.pallas_call(angles_kernel, grid=(steps,), out_shape=shapes, in_specs=[...]
    convert_element_type x1, local copies, waits for them, and re-layouts: 1.07 us -> 0.03 us  [with_squares(): return jnp.concatenate([rows.astype(BF16), high, low, blank], axis=0)]
    ppermute x20 -> x18, waiting for transfers between devices: 27.1 us -> 26.5 us  [swap(): return lax.ppermute(x, axis, [(i, i ^ bit) for i in range(n)])]
    ppermute x20 -> x18, starting transfers between devices: 22.1 us -> 21.6 us  [swap(): return lax.ppermute(x, axis, [(i, i ^ bit) for i in range(n)])]
  transfers between devices with their start and end apart: 20 -> 18, of which waited for: 12 -> 10; matrix products, arithmetic and copies ran while one was open for 10% -> 18% of each run, Pallas kernels for 12% -> 9%
where the time goes in v1:
time: 85.9 us; the launch traced here: 85.5 us
  waiting for transfers between devices  26.5 us (31%)
  starting transfers between devices  21.6 us (25%)
  Pallas kernels  16.9 us (20%)
  matrix products  9.78 us (11%)
  other arithmetic  6.53 us (8%)
  local copies, waits for them, and re-layouts  3.08 us (4%)
  between operations  1.06 us (1%)
    ppermute x18, waiting for transfers between devices, swap(): return lax.ppermute(x, axis, [(i, i ^ bit) for i in range(n)])  26.5 us
    ppermute x18, starting transfers between devices, swap(): return lax.ppermute(x, axis, [(i, i ^ bit) for i in range(n)])  21.6 us
    dot_general x5, matrix products, dot_nn(): return jnp.dot(a, b, preferred_element_type=F32)  9.03 us
    pallas_call x1, Pallas kernels, base_product(): pl.pallas_call(base_kernel, grid=(rows // block,), out_shape=(out((2 * ha...  7.27 us
    pallas_call x1, Pallas kernels, second_product(): pl.pallas_call(second_kernel, grid=(steps,), out_shape=(out((2 * half, ro...  4.25 us
    pallas_call x1, Pallas kernels, angles_product(): pl.pallas_call(angles_kernel, grid=(steps,), out_shape=shapes, in_specs=[...  3.56 us
    pallas_call x1, Pallas kernels, packed_side(): pl.pallas_call(plain_kernel, out_shape=out((injection.shape[0], injection...  1.82 us
  transfers between devices with their start and end apart: 18, of which 10 were waited for; matrix products, arithmetic and copies ran while one was open for 18% of the time, Pallas kernels for 9%

profile of v1, /device:TPU:0, one launch (start us, length us, event | category | flops | bytes accessed | tf_op | source)
XLA Modules:
  0.0 85.5 jit_solution(4159462750928926577)
XLA Ops:
  0.6 1.8 %shard_map.85 = bf16[32,4608]{1,0:T(8,128)(2,1)} custom-call(s32[8]{0:T(128)} %area_size.3, f32[32,4096]{1,0:T(8,128)} %bitcast.36, f32[32,512]{1,0:T(8,128)} %bitcast.37), custom_call_target="tpu_custom_call" | custom-call | tf_op jit(solution)/shard_map/pallas_call | solution.py:56
  2.5 3.0 %collective-permute-start = (bf16[32,4608]{1,0:T(8,128)(2,1)}, bf16[32,4608]{1,0:T(8,128)(2,1)S(1)}, u32[]{:S(2)}, u32[]{:S(2)}) collective-permute-start(bf16[32,4608]{1,0:T(8,128)(2,1)} %shard_map.85), channel_id=1, source_target_pairs={{0,2},{1,3},{2,0},{3,1},{4,6},{5,7},{6,4},{7,5},{8,10},{9,11},{10,... | collective-permute-start | bytes 884744 | tf_op jit(solution)/shard_map/ppermute | solution.py:36
  5.5 1.2 %dynamic_slice.15 = s32[1]{0:T(128)} dynamic-slice(s32[8]{0:T(128)} %area_size.3, s32[]{:T(128)S(6)} %select_n.95), dynamic_slice_sizes={1} | dynamic-slice | bytes 12 | tf_op jit(solution)/shard_map/dynamic_slice | solution.py:186
  6.7 0.7 add_compare_fusion
  7.3 0.8 fusion.28
  8.1 7.9 %select_convert_fusion = bf16[512,1024]{0,1:T(8,128)(2,1)S(1)} fusion(s32[512]{0:T(512)S(1)} %bitcast.45, pred[1024]{0:T(1024)(128)(4,1)S(1)} %add_compare_fusion, bf16[1,1024,4096]{2,1,0:T(8,128)(2,1)} %param.7), kind=kOutput, calls=%fused_computation.3 | convolution fusion | flops 4298113024 | bytes 9440256 | tf_op jit(solution)/shard_map/dot_general | solution.py:31
  16.0 0.0 copy-start.2
  16.1 0.8 fusion.4
  16.8 0.2 copy-done
  17.1 0.1 pad.13.clone
  17.2 0.1 maximum_maximum_fusion
  17.3 0.1 collective-permute-start.12
  17.4 0.0 collective-permute-done
  17.5 0.5 collective-permute-start.1
  18.0 1.1 %collective-permute-done.12 = bf16[272,512]{1,0:T(8,128)(2,1)} collective-permute-done((bf16[272,512]{1,0:T(8,128)(2,1)S(1)}, bf16[272,512]{1,0:T(8,128)(2,1)}, u32[]{:S(2)}, u32[]{:S(2)}) %collective-permute-start.12) | collective-permute-done | bytes 278560 | tf_op jit(solution)/shard_map/ppermute | solution.py:36
  19.1 1.0 %convert_element_type.154 = f32[272,512]{1,0:T(8,128)S(1)} convert(bf16[272,512]{1,0:T(8,128)(2,1)} %collective-permute-done.12) | non-fusion elementwise | flops 139264 | bytes 835584 | tf_op jit(solution)/shard_map/convert_element_type | solution.py:213
  20.1 0.1 fusion.12
  20.2 0.0 collective-permute-done.1.far
  20.3 0.8 copy-done.3
  21.1 7.3 %shard_map.86 = (f32[128,1024]{1,0:T(8,128)}, f32[64,512]{1,0:T(8,128)}, f32[64,512]{1,0:T(8,128)}) custom-call(s32[8]{0:T(128)} %area_size.3, bf16[64,4608]{1,0:T(8,128)(2,1)} %copy-done.1, bf16[64,4608]{1,0:T(8,128)(2,1)} %copy-done.3, f32[32,512]{1,0:T(8,128)} %bitcast.38, bf16[1024,4096]{1,0:T(8,128)(2,1)} %bitcast.31, bf16[1024,512]{1,0:T(8,128)(2,1)} %bitcast.34), custom_call_target="tpu_custom_call" | custom-call | tf_op jit(solution)/shard_map/pallas_call | solution.py:98
  28.3 0.2 collective-permute-start.2
  28.5 1.4 %collective-permute-done.2 = f32[64,512]{1,0:T(8,128)S(1)} collective-permute-done((f32[64,512]{1,0:T(8,128)}, f32[64,512]{1,0:T(8,128)S(1)}, u32[]{:S(2)}, u32[]{:S(2)}) %collective-permute-start.2) | collective-permute-done | bytes 131104 | tf_op jit(solution)/shard_map/ppermute | solution.py:36
  29.9 0.9 %fusion.36 = (bf16[64,512]{1,0:T(8,128)(2,1)S(1)}, f32[64,512]{1,0:T(8,128)S(1)}) fusion(f32[64,512]{1,0:T(8,128)} %get-tuple-element.12, f32[64,512]{1,0:T(8,128)S(1)} %collective-permute-done.2), kind=kLoop, calls=%fused_computation.100 | loop fusion | flops 65536 | bytes 458752 | tf_op jit(solution)/shard_map/convert_element_type | solution.py:40
  30.9 0.1 collective-permute-start.3
  31.0 0.1 maximum_maximum_fusion.1
  31.1 2.1 %collective-permute-start.13 = (bf16[272,512]{1,0:T(8,128)(2,1)S(1)}, bf16[272,512]{1,0:T(8,128)(2,1)S(1)}, u32[]{:S(2)}, u32[]{:S(2)}) collective-permute-start(bf16[272,512]{1,0:T(8,128)(2,1)S(1)} %maximum_maximum_fusion.1), channel_id=1, source_target_pairs={{0,2},{1,3},{2,0},{3,1},{4,6},{5,7},{6,4},{7,5},{8,10},{9,11},{10,... | collective-permute-start | bytes 835592 | tf_op jit(solution)/shard_map/ppermute | solution.py:36
  33.2 3.5 %collective-permute-done.3 = bf16[96,512]{1,0:T(8,128)(2,1)S(1)} collective-permute-done((bf16[96,512]{1,0:T(8,128)(2,1)S(1)}, bf16[96,512]{1,0:T(8,128)(2,1)S(1)}, u32[]{:S(2)}, u32[]{:S(2)}) %collective-permute-start.3) | collective-permute-done | bytes 98336 | tf_op jit(solution)/shard_map/ppermute | solution.py:36
  36.7 1.6 %collective-permute-start.4 = (bf16[96,512]{1,0:T(8,128)(2,1)S(1)}, bf16[96,512]{1,0:T(8,128)(2,1)S(1)}, u32[]{:S(2)}, u32[]{:S(2)}) collective-permute-start(bf16[96,512]{1,0:T(8,128)(2,1)S(1)} %pad_maximum_fusion.2), channel_id=1, source_target_pairs={{0,4},{4,0},{8,12},{12,8},{16,20},{20,16},{24,28},{28,24},{1,5},{5... | collective-permute-start | bytes 294920 | tf_op jit(solution)/shard_map/ppermute | solution.py:36
  38.3 3.4 %collective-permute-done.13 = bf16[272,512]{1,0:T(8,128)(2,1)S(1)} collective-permute-done((bf16[272,512]{1,0:T(8,128)(2,1)S(1)}, bf16[272,512]{1,0:T(8,128)(2,1)S(1)}, u32[]{:S(2)}, u32[]{:S(2)}) %collective-permute-start.13) | collective-permute-done | bytes 278560 | tf_op jit(solution)/shard_map/ppermute | solution.py:36
  41.8 0.1 convert_element_type.159
  41.8 0.0 copy-start.6
  41.9 0.0 collective-permute-done.4
  41.9 1.6 %collective-permute-start.5 = (bf16[96,512]{1,0:T(8,128)(2,1)S(1)}, bf16[96,512]{1,0:T(8,128)(2,1)S(1)}, u32[]{:S(2)}, u32[]{:S(2)}) collective-permute-start(bf16[96,512]{1,0:T(8,128)(2,1)S(1)} %broadcast_select_fusion), channel_id=1, source_target_pairs={{0,8},{4,12},{8,0},{12,4},{16,24},{20,28},{24,16},{28,20},{1,9},{5... | collective-permute-start | bytes 294920 | tf_op jit(solution)/shard_map/ppermute | solution.py:36
  43.5 0.2 fusion.7
  43.7 2.9 %collective-permute-done.5 = bf16[96,512]{1,0:T(8,128)(2,1)S(1)} collective-permute-done((bf16[96,512]{1,0:T(8,128)(2,1)S(1)}, bf16[96,512]{1,0:T(8,128)(2,1)S(1)}, u32[]{:S(2)}, u32[]{:S(2)}) %collective-permute-start.5) | collective-permute-done | bytes 98336 | tf_op jit(solution)/shard_map/ppermute | solution.py:36
  46.6 2.7 %collective-permute-start.6 = (bf16[96,512]{1,0:T(8,128)(2,1)S(1)}, bf16[96,512]{1,0:T(8,128)(2,1)S(1)}, u32[]{:S(2)}, u32[]{:S(2)}) collective-permute-start(bf16[96,512]{1,0:T(8,128)(2,1)S(1)} %broadcast_select_fusion.1), channel_id=1, source_target_pairs={{0,16},{4,20},{8,24},{12,28},{16,0},{20,4},{24,8},{28,12},{1,17},{... | collective-permute-start | bytes 294920 | tf_op jit(solution)/shard_map/ppermute | solution.py:36
  49.3 0.0 collective-permute-start.14
  49.3 2.9 %collective-permute-done.6 = bf16[96,512]{1,0:T(8,128)(2,1)S(1)} collective-permute-done((bf16[96,512]{1,0:T(8,128)(2,1)S(1)}, bf16[96,512]{1,0:T(8,128)(2,1)S(1)}, u32[]{:S(2)}, u32[]{:S(2)}) %collective-permute-start.6) | collective-permute-done | bytes 98336 | tf_op jit(solution)/shard_map/ppermute | solution.py:36
  52.2 0.3 fusion.6
  52.6 0.0 copy-start.7
  52.6 0.0 collective-permute-done.14
  52.6 0.2 fusion.15
  52.8 0.3 fusion.37
  53.1 1.6 %collective-permute-start.15 = (bf16[64,512]{1,0:T(8,128)(2,1)S(1)}, bf16[64,512]{1,0:T(8,128)(2,1)S(1)}, u32[]{:S(2)}, u32[]{:S(2)}) collective-permute-start(bf16[64,512]{1,0:T(8,128)(2,1)S(1)} %pad_maximum_fusion.3), channel_id=1, source_target_pairs={{0,4},{4,0},{8,12},{12,8},{16,20},{20,16},{24,28},{28,24},{1,5},{5... | collective-permute-start | bytes 196616 | tf_op jit(solution)/shard_map/ppermute | solution.py:36
  54.7 2.8 %collective-permute-done.15 = bf16[64,512]{1,0:T(8,128)(2,1)S(1)} collective-permute-done((bf16[64,512]{1,0:T(8,128)(2,1)S(1)}, bf16[64,512]{1,0:T(8,128)(2,1)S(1)}, u32[]{:S(2)}, u32[]{:S(2)}) %collective-permute-start.15) | collective-permute-done | bytes 65568 | tf_op jit(solution)/shard_map/ppermute | solution.py:36
  57.5 1.8 %collective-permute-start.16 = (bf16[64,512]{1,0:T(8,128)(2,1)S(1)}, bf16[64,512]{1,0:T(8,128)(2,1)S(1)}, u32[]{:S(2)}, u32[]{:S(2)}) collective-permute-start(bf16[64,512]{1,0:T(8,128)(2,1)S(1)} %broadcast_select_fusion.2), channel_id=1, source_target_pairs={{0,8},{4,12},{8,0},{12,4},{16,24},{20,28},{24,16},{28,20},{1,9},{5... | collective-permute-start | bytes 196616 | tf_op jit(solution)/shard_map/ppermute | solution.py:36
  59.3 0.0 collective-permute-start.7
  59.3 2.5 %collective-permute-done.16 = bf16[64,512]{1,0:T(8,128)(2,1)S(1)} collective-permute-done((bf16[64,512]{1,0:T(8,128)(2,1)S(1)}, bf16[64,512]{1,0:T(8,128)(2,1)S(1)}, u32[]{:S(2)}, u32[]{:S(2)}) %collective-permute-start.16) | collective-permute-done | bytes 65568 | tf_op jit(solution)/shard_map/ppermute | solution.py:36
  61.8 3.8 %collective-permute-start.17 = (bf16[64,512]{1,0:T(8,128)(2,1)S(1)}, bf16[64,512]{1,0:T(8,128)(2,1)S(1)}, u32[]{:S(2)}, u32[]{:S(2)}) collective-permute-start(bf16[64,512]{1,0:T(8,128)(2,1)S(1)} %broadcast_select_fusion.3), channel_id=1, source_target_pairs={{0,16},{4,20},{8,24},{12,28},{16,0},{20,4},{24,8},{28,12},{1,17},{... | collective-permute-start | bytes 196616 | tf_op jit(solution)/shard_map/ppermute | solution.py:36
  65.7 0.7 iota_compare_fusion.8
  66.3 0.0 collective-permute-done.7.far
  66.3 0.0 copy-start.8
  66.3 0.6 copy-done.8
  67.0 4.2 %shard_map.87 = (bf16[128,1024]{1,0:T(8,128)(2,1)}, f32[64,2048]{1,0:T(8,128)}, bf16[64,2048]{1,0:T(8,128)(2,1)}) custom-call(f32[128,1024]{1,0:T(8,128)} %get-tuple-element.11.base, bf16[64,512]{1,0:T(8,128)(2,1)} %copy-done.7, bf16[64,512]{1,0:T(8,128)(2,1)} %copy-done.8, bf16[1024,512]{1,0:T(8,128)(2,1)} %bitcast.35, bf16[1024,4096]{1,0:T(8,128)(2,1)} %bitcast.32), custom_call_target="tpu_custom_call" | custom-call | tf_op jit(solution)/shard_map/pallas_call | solution.py:147
  71.2 3.6 %shard_map.88 = (f32[64,2048]{1,0:T(8,128)}, bf16[64,2048]{1,0:T(8,128)(2,1)}) custom-call(bf16[128,1024]{1,0:T(8,128)(2,1)} %get-tuple-element.16.second, bf16[1024,4096]{1,0:T(8,128)(2,1)} %bitcast.33), custom_call_target="tpu_custom_call" | custom-call | tf_op jit(solution)/shard_map/pallas_call | solution.py:168
  74.8 0.5 collective-permute-start.10
  75.3 0.3 fusion.5
  75.6 0.7 multiply_bitcast_fusion
  76.3 0.0 collective-permute-done.8
  76.3 0.6 collective-permute-start.9
  77.0 1.6 %collective-permute-start.11 = (bf16[32,2048]{1,0:T(8,128)(2,1)S(1)}, bf16[32,2048]{1,0:T(8,128)(2,1)S(1)}, u32[]{:S(2)}, u32[]{:S(2)}) collective-permute-start(bf16[32,2048]{1,0:T(8,128)(2,1)S(1)} %slice.185), channel_id=1, source_target_pairs={{0,2},{1,3},{2,0},{3,1},{4,6},{5,7},{6,4},{7,5},{8,10},{9,11},{10,... | collective-permute-start | bytes 393224 | tf_op jit(solution)/shard_map/ppermute | solution.py:36
  78.6 4.2 %collective-permute-done.9 = bf16[32,2048]{1,0:T(8,128)(2,1)S(1)} collective-permute-done((bf16[32,2048]{1,0:T(8,128)(2,1)S(1)}, bf16[32,2048]{1,0:T(8,128)(2,1)S(1)}, u32[]{:S(2)}, u32[]{:S(2)}) %collective-permute-start.9) | collective-permute-done | bytes 131104 | tf_op jit(solution)/shard_map/ppermute | solution.py:36
  82.8 1.8 %collective-permute-done.11 = bf16[32,2048]{1,0:T(8,128)(2,1)S(1)} collective-permute-done((bf16[32,2048]{1,0:T(8,128)(2,1)S(1)}, bf16[32,2048]{1,0:T(8,128)(2,1)S(1)}, u32[]{:S(2)}, u32[]{:S(2)}) %collective-permute-start.11) | collective-permute-done | bytes 131104 | tf_op jit(solution)/shard_map/ppermute | solution.py:36
  84.7 0.8 maximum_select_fusion
  (44 shorter events, 0.6 us)
Async XLA Ops:
  2.5 15.0 %collective-permute-start = (bf16[32,4608]{1,0:T(8,128)(2,1)}, bf16[32,4608]{1,0:T(8,128)(2,1)S(1)}, u32[]{:S(2)}, u32[]{:S(2)}) collective-permute-start(bf16[32,4608]{1,0:T(8,128)(2,1)} %shard_map.85), channel_id=1, source_target_pairs={{0,2},{1,3},{2,0},{3,1},{4,6},{5,7},{6,4},{7,5},{8,10},{9,11},{10,... | collective-permute-start | bytes 884744 | tf_op jit(solution)/shard_map/ppermute | solution.py:36
  16.0 1.0 %copy-start = (bf16[512,1024]{0,1:T(8,128)(2,1)}, bf16[512,1024]{0,1:T(8,128)(2,1)S(1)}, u32[]{:S(2)}) copy-start(bf16[512,1024]{0,1:T(8,128)(2,1)S(1)} %select_convert_fusion) | copy-start | bytes 3145732
  16.0 1.4 %copy-start.2 = (bf16[32,4608]{1,0:T(8,128)(2,1)S(1)}, bf16[32,4608]{1,0:T(8,128)(2,1)}, u32[]{:S(2)}) copy-start(bf16[32,4608]{1,0:T(8,128)(2,1)} %shard_map.85) | copy-start | bytes 884740
  17.3 1.8 %collective-permute-start.12 = (bf16[272,512]{1,0:T(8,128)(2,1)S(1)}, bf16[272,512]{1,0:T(8,128)(2,1)}, u32[]{:S(2)}, u32[]{:S(2)}) collective-permute-start(bf16[272,512]{1,0:T(8,128)(2,1)S(1)} %maximum_maximum_fusion), channel_id=1, source_target_pairs={{0,1},{1,0},{2,3},{3,2},{4,5},{5,4},{6,7},{7,6},{8,9},{9,8},{10,11... | collective-permute-start | bytes 835592 | tf_op jit(solution)/shard_map/ppermute | solution.py:36
  17.5 2.8 %copy-start.1 = (bf16[64,4608]{1,0:T(8,128)(2,1)}, bf16[64,4608]{1,0:T(8,128)(2,1)S(1)}, u32[]{:S(2)}) copy-start(bf16[64,4608]{1,0:T(8,128)(2,1)S(1)} %pad_maximum_fusion.near) | copy-start | bytes 1769476
  17.5 2.7 %collective-permute-start.1 = (bf16[64,4608]{1,0:T(8,128)(2,1)S(1)}, bf16[64,4608]{1,0:T(8,128)(2,1)S(1)}, u32[]{:S(2)}, u32[]{:S(2)}) collective-permute-start(bf16[64,4608]{1,0:T(8,128)(2,1)S(1)} %pad_maximum_fusion.near), channel_id=1, source_target_pairs={{0,1},{1,0},{2,3},{3,2},{4,5},{5,4},{6,7},{7,6},{8,9},{9,8},{10,11... | collective-permute-start | bytes 1769480 | tf_op jit(solution)/shard_map/ppermute | solution.py:36
  20.2 0.8 copy-start.3
  28.3 1.6 %collective-permute-start.2 = (f32[64,512]{1,0:T(8,128)}, f32[64,512]{1,0:T(8,128)S(1)}, u32[]{:S(2)}, u32[]{:S(2)}) collective-permute-start(f32[64,512]{1,0:T(8,128)} %get-tuple-element.13), channel_id=1, source_target_pairs={{0,1},{1,0},{2,3},{3,2},{4,5},{5,4},{6,7},{7,6},{8,9},{9,8},{10,11... | collective-permute-start | bytes 393224 | tf_op jit(solution)/shard_map/ppermute | solution.py:36
  30.9 5.7 %collective-permute-start.3 = (bf16[96,512]{1,0:T(8,128)(2,1)S(1)}, bf16[96,512]{1,0:T(8,128)(2,1)S(1)}, u32[]{:S(2)}, u32[]{:S(2)}) collective-permute-start(bf16[96,512]{1,0:T(8,128)(2,1)S(1)} %pad_maximum_fusion.1), channel_id=1, source_target_pairs={{0,2},{1,3},{2,0},{3,1},{4,6},{5,7},{6,4},{7,5},{8,10},{9,11},{10,... | collective-permute-start | bytes 294920 | tf_op jit(solution)/shard_map/ppermute | solution.py:36
  31.1 10.7 %collective-permute-start.13 = (bf16[272,512]{1,0:T(8,128)(2,1)S(1)}, bf16[272,512]{1,0:T(8,128)(2,1)S(1)}, u32[]{:S(2)}, u32[]{:S(2)}) collective-permute-start(bf16[272,512]{1,0:T(8,128)(2,1)S(1)} %maximum_maximum_fusion.1), channel_id=1, source_target_pairs={{0,2},{1,3},{2,0},{3,1},{4,6},{5,7},{6,4},{7,5},{8,10},{9,11},{10,... | collective-permute-start | bytes 835592 | tf_op jit(solution)/shard_map/ppermute | solution.py:36
  36.7 5.1 %collective-permute-start.4 = (bf16[96,512]{1,0:T(8,128)(2,1)S(1)}, bf16[96,512]{1,0:T(8,128)(2,1)S(1)}, u32[]{:S(2)}, u32[]{:S(2)}) collective-permute-start(bf16[96,512]{1,0:T(8,128)(2,1)S(1)} %pad_maximum_fusion.2), channel_id=1, source_target_pairs={{0,4},{4,0},{8,12},{12,8},{16,20},{20,16},{24,28},{28,24},{1,5},{5... | collective-permute-start | bytes 294920 | tf_op jit(solution)/shard_map/ppermute | solution.py:36
  41.8 10.7 %copy-start.6 = (f32[1,32,512]{2,1,0:T(8,128)S(1)}, f32[1,32,512]{2,1,0:T(8,128)}, u32[]{:S(2)}) copy-start(f32[1,32,512]{2,1,0:T(8,128)} %param.8) | copy-start | bytes 196612
  41.9 4.7 %collective-permute-start.5 = (bf16[96,512]{1,0:T(8,128)(2,1)S(1)}, bf16[96,512]{1,0:T(8,128)(2,1)S(1)}, u32[]{:S(2)}, u32[]{:S(2)}) collective-permute-start(bf16[96,512]{1,0:T(8,128)(2,1)S(1)} %broadcast_select_fusion), channel_id=1, source_target_pairs={{0,8},{4,12},{8,0},{12,4},{16,24},{20,28},{24,16},{28,20},{1,9},{5... | collective-permute-start | bytes 294920 | tf_op jit(solution)/shard_map/ppermute | solution.py:36
  46.6 5.6 %collective-permute-start.6 = (bf16[96,512]{1,0:T(8,128)(2,1)S(1)}, bf16[96,512]{1,0:T(8,128)(2,1)S(1)}, u32[]{:S(2)}, u32[]{:S(2)}) collective-permute-start(bf16[96,512]{1,0:T(8,128)(2,1)S(1)} %broadcast_select_fusion.1), channel_id=1, source_target_pairs={{0,16},{4,20},{8,24},{12,28},{16,0},{20,4},{24,8},{28,12},{1,17},{... | collective-permute-start | bytes 294920 | tf_op jit(solution)/shard_map/ppermute | solution.py:36
  49.3 3.3 %collective-permute-start.14 = (bf16[256,512]{1,0:T(8,128)(2,1)S(1)}, bf16[256,512]{1,0:T(8,128)(2,1)S(1)}, u32[]{:S(2)}, u32[]{:S(2)}) collective-permute-start(bf16[256,512]{1,0:T(8,128)(2,1)S(1)} %fusion.7), channel_id=1, source_target_pairs={{0,1},{1,0},{2,3},{3,2},{4,5},{5,4},{6,7},{7,6},{8,9},{9,8},{10,11... | collective-permute-start | bytes 786440 | tf_op jit(solution)/shard_map/ppermute | solution.py:36
  52.6 6.7 %copy-start.7 = (bf16[64,512]{1,0:T(8,128)(2,1)}, bf16[64,512]{1,0:T(8,128)(2,1)S(1)}, u32[]{:S(2)}) copy-start(bf16[64,512]{1,0:T(8,128)(2,1)S(1)} %get-tuple-element.33.near) | copy-start | bytes 196612
  53.1 4.3 %collective-permute-start.15 = (bf16[64,512]{1,0:T(8,128)(2,1)S(1)}, bf16[64,512]{1,0:T(8,128)(2,1)S(1)}, u32[]{:S(2)}, u32[]{:S(2)}) collective-permute-start(bf16[64,512]{1,0:T(8,128)(2,1)S(1)} %pad_maximum_fusion.3), channel_id=1, source_target_pairs={{0,4},{4,0},{8,12},{12,8},{16,20},{20,16},{24,28},{28,24},{1,5},{5... | collective-permute-start | bytes 196616 | tf_op jit(solution)/shard_map/ppermute | solution.py:36
  57.5 4.3 %collective-permute-start.16 = (bf16[64,512]{1,0:T(8,128)(2,1)S(1)}, bf16[64,512]{1,0:T(8,128)(2,1)S(1)}, u32[]{:S(2)}, u32[]{:S(2)}) collective-permute-start(bf16[64,512]{1,0:T(8,128)(2,1)S(1)} %broadcast_select_fusion.2), channel_id=1, source_target_pairs={{0,8},{4,12},{8,0},{12,4},{16,24},{20,28},{24,16},{28,20},{1,9},{5... | collective-permute-start | bytes 196616 | tf_op jit(solution)/shard_map/ppermute | solution.py:36
  59.3 7.1 %collective-permute-start.7 = (bf16[64,512]{1,0:T(8,128)(2,1)S(1)}, bf16[64,512]{1,0:T(8,128)(2,1)S(1)}, u32[]{:S(2)}, u32[]{:S(2)}) collective-permute-start(bf16[64,512]{1,0:T(8,128)(2,1)S(1)} %get-tuple-element.33.near), channel_id=1, source_target_pairs={{0,1},{1,0},{2,3},{3,2},{4,5},{5,4},{6,7},{7,6},{8,9},{9,8},{10,11... | collective-permute-start | bytes 196616 | tf_op jit(solution)/shard_map/ppermute | solution.py:36
  61.8 13.5 %collective-permute-start.17 = (bf16[64,512]{1,0:T(8,128)(2,1)S(1)}, bf16[64,512]{1,0:T(8,128)(2,1)S(1)}, u32[]{:S(2)}, u32[]{:S(2)}) collective-permute-start(bf16[64,512]{1,0:T(8,128)(2,1)S(1)} %broadcast_select_fusion.3), channel_id=1, source_target_pairs={{0,16},{4,20},{8,24},{12,28},{16,0},{20,4},{24,8},{28,12},{1,17},{... | collective-permute-start | bytes 196616 | tf_op jit(solution)/shard_map/ppermute | solution.py:36
  66.3 0.6 copy-start.8
  71.2 5.1 %collective-permute-start.8 = (bf16[64,2048]{1,0:T(8,128)(2,1)}, bf16[64,2048]{1,0:T(8,128)(2,1)S(1)}, u32[]{:S(2)}, u32[]{:S(2)}) collective-permute-start(bf16[64,2048]{1,0:T(8,128)(2,1)} %get-tuple-element.15), channel_id=1, source_target_pairs={{0,1},{1,0},{2,3},{3,2},{4,5},{5,4},{6,7},{7,6},{8,9},{9,8},{10,11... | collective-permute-start | bytes 786440 | tf_op jit(solution)/shard_map/ppermute | solution.py:36
  71.2 5.1 %copy-start.5 = (f32[64,2048]{1,0:T(8,128)S(1)}, f32[64,2048]{1,0:T(8,128)}, u32[]{:S(2)}) copy-start(f32[64,2048]{1,0:T(8,128)} %get-tuple-element.14) | copy-start | bytes 1572868
  74.8 2.1 %copy-start.4 = (f32[64,2048]{1,0:T(8,128)S(1)}, f32[64,2048]{1,0:T(8,128)}, u32[]{:S(2)}) copy-start(f32[64,2048]{1,0:T(8,128)} %get-tuple-element.17) | copy-start | bytes 1572868
  74.8 2.1 %collective-permute-start.10 = (bf16[64,2048]{1,0:T(8,128)(2,1)}, bf16[64,2048]{1,0:T(8,128)(2,1)S(1)}, u32[]{:S(2)}, u32[]{:S(2)}) collective-permute-start(bf16[64,2048]{1,0:T(8,128)(2,1)} %get-tuple-element.18), channel_id=1, source_target_pairs={{0,1},{1,0},{2,3},{3,2},{4,5},{5,4},{6,7},{7,6},{8,9},{9,8},{10,11... | collective-permute-start | bytes 786440 | tf_op jit(solution)/shard_map/ppermute | solution.py:36
  76.3 6.4 %collective-permute-start.9 = (bf16[32,2048]{1,0:T(8,128)(2,1)S(1)}, bf16[32,2048]{1,0:T(8,128)(2,1)S(1)}, u32[]{:S(2)}, u32[]{:S(2)}) collective-permute-start(bf16[32,2048]{1,0:T(8,128)(2,1)S(1)} %slice.186), channel_id=1, source_target_pairs={{0,2},{1,3},{2,0},{3,1},{4,6},{5,7},{6,4},{7,5},{8,10},{9,11},{10,... | collective-permute-start | bytes 393224 | tf_op jit(solution)/shard_map/ppermute | solution.py:36
  77.0 7.6 %collective-permute-start.11 = (bf16[32,2048]{1,0:T(8,128)(2,1)S(1)}, bf16[32,2048]{1,0:T(8,128)(2,1)S(1)}, u32[]{:S(2)}, u32[]{:S(2)}) collective-permute-start(bf16[32,2048]{1,0:T(8,128)(2,1)S(1)} %slice.185), channel_id=1, source_target_pairs={{0,2},{1,3},{2,0},{3,1},{4,6},{5,7},{6,4},{7,5},{8,10},{9,11},{10,... | collective-permute-start | bytes 393224 | tf_op jit(solution)/shard_map/ppermute | solution.py:36

commit v2 on v1

v2 whole, which is shorter than its diff:
```python
import functools

import jax
import jax.numpy as jnp
from jax import lax
from jax.experimental import pallas as pl
from jax.experimental.pallas import tpu as pltpu
from jax.sharding import PartitionSpec as P


CAP = 128
PENALTY = 1.5
PROXIMAL = 0.5
DENOM = 2.0 * PENALTY + PROXIMAL

F32 = jnp.float32
BF16 = jnp.bfloat16

WHOLE = pl.BlockSpec(memory_space=pltpu.VMEM)
SCALARS = pl.BlockSpec(memory_space=pltpu.SMEM)


def dot_nt(a, b):
    return lax.dot_general(a, b, (((1,), (1,)), ((), ())), preferred_element_type=F32)


def dot_nn(a, b):
    return jnp.dot(a, b, preferred_element_type=F32)


def swap(x, axis, bit):
    n = lax.axis_size(axis)
    return lax.ppermute(x, axis, [(i, i ^ bit) for i in range(n)])


def halves(x):
    high = x.astype(BF16)
    return high, (x - high.astype(F32)).astype(BF16)


def out(shape, dtype):
    return jax.ShapeDtypeStruct(shape, dtype)


def plain_kernel(area_size, injection, dual, packed):
    width = injection.shape[1]
    live = lax.broadcasted_iota(jnp.int32, injection.shape, 1) < area_size[lax.axis_index("area")]
    packed[:, :width] = jnp.where(live, injection[...], 0.0).astype(BF16)
    packed[:, width:] = dual[...].astype(BF16)


def packed_side(area_size, injection, dual):
    return pl.pallas_call(
        plain_kernel,
        out_shape=out((injection.shape[0], injection.shape[1] + dual.shape[1]), BF16),
        in_specs=[SCALARS, WHOLE, WHOLE],
        out_specs=WHOLE,
    )(area_size, injection, dual)


def base_kernel(area_size, near, far, dual, factor, factor_ends, base, keep, send, side, partial):
    step = pl.program_id(0)
    half = near.shape[0]
    block, width = factor.shape

    @pl.when(step == 0)
    def _():
        side[:half] = near[...]
        side[half:] = far[...]
        partial[...] = jnp.zeros_like(partial)

    here = factor_ends[...]
    value = dot_nt(side[:, :width], factor[...])
    start = lax.axis_index("scen") * (pl.num_programs(0) * block) + step * block
    live = start + lax.broadcasted_iota(jnp.int32, value.shape, 1) < area_size[lax.axis_index("area")]
    base[...] = value
    first = jnp.where(live, value - dot_nt(side[:, width:], here), 0.0).astype(BF16)
    partial[...] += dot_nn(first, here)

    @pl.when(step == pl.num_programs(0) - 1)
    def _():
        count = dual.shape[0]
        keep[:count] = PENALTY * partial[:count] + dual[...]
        keep[count:] = PENALTY * partial[count:half]
        send[...] = PENALTY * partial[half:]


def base_product(area_size, near, far, dual, factor, factor_ends):
    rows, width = factor.shape
    half, packed_width = near.shape
    ends_total = factor_ends.shape[1]
    block = 512
    fixed = pl.BlockSpec((half, ends_total), lambda i: (0, 0))
    return pl.pallas_call(
        base_kernel,
        grid=(rows // block,),
        out_shape=(
            out((2 * half, rows), F32),
            out((half, ends_total), F32),
            out((half, ends_total), F32),
        ),
        in_specs=[
            SCALARS,
            WHOLE,
            WHOLE,
            WHOLE,
            pl.BlockSpec((block, width), lambda i: (i, 0)),
            pl.BlockSpec((block, ends_total), lambda i: (i, 0)),
        ],
        out_specs=(pl.BlockSpec((2 * half, block), lambda i: (0, i)), fixed, fixed),
        scratch_shapes=[
            pltpu.VMEM((2 * half, packed_width), BF16),
            pltpu.VMEM((2 * half, ends_total), F32),
        ],
    )(area_size, near, far, dual, factor, factor_ends)


def second_kernel(area_size, base, near, far, factor_ends, second, keep, send, spread):
    half = near.shape[0]
    spread[:half] = near[...]
    spread[half:] = far[...]
    here = factor_ends[...]
    start = lax.axis_index("scen") * here.shape[0]
    live = start + lax.broadcasted_iota(jnp.int32, base.shape, 1) < area_size[lax.axis_index("area")]
    rows = jnp.where(live, base[...] - dot_nt(spread[...], here), 0.0).astype(BF16)
    second[...] = rows
    partial = PENALTY * dot_nn(rows, here)
    keep[...] = partial[:half]
    send[...] = partial[half:]


def second_product(area_size, base, near, far, factor_ends):
    half, ends_total = near.shape
    shape = out((half, ends_total), F32)
    return pl.pallas_call(
        second_kernel,
        out_shape=(out(base.shape, BF16), shape, shape),
        in_specs=[SCALARS, WHOLE, WHOLE, WHOLE, WHOLE],
        out_specs=(WHOLE, WHOLE, WHOLE),
        scratch_shapes=[pltpu.VMEM((2 * half, ends_total), BF16)],
    )(area_size, base, near, far, factor_ends)


def angles_kernel(first_bus, area_size, second, factor, keep, send):
    half, depth = keep.shape
    value = dot_nn(second[...], factor[...])
    start = first_bus + pl.program_id(0) * depth
    live = start + lax.broadcasted_iota(jnp.int32, value.shape, 1) < area_size[lax.axis_index("area")]
    value = jnp.where(live, value, 0.0)
    keep[...] = value[:half]
    send[...] = value[half:].astype(BF16)


def angles_product(area_size, second, factor, parts, part):
    rows, width = factor.shape
    half = second.shape[0] // 2
    depth = 1024
    size = width // parts
    steps = size // depth
    spec = pl.BlockSpec((half, depth), lambda i: (0, i))
    return pl.pallas_call(
        functools.partial(angles_kernel, part * size),
        grid=(steps,),
        out_shape=(out((half, size), F32), out((half, size), BF16)),
        in_specs=[SCALARS, WHOLE, pl.BlockSpec((rows, depth), lambda i: (0, part * steps + i))],
        out_specs=(spec, spec),
    )(area_size, second, factor)


def shards(injection, kkt_factor, dual_price, area_size, bnd_bus, peer_end):
    area_id = lax.axis_index("area")
    areas_all = lax.axis_size("area")
    factor = kkt_factor[0]
    width = factor.shape[1]
    injection_here = injection[0]
    dual_here = dual_price[0]
    columns, ends_total = dual_here.shape
    buses = bnd_bus[area_id]
    peers = peer_end[area_id]
    offset = (peers // ends_total) ^ area_id

    packed = packed_side(area_size, injection_here, dual_here)
    other = swap(packed, "scen", 2)
    pair = jnp.concatenate([packed, other], axis=0)
    pair_far = swap(pair, "scen", 1)

    pick = (jnp.arange(width)[:, None] == buses[None, :]).astype(BF16)
    factor_ends = dot_nn(factor, pick).astype(BF16)
    slots = jnp.arange(ends_total)
    mate = ((slots // CAP * CAP + peers % CAP)[None, :] == slots[:, None]).astype(BF16)

    base, keep, send = base_product(
        area_size, pair, pair_far, dual_here, factor, factor_ends
    )

    def exchange(q):
        moved = q
        bit = 1
        while bit < areas_all:
            moved = jnp.where((offset & bit)[None, :] != 0, swap(moved, "area", bit), moved)
            bit *= 2
        return dot_nn(moved, mate)

    def with_low(x, low_rows):
        high, low = halves(x)
        return jnp.concatenate([high, low[low_rows]], axis=0)

    pair_rows = 2 * columns
    keep = keep + swap(send, "scen", 1)
    pair_rows = 2 * columns
    first_rows, last_rows = slice(0, columns), slice(columns, pair_rows)
    other = swap(with_low(keep, last_rows), "scen", 2).astype(F32)
    q = keep + jnp.concatenate([other[last_rows] + other[pair_rows:], other[first_rows]], axis=0)
    moved = exchange(with_low(q, first_rows))
    moved = jnp.concatenate([moved[first_rows] + moved[pair_rows:], moved[last_rows]], axis=0)
    consensus = (q + moved) / DENOM
    spread = q - 2.0 * PENALTY * consensus
    spread_pair = spread.astype(BF16)
    spread_far = swap(spread_pair, "scen", 1)

    q_own, consensus_own = q[:columns], consensus[:columns]
    second, keep, send = second_product(area_size, base, spread_pair, spread_far, factor_ends)
    far = swap(send, "scen", 1)
    keep = keep + far
    other = swap(with_low(keep[columns:], first_rows), "scen", 2).astype(F32)
    parts = 2
    products = []
    for part in range(parts):
        products.append(angles_product(area_size, second, factor, parts, part))
    q_last = keep[:columns] + other[first_rows] + other[last_rows]
    q_last = q_last + (q_own - PENALTY * consensus_own)
    moved = exchange(with_low(q_last, first_rows))
    moved = moved[first_rows] + moved[last_rows]
    consensus_last = (q_last + moved + PROXIMAL * consensus_own) / DENOM
    dual_last = q_last - PENALTY * consensus_last

    pieces = []
    for keep, send in products:
        keep = keep + swap(send, "scen", 1).astype(F32)
        pieces.append(keep[:columns] + swap(keep[columns:].astype(BF16), "scen", 2).astype(F32))
    angles_here = jnp.concatenate(pieces, axis=1)
    return (angles_here[None], dual_last[None], consensus_last[None])


def solution(mesh):
    spec = P("area", "scen", None)
    return jax.shard_map(
        shards,
        mesh=mesh,
        in_specs=(spec, spec, spec, P(), P(), P()),
        out_specs=(spec, spec, spec),
        check_vma=False,
    )
```

time: 85.9 us -> 89.5 us (1.042)
  starting transfers between devices: 21.6 us -> 24.5 us
  Pallas kernels: 16.9 us -> 19 us
  local copies, waits for them, and re-layouts: 3.08 us -> 1.49 us
  waiting for transfers between devices: 26.5 us -> 27.7 us
    ppermute x18 -> x17, starting transfers between devices: 21.6 us -> 24.5 us  [swap(): return lax.ppermute(x, axis, [(i, i ^ bit) for i in range(n)])]
    pallas_call x2 -> x3, Pallas kernels: 7.81 us -> 9.94 us  [the longest x2 7.15 us: angles_product(): pl.pallas_call(functools.partial(angles_kernel, part * size), grid=(steps...]
    convert_element_type x4 -> x1, other arithmetic: 1.33 us -> 0.01 us  [shards(): other = swap(with_low(keep[columns:], first_rows), 'scen', 2).astype(F32)]
    lt x2 -> x0, other arithmetic: 1.3 us -> none  [the longest x1 0.65 us: shards(): live_mask = jnp.arange(width) < size_here]
    ppermute x18 -> x17, waiting for transfers between devices: 26.5 us -> 27.7 us  [swap(): return lax.ppermute(x, axis, [(i, i ^ bit) for i in range(n)])]
    dynamic_slice x1 -> x0, local copies, waits for them, and re-layouts: 1.24 us -> none  [shards(): size_here = area_size[area_id]]
    add x2, other arithmetic: 0.09 us -> 1.15 us  [shards(): keep = keep + swap(send, 'scen', 1).astype(F32)]
    add x1 -> x3, other arithmetic: 0.01 us -> 0.99 us  [the longest x1 0.92 us: shards(): keep = keep + far]
  transfers between devices with their start and end apart: 18 -> 17, of which waited for: 10 -> 11; matrix products, arithmetic and copies ran while one was open for 18% -> 13% of each run, Pallas kernels for 9% -> 8%
where the time goes in v2:
time: 89.5 us; the launch traced here: 89.2 us
  waiting for transfers between devices  27.7 us (31%)
  starting transfers between devices  24.5 us (27%)
  Pallas kernels  19 us (21%)
  matrix products  8.9 us (10%)
  other arithmetic  6.64 us (7%)
  local copies, waits for them, and re-layouts  1.49 us (2%)
    ppermute x17, waiting for transfers between devices, swap(): return lax.ppermute(x, axis, [(i, i ^ bit) for i in range(n)])  27.7 us
    ppermute x17, starting transfers between devices, swap(): return lax.ppermute(x, axis, [(i, i ^ bit) for i in range(n)])  24.5 us
    dot_general x3, matrix products, dot_nn(): return jnp.dot(a, b, preferred_element_type=F32)  8.9 us
    pallas_call x1, Pallas kernels, base_product(): pl.pallas_call(base_kernel, grid=(rows // block,), out_shape=(out((2 * ha...  7.28 us
    pallas_call x2, Pallas kernels, angles_product(): pl.pallas_call(functools.partial(angles_kernel, part * size), grid=(steps...  7.15 us
    pallas_call x1, Pallas kernels, second_product(): pl.pallas_call(second_kernel, out_shape=(out(base.shape, BF16), shape, sh...  2.78 us
    pallas_call x1, Pallas kernels, packed_side(): pl.pallas_call(plain_kernel, out_shape=out((injection.shape[0], injection...  1.82 us
  transfers between devices with their start and end apart: 17, of which 11 were waited for; matrix products, arithmetic and copies ran while one was open for 13% of the time, Pallas kernels for 8%

profile of v2, /device:TPU:0, one launch (start us, length us, event | category | flops | bytes accessed | tf_op | source)
XLA Modules:
  0.0 89.2 jit_solution(3133032175771877718)
XLA Ops:
  0.6 1.8 %shard_map.85 = bf16[32,4608]{1,0:T(8,128)(2,1)} custom-call(s32[8]{0:T(128)} %area_size.9, f32[32,4096]{1,0:T(8,128)} %bitcast.18, f32[32,512]{1,0:T(8,128)} %bitcast.19), custom_call_target="tpu_custom_call" | custom-call | tf_op jit(solution)/shard_map/pallas_call | solution.py:53
  2.5 3.0 %collective-permute-start = (bf16[32,4608]{1,0:T(8,128)(2,1)}, bf16[32,4608]{1,0:T(8,128)(2,1)S(1)}, u32[]{:S(2)}, u32[]{:S(2)}) collective-permute-start(bf16[32,4608]{1,0:T(8,128)(2,1)} %shard_map.85), channel_id=1, source_target_pairs={{0,2},{1,3},{2,0},{3,1},{4,6},{5,7},{6,4},{7,5},{8,10},{9,11},{10,... | collective-permute-start | bytes 884744 | tf_op jit(solution)/shard_map/ppermute | solution.py:33
  5.5 0.8 fusion.18
  6.2 6.5 %collective-permute-done = bf16[32,4608]{1,0:T(8,128)(2,1)S(1)} collective-permute-done((bf16[32,4608]{1,0:T(8,128)(2,1)}, bf16[32,4608]{1,0:T(8,128)(2,1)S(1)}, u32[]{:S(2)}, u32[]{:S(2)}) %collective-permute-start) | collective-permute-done | bytes 294944 | tf_op jit(solution)/shard_map/ppermute | solution.py:33
  12.7 1.0 %pad_maximum_fusion.near = bf16[64,4608]{1,0:T(8,128)(2,1)S(1)} fusion(bf16[32,4608]{1,0:T(8,128)(2,1)S(1)} %collective-permute-done, bf16[32,4608]{1,0:T(8,128)(2,1)} %shard_map.85), kind=kLoop, calls=%fused_computation.8 | loop fusion | flops 1179648 | bytes 1179648 | tf_op jit(solution)/shard_map/concatenate | solution.py:184
  13.7 0.0 copy-start
  13.7 0.1 collective-permute-start.1
  13.8 8.3 %fusion.3.factor_ends = bf16[1024,512]{1,0:T(8,128)(2,1)} fusion(s32[512]{0:T(512)S(1)} %bitcast.23, bf16[1,1024,4096]{2,1,0:T(8,128)(2,1)} %param.7), kind=kOutput, calls=%fused_computation.4 | convolution fusion | flops 4297588736 | bytes 9439232 | tf_op jit(solution)/shard_map/dot_general | solution.py:28
  22.1 0.0 copy-done
  22.1 0.0 collective-permute-done.1.far
  22.1 0.0 copy-start.1
  22.1 0.8 copy-done.1
  22.9 7.3 %shard_map.86 = (f32[128,1024]{1,0:T(8,128)}, f32[64,512]{1,0:T(8,128)}, f32[64,512]{1,0:T(8,128)}) custom-call(s32[8]{0:T(128)} %area_size.9, bf16[64,4608]{1,0:T(8,128)(2,1)} %copy-done, bf16[64,4608]{1,0:T(8,128)(2,1)} %copy-done.1, f32[32,512]{1,0:T(8,128)} %bitcast.20, bf16[1024,4096]{1,0:T(8,128)(2,1)} %bitcast.15, bf16[1024,512]{1,0:T(8,128)(2,1)} %fusion.3.factor_ends), custom_call_target="tpu_custom_call" | custom-call | tf_op jit(solution)/shard_map/pallas_call | solution.py:94
  30.2 0.4 collective-permute-start.2
  30.6 1.2 %collective-permute-done.2 = f32[64,512]{1,0:T(8,128)S(1)} collective-permute-done((f32[64,512]{1,0:T(8,128)}, f32[64,512]{1,0:T(8,128)S(1)}, u32[]{:S(2)}, u32[]{:S(2)}) %collective-permute-start.2) | collective-permute-done | bytes 131104 | tf_op jit(solution)/shard_map/ppermute | solution.py:33
  31.8 0.9 %fusion.23 = (bf16[64,512]{1,0:T(8,128)(2,1)S(1)}, f32[64,512]{1,0:T(8,128)S(1)}) fusion(f32[64,512]{1,0:T(8,128)} %get-tuple-element.14, f32[64,512]{1,0:T(8,128)S(1)} %collective-permute-done.2), kind=kLoop, calls=%fused_computation.70 | loop fusion | flops 65536 | bytes 458752 | tf_op jit(solution)/shard_map/convert_element_type | solution.py:37
  32.7 1.8 %collective-permute-start.3 = (bf16[96,512]{1,0:T(8,128)(2,1)S(1)}, bf16[96,512]{1,0:T(8,128)(2,1)S(1)}, u32[]{:S(2)}, u32[]{:S(2)}) collective-permute-start(bf16[96,512]{1,0:T(8,128)(2,1)S(1)} %pad_maximum_fusion.1), channel_id=1, source_target_pairs={{0,2},{1,3},{2,0},{3,1},{4,6},{5,7},{6,4},{7,5},{8,10},{9,11},{10,... | collective-permute-start | bytes 294920 | tf_op jit(solution)/shard_map/ppermute | solution.py:33
  34.5 3.3 %collective-permute-done.3 = bf16[96,512]{1,0:T(8,128)(2,1)S(1)} collective-permute-done((bf16[96,512]{1,0:T(8,128)(2,1)S(1)}, bf16[96,512]{1,0:T(8,128)(2,1)S(1)}, u32[]{:S(2)}, u32[]{:S(2)}) %collective-permute-start.3) | collective-permute-done | bytes 98336 | tf_op jit(solution)/shard_map/ppermute | solution.py:33
  38.0 1.8 %collective-permute-start.4 = (bf16[96,512]{1,0:T(8,128)(2,1)S(1)}, bf16[96,512]{1,0:T(8,128)(2,1)S(1)}, u32[]{:S(2)}, u32[]{:S(2)}) collective-permute-start(bf16[96,512]{1,0:T(8,128)(2,1)S(1)} %pad_maximum_fusion.2), channel_id=1, source_target_pairs={{0,4},{4,0},{8,12},{12,8},{16,20},{20,16},{24,28},{28,24},{1,5},{5... | collective-permute-start | bytes 294920 | tf_op jit(solution)/shard_map/ppermute | solution.py:33
  39.8 2.9 %collective-permute-done.4 = bf16[96,512]{1,0:T(8,128)(2,1)S(1)} collective-permute-done((bf16[96,512]{1,0:T(8,128)(2,1)S(1)}, bf16[96,512]{1,0:T(8,128)(2,1)S(1)}, u32[]{:S(2)}, u32[]{:S(2)}) %collective-permute-start.4) | collective-permute-done | bytes 98336 | tf_op jit(solution)/shard_map/ppermute | solution.py:33
  42.7 1.9 %collective-permute-start.5 = (bf16[96,512]{1,0:T(8,128)(2,1)S(1)}, bf16[96,512]{1,0:T(8,128)(2,1)S(1)}, u32[]{:S(2)}, u32[]{:S(2)}) collective-permute-start(bf16[96,512]{1,0:T(8,128)(2,1)S(1)} %broadcast_select_fusion), channel_id=1, source_target_pairs={{0,8},{4,12},{8,0},{12,4},{16,24},{20,28},{24,16},{28,20},{1,9},{5... | collective-permute-start | bytes 294920 | tf_op jit(solution)/shard_map/ppermute | solution.py:33
  44.6 2.8 %collective-permute-done.5 = bf16[96,512]{1,0:T(8,128)(2,1)S(1)} collective-permute-done((bf16[96,512]{1,0:T(8,128)(2,1)S(1)}, bf16[96,512]{1,0:T(8,128)(2,1)S(1)}, u32[]{:S(2)}, u32[]{:S(2)}) %collective-permute-start.5) | collective-permute-done | bytes 98336 | tf_op jit(solution)/shard_map/ppermute | solution.py:33
  47.4 3.1 %collective-permute-start.6 = (bf16[96,512]{1,0:T(8,128)(2,1)S(1)}, bf16[96,512]{1,0:T(8,128)(2,1)S(1)}, u32[]{:S(2)}, u32[]{:S(2)}) collective-permute-start(bf16[96,512]{1,0:T(8,128)(2,1)S(1)} %broadcast_select_fusion.1), channel_id=1, source_target_pairs={{0,16},{4,20},{8,24},{12,28},{16,0},{20,4},{24,8},{28,12},{1,17},{... | collective-permute-start | bytes 294920 | tf_op jit(solution)/shard_map/ppermute | solution.py:33
  50.5 2.6 %collective-permute-done.6 = bf16[96,512]{1,0:T(8,128)(2,1)S(1)} collective-permute-done((bf16[96,512]{1,0:T(8,128)(2,1)S(1)}, bf16[96,512]{1,0:T(8,128)(2,1)S(1)}, u32[]{:S(2)}, u32[]{:S(2)}) %collective-permute-start.6) | collective-permute-done | bytes 98336 | tf_op jit(solution)/shard_map/ppermute | solution.py:33
  53.1 0.3 fusion.5
  53.5 0.0 copy-start.3
  53.5 0.1 collective-permute-start.7
  53.6 1.2 %collective-permute-done.7.far = bf16[64,512]{1,0:T(8,128)(2,1)S(1)} collective-permute-done((bf16[64,512]{1,0:T(8,128)(2,1)S(1)}, bf16[64,512]{1,0:T(8,128)(2,1)S(1)}, u32[]{:S(2)}, u32[]{:S(2)}) %collective-permute-start.7) | collective-permute-done | bytes 65568 | tf_op jit(solution)/shard_map/ppermute | solution.py:33
  54.8 0.0 copy-start.4
  54.8 0.0 copy-done.3
  54.8 0.6 copy-done.4
  55.4 2.8 %shard_map.87 = (bf16[128,1024]{1,0:T(8,128)(2,1)}, f32[64,512]{1,0:T(8,128)}, f32[64,512]{1,0:T(8,128)}) custom-call(s32[8]{0:T(128)} %area_size.9, f32[128,1024]{1,0:T(8,128)} %get-tuple-element.13.base, bf16[64,512]{1,0:T(8,128)(2,1)} %copy-done.3, bf16[64,512]{1,0:T(8,128)(2,1)} %copy-done.4, bf16[1024,512]{1,0:T(8,128)(2,1)} %fusion.3.factor_ends), custom_call_target="tpu_custom_call" | custom-call | tf_op jit(solution)/shard_map/pallas_call | solution.py:135
  58.2 0.2 collective-permute-start.12
  58.4 1.4 %collective-permute-done.12 = f32[64,512]{1,0:T(8,128)S(1)} collective-permute-done((f32[64,512]{1,0:T(8,128)}, f32[64,512]{1,0:T(8,128)S(1)}, u32[]{:S(2)}, u32[]{:S(2)}) %collective-permute-start.12) | collective-permute-done | bytes 131104 | tf_op jit(solution)/shard_map/ppermute | solution.py:33
  59.8 0.9 %add.87 = f32[64,512]{1,0:T(8,128)S(1)} add(f32[64,512]{1,0:T(8,128)} %get-tuple-element.21, f32[64,512]{1,0:T(8,128)S(1)} %collective-permute-done.12) | non-fusion elementwise | flops 32768 | bytes 393216 | tf_op jit(solution)/shard_map/add | solution.py:224
  60.7 1.7 %collective-permute-start.13 = (bf16[64,512]{1,0:T(8,128)(2,1)S(1)}, bf16[64,512]{1,0:T(8,128)(2,1)S(1)}, u32[]{:S(2)}, u32[]{:S(2)}) collective-permute-start(bf16[64,512]{1,0:T(8,128)(2,1)S(1)} %pad_maximum_fusion.3), channel_id=1, source_target_pairs={{0,2},{1,3},{2,0},{3,1},{4,6},{5,7},{6,4},{7,5},{8,10},{9,11},{10,... | collective-permute-start | bytes 196616 | tf_op jit(solution)/shard_map/ppermute | solution.py:33
  62.4 2.6 %collective-permute-done.13 = bf16[64,512]{1,0:T(8,128)(2,1)S(1)} collective-permute-done((bf16[64,512]{1,0:T(8,128)(2,1)S(1)}, bf16[64,512]{1,0:T(8,128)(2,1)S(1)}, u32[]{:S(2)}, u32[]{:S(2)}) %collective-permute-start.13) | collective-permute-done | bytes 65568 | tf_op jit(solution)/shard_map/ppermute | solution.py:33
  65.1 1.7 %collective-permute-start.14 = (bf16[64,512]{1,0:T(8,128)(2,1)S(1)}, bf16[64,512]{1,0:T(8,128)(2,1)S(1)}, u32[]{:S(2)}, u32[]{:S(2)}) collective-permute-start(bf16[64,512]{1,0:T(8,128)(2,1)S(1)} %pad_maximum_fusion.4), channel_id=1, source_target_pairs={{0,4},{4,0},{8,12},{12,8},{16,20},{20,16},{24,28},{28,24},{1,5},{5... | collective-permute-start | bytes 196616 | tf_op jit(solution)/shard_map/ppermute | solution.py:33
  66.8 3.5 %shard_map.89 = (f32[64,2048]{1,0:T(8,128)}, bf16[64,2048]{1,0:T(8,128)(2,1)}) custom-call(s32[8]{0:T(128)} %area_size.9, bf16[128,1024]{1,0:T(8,128)(2,1)} %get-tuple-element.16.second, bf16[1024,4096]{1,0:T(8,128)(2,1)} %bitcast.16), custom_call_target="tpu_custom_call" | custom-call | tf_op jit(solution)/shard_map/pallas_call | solution.py:161
  70.3 0.0 copy-start.2
  70.3 0.0 collective-permute-start.10
  70.3 3.6 %shard_map.88 = (f32[64,2048]{1,0:T(8,128)}, bf16[64,2048]{1,0:T(8,128)(2,1)}) custom-call(s32[8]{0:T(128)} %area_size.9, bf16[128,1024]{1,0:T(8,128)(2,1)} %get-tuple-element.16.second, bf16[1024,4096]{1,0:T(8,128)(2,1)} %bitcast.17), custom_call_target="tpu_custom_call" | custom-call | tf_op jit(solution)/shard_map/pallas_call | solution.py:161
  74.0 0.4 collective-permute-start.8
  74.4 0.0 collective-permute-done.14
  74.4 1.9 %collective-permute-start.15 = (bf16[64,512]{1,0:T(8,128)(2,1)S(1)}, bf16[64,512]{1,0:T(8,128)(2,1)S(1)}, u32[]{:S(2)}, u32[]{:S(2)}) collective-permute-start(bf16[64,512]{1,0:T(8,128)(2,1)S(1)} %broadcast_select_fusion.2), channel_id=1, source_target_pairs={{0,8},{4,12},{8,0},{12,4},{16,24},{20,28},{24,16},{28,20},{1,9},{5... | collective-permute-start | bytes 196616 | tf_op jit(solution)/shard_map/ppermute | solution.py:33
  76.3 0.0 collective-permute-done.10
  76.3 0.0 copy-done.2
  76.4 1.6 %collective-permute-start.11 = (bf16[32,2048]{1,0:T(8,128)(2,1)S(1)}, bf16[32,2048]{1,0:T(8,128)(2,1)S(1)}, u32[]{:S(2)}, u32[]{:S(2)}) collective-permute-start(bf16[32,2048]{1,0:T(8,128)(2,1)S(1)} %slice.151), channel_id=1, source_target_pairs={{0,2},{1,3},{2,0},{3,1},{4,6},{5,7},{6,4},{7,5},{8,10},{9,11},{10,... | collective-permute-start | bytes 393224 | tf_op jit(solution)/shard_map/ppermute | solution.py:33
  78.0 0.8 collective-permute-done.15
  78.8 3.3 %collective-permute-start.16 = (bf16[64,512]{1,0:T(8,128)(2,1)S(1)}, bf16[64,512]{1,0:T(8,128)(2,1)S(1)}, u32[]{:S(2)}, u32[]{:S(2)}) collective-permute-start(bf16[64,512]{1,0:T(8,128)(2,1)S(1)} %broadcast_select_fusion.3), channel_id=1, source_target_pairs={{0,16},{4,20},{8,24},{12,28},{16,0},{20,4},{24,8},{28,12},{1,17},{... | collective-permute-start | bytes 196616 | tf_op jit(solution)/shard_map/ppermute | solution.py:33
  82.1 0.0 collective-permute-done.8
  82.1 1.1 %convert_add_fusion.1 = f32[64,2048]{1,0:T(8,128)S(1)} fusion(f32[64,2048]{1,0:T(8,128)} %get-tuple-element.17, bf16[64,2048]{1,0:T(8,128)(2,1)S(1)} %collective-permute-done.8), kind=kLoop, calls=%fused_computation.11 | loop fusion | flops 262144 | bytes 1310720 | tf_op jit(solution)/shard_map/add | solution.py:239
  83.3 1.6 %collective-permute-start.9 = (bf16[32,2048]{1,0:T(8,128)(2,1)S(1)}, bf16[32,2048]{1,0:T(8,128)(2,1)S(1)}, u32[]{:S(2)}, u32[]{:S(2)}) collective-permute-start(bf16[32,2048]{1,0:T(8,128)(2,1)S(1)} %slice.152), channel_id=1, source_target_pairs={{0,2},{1,3},{2,0},{3,1},{4,6},{5,7},{6,4},{7,5},{8,10},{9,11},{10,... | collective-permute-start | bytes 393224 | tf_op jit(solution)/shard_map/ppermute | solution.py:33
  84.8 0.0 collective-permute-done.16
  84.8 0.3 fusion.4
  85.1 0.0 collective-permute-done.11
  85.2 0.7 multiply_bitcast_fusion
  85.9 2.4 %collective-permute-done.9 = bf16[32,2048]{1,0:T(8,128)(2,1)S(1)} collective-permute-done((bf16[32,2048]{1,0:T(8,128)(2,1)S(1)}, bf16[32,2048]{1,0:T(8,128)(2,1)S(1)}, u32[]{:S(2)}, u32[]{:S(2)}) %collective-permute-start.9) | collective-permute-done | bytes 131104 | tf_op jit(solution)/shard_map/ppermute | solution.py:33
  88.3 0.8 maximum_bitcast_fusion
  (26 shorter events, 0.5 us)
Async XLA Ops:
  2.5 10.2 %collective-permute-start = (bf16[32,4608]{1,0:T(8,128)(2,1)}, bf16[32,4608]{1,0:T(8,128)(2,1)S(1)}, u32[]{:S(2)}, u32[]{:S(2)}) collective-permute-start(bf16[32,4608]{1,0:T(8,128)(2,1)} %shard_map.85), channel_id=1, source_target_pairs={{0,2},{1,3},{2,0},{3,1},{4,6},{5,7},{6,4},{7,5},{8,10},{9,11},{10,... | collective-permute-start | bytes 884744 | tf_op jit(solution)/shard_map/ppermute | solution.py:33
  13.7 8.4 %copy-start = (bf16[64,4608]{1,0:T(8,128)(2,1)}, bf16[64,4608]{1,0:T(8,128)(2,1)S(1)}, u32[]{:S(2)}) copy-start(bf16[64,4608]{1,0:T(8,128)(2,1)S(1)} %pad_maximum_fusion.near) | copy-start | bytes 1769476
  13.7 8.4 %collective-permute-start.1 = (bf16[64,4608]{1,0:T(8,128)(2,1)S(1)}, bf16[64,4608]{1,0:T(8,128)(2,1)S(1)}, u32[]{:S(2)}, u32[]{:S(2)}) collective-permute-start(bf16[64,4608]{1,0:T(8,128)(2,1)S(1)} %pad_maximum_fusion.near), channel_id=1, source_target_pairs={{0,1},{1,0},{2,3},{3,2},{4,5},{5,4},{6,7},{7,6},{8,9},{9,8},{10,11... | collective-permute-start | bytes 1769480 | tf_op jit(solution)/shard_map/ppermute | solution.py:33
  22.1 0.8 copy-start.1
  30.2 1.6 %collective-permute-start.2 = (f32[64,512]{1,0:T(8,128)}, f32[64,512]{1,0:T(8,128)S(1)}, u32[]{:S(2)}, u32[]{:S(2)}) collective-permute-start(f32[64,512]{1,0:T(8,128)} %get-tuple-element.15), channel_id=1, source_target_pairs={{0,1},{1,0},{2,3},{3,2},{4,5},{5,4},{6,7},{7,6},{8,9},{9,8},{10,11... | collective-permute-start | bytes 393224 | tf_op jit(solution)/shard_map/ppermute | solution.py:33
  32.7 5.1 %collective-permute-start.3 = (bf16[96,512]{1,0:T(8,128)(2,1)S(1)}, bf16[96,512]{1,0:T(8,128)(2,1)S(1)}, u32[]{:S(2)}, u32[]{:S(2)}) collective-permute-start(bf16[96,512]{1,0:T(8,128)(2,1)S(1)} %pad_maximum_fusion.1), channel_id=1, source_target_pairs={{0,2},{1,3},{2,0},{3,1},{4,6},{5,7},{6,4},{7,5},{8,10},{9,11},{10,... | collective-permute-start | bytes 294920 | tf_op jit(solution)/shard_map/ppermute | solution.py:33
  38.0 4.7 %collective-permute-start.4 = (bf16[96,512]{1,0:T(8,128)(2,1)S(1)}, bf16[96,512]{1,0:T(8,128)(2,1)S(1)}, u32[]{:S(2)}, u32[]{:S(2)}) collective-permute-start(bf16[96,512]{1,0:T(8,128)(2,1)S(1)} %pad_maximum_fusion.2), channel_id=1, source_target_pairs={{0,4},{4,0},{8,12},{12,8},{16,20},{20,16},{24,28},{28,24},{1,5},{5... | collective-permute-start | bytes 294920 | tf_op jit(solution)/shard_map/ppermute | solution.py:33
  42.7 4.7 %collective-permute-start.5 = (bf16[96,512]{1,0:T(8,128)(2,1)S(1)}, bf16[96,512]{1,0:T(8,128)(2,1)S(1)}, u32[]{:S(2)}, u32[]{:S(2)}) collective-permute-start(bf16[96,512]{1,0:T(8,128)(2,1)S(1)} %broadcast_select_fusion), channel_id=1, source_target_pairs={{0,8},{4,12},{8,0},{12,4},{16,24},{20,28},{24,16},{28,20},{1,9},{5... | collective-permute-start | bytes 294920 | tf_op jit(solution)/shard_map/ppermute | solution.py:33
  47.4 5.7 %collective-permute-start.6 = (bf16[96,512]{1,0:T(8,128)(2,1)S(1)}, bf16[96,512]{1,0:T(8,128)(2,1)S(1)}, u32[]{:S(2)}, u32[]{:S(2)}) collective-permute-start(bf16[96,512]{1,0:T(8,128)(2,1)S(1)} %broadcast_select_fusion.1), channel_id=1, source_target_pairs={{0,16},{4,20},{8,24},{12,28},{16,0},{20,4},{24,8},{28,12},{1,17},{... | collective-permute-start | bytes 294920 | tf_op jit(solution)/shard_map/ppermute | solution.py:33
  53.5 1.3 %copy-start.3 = (bf16[64,512]{1,0:T(8,128)(2,1)}, bf16[64,512]{1,0:T(8,128)(2,1)S(1)}, u32[]{:S(2)}) copy-start(bf16[64,512]{1,0:T(8,128)(2,1)S(1)} %get-tuple-element.37.near) | copy-start | bytes 196612
  53.5 1.3 %collective-permute-start.7 = (bf16[64,512]{1,0:T(8,128)(2,1)S(1)}, bf16[64,512]{1,0:T(8,128)(2,1)S(1)}, u32[]{:S(2)}, u32[]{:S(2)}) collective-permute-start(bf16[64,512]{1,0:T(8,128)(2,1)S(1)} %get-tuple-element.37.near), channel_id=1, source_target_pairs={{0,1},{1,0},{2,3},{3,2},{4,5},{5,4},{6,7},{7,6},{8,9},{9,8},{10,11... | collective-permute-start | bytes 196616 | tf_op jit(solution)/shard_map/ppermute | solution.py:33
  54.8 0.6 copy-start.4
  58.2 1.6 %collective-permute-start.12 = (f32[64,512]{1,0:T(8,128)}, f32[64,512]{1,0:T(8,128)S(1)}, u32[]{:S(2)}, u32[]{:S(2)}) collective-permute-start(f32[64,512]{1,0:T(8,128)} %get-tuple-element.22), channel_id=1, source_target_pairs={{0,1},{1,0},{2,3},{3,2},{4,5},{5,4},{6,7},{7,6},{8,9},{9,8},{10,11... | collective-permute-start | bytes 393224 | tf_op jit(solution)/shard_map/ppermute | solution.py:33
  60.7 4.3 %collective-permute-start.13 = (bf16[64,512]{1,0:T(8,128)(2,1)S(1)}, bf16[64,512]{1,0:T(8,128)(2,1)S(1)}, u32[]{:S(2)}, u32[]{:S(2)}) collective-permute-start(bf16[64,512]{1,0:T(8,128)(2,1)S(1)} %pad_maximum_fusion.3), channel_id=1, source_target_pairs={{0,2},{1,3},{2,0},{3,1},{4,6},{5,7},{6,4},{7,5},{8,10},{9,11},{10,... | collective-permute-start | bytes 196616 | tf_op jit(solution)/shard_map/ppermute | solution.py:33
  65.1 9.3 %collective-permute-start.14 = (bf16[64,512]{1,0:T(8,128)(2,1)S(1)}, bf16[64,512]{1,0:T(8,128)(2,1)S(1)}, u32[]{:S(2)}, u32[]{:S(2)}) collective-permute-start(bf16[64,512]{1,0:T(8,128)(2,1)S(1)} %pad_maximum_fusion.4), channel_id=1, source_target_pairs={{0,4},{4,0},{8,12},{12,8},{16,20},{20,16},{24,28},{28,24},{1,5},{5... | collective-permute-start | bytes 196616 | tf_op jit(solution)/shard_map/ppermute | solution.py:33
  70.3 6.0 %copy-start.2 = (f32[64,2048]{1,0:T(8,128)S(1)}, f32[64,2048]{1,0:T(8,128)}, u32[]{:S(2)}) copy-start(f32[64,2048]{1,0:T(8,128)} %get-tuple-element.19) | copy-start | bytes 1572868
  70.3 6.0 %collective-permute-start.10 = (bf16[64,2048]{1,0:T(8,128)(2,1)}, bf16[64,2048]{1,0:T(8,128)(2,1)S(1)}, u32[]{:S(2)}, u32[]{:S(2)}) collective-permute-start(bf16[64,2048]{1,0:T(8,128)(2,1)} %get-tuple-element.20), channel_id=1, source_target_pairs={{0,1},{1,0},{2,3},{3,2},{4,5},{5,4},{6,7},{7,6},{8,9},{9,8},{10,11... | collective-permute-start | bytes 786440 | tf_op jit(solution)/shard_map/ppermute | solution.py:33
  74.0 8.2 %collective-permute-start.8 = (bf16[64,2048]{1,0:T(8,128)(2,1)}, bf16[64,2048]{1,0:T(8,128)(2,1)S(1)}, u32[]{:S(2)}, u32[]{:S(2)}) collective-permute-start(bf16[64,2048]{1,0:T(8,128)(2,1)} %get-tuple-element.18), channel_id=1, source_target_pairs={{0,1},{1,0},{2,3},{3,2},{4,5},{5,4},{6,7},{7,6},{8,9},{9,8},{10,11... | collective-permute-start | bytes 786440 | tf_op jit(solution)/shard_map/ppermute | solution.py:33
  74.4 4.3 %collective-permute-start.15 = (bf16[64,512]{1,0:T(8,128)(2,1)S(1)}, bf16[64,512]{1,0:T(8,128)(2,1)S(1)}, u32[]{:S(2)}, u32[]{:S(2)}) collective-permute-start(bf16[64,512]{1,0:T(8,128)(2,1)S(1)} %broadcast_select_fusion.2), channel_id=1, source_target_pairs={{0,8},{4,12},{8,0},{12,4},{16,24},{20,28},{24,16},{28,20},{1,9},{5... | collective-permute-start | bytes 196616 | tf_op jit(solution)/shard_map/ppermute | solution.py:33
  76.4 8.7 %collective-permute-start.11 = (bf16[32,2048]{1,0:T(8,128)(2,1)S(1)}, bf16[32,2048]{1,0:T(8,128)(2,1)S(1)}, u32[]{:S(2)}, u32[]{:S(2)}) collective-permute-start(bf16[32,2048]{1,0:T(8,128)(2,1)S(1)} %slice.151), channel_id=1, source_target_pairs={{0,2},{1,3},{2,0},{3,1},{4,6},{5,7},{6,4},{7,5},{8,10},{9,11},{10,... | collective-permute-start | bytes 393224 | tf_op jit(solution)/shard_map/ppermute | solution.py:33
  78.8 6.1 %collective-permute-start.16 = (bf16[64,512]{1,0:T(8,128)(2,1)S(1)}, bf16[64,512]{1,0:T(8,128)(2,1)S(1)}, u32[]{:S(2)}, u32[]{:S(2)}) collective-permute-start(bf16[64,512]{1,0:T(8,128)(2,1)S(1)} %broadcast_select_fusion.3), channel_id=1, source_target_pairs={{0,16},{4,20},{8,24},{12,28},{16,0},{20,4},{24,8},{28,12},{1,17},{... | collective-permute-start | bytes 196616 | tf_op jit(solution)/shard_map/ppermute | solution.py:33
  83.3 5.0 %collective-permute-start.9 = (bf16[32,2048]{1,0:T(8,128)(2,1)S(1)}, bf16[32,2048]{1,0:T(8,128)(2,1)S(1)}, u32[]{:S(2)}, u32[]{:S(2)}) collective-permute-start(bf16[32,2048]{1,0:T(8,128)(2,1)S(1)} %slice.152), channel_id=1, source_target_pairs={{0,2},{1,3},{2,0},{3,1},{4,6},{5,7},{6,4},{7,5},{8,10},{9,11},{10,... | collective-permute-start | bytes 393224 | tf_op jit(solution)/shard_map/ppermute | solution.py:33

commit v3 on v2

--- a/solution.py
+++ b/solution.py
@@ -42,6 +42,10 @@
     return jax.ShapeDtypeStruct(shape, dtype)
 
 
+def on_chip(x):
+    return pltpu.with_memory_space_constraint(x, pltpu.VMEM)
+
+
 def plain_kernel(area_size, injection, dual, packed):
     width = injection.shape[1]
     live = lax.broadcasted_iota(jnp.int32, injection.shape, 1) < area_size[lax.axis_index("area")]
@@ -58,7 +62,9 @@
     )(area_size, injection, dual)
 
 
-def base_kernel(area_size, near, far, dual, factor, factor_ends, base, keep, send, side, partial):
+def base_kernel(
+    area_size, near, far, dual, factor, ends_low, ends_high, base, keep, send, side, partial
+):
     step = pl.program_id(0)
     half = near.shape[0]
     block, width = factor.shape
@@ -69,7 +75,7 @@
         side[half:] = far[...]
         partial[...] = jnp.zeros_like(partial)
 
-    here = factor_ends[...]
+    here = jnp.concatenate([ends_low[...], ends_high[...]], axis=1)
     value = dot_nt(side[:, :width], factor[...])
     start = lax.axis_index("scen") * (pl.num_programs(0) * block) + step * block
     live = start + lax.broadcasted_iota(jnp.int32, value.shape, 1) < area_size[lax.axis_index("area")]
@@ -88,16 +94,16 @@
 def base_product(area_size, near, far, dual, factor, factor_ends):
     rows, width = factor.shape
     half, packed_width = near.shape
-    ends_total = factor_ends.shape[1]
+    ends_total = dual.shape[1]
     block = 512
     fixed = pl.BlockSpec((half, ends_total), lambda i: (0, 0))
     return pl.pallas_call(
         base_kernel,
         grid=(rows // block,),
         out_shape=(
-            out((2 * half, rows), F32),
-            out((half, ends_total), F32),
-            out((half, ends_total), F32),
+            pltpu.VMEM((2 * half, rows), F32),
+            pltpu.VMEM((half, ends_total), F32),
+            pltpu.VMEM((half, ends_total), F32),
         ),
         in_specs=[
             SCALARS,
@@ -105,21 +111,24 @@
             WHOLE,
             WHOLE,
             pl.BlockSpec((block, width), lambda i: (i, 0)),
-            pl.BlockSpec((block, ends_total), lambda i: (i, 0)),
+            pl.BlockSpec((block, ends_total // 2), lambda i: (i, 0)),
+            pl.BlockSpec((block, ends_total // 2), lambda i: (i, 0)),
         ],
         out_specs=(pl.BlockSpec((2 * half, block), lambda i: (0, i)), fixed, fixed),
         scratch_shapes=[
             pltpu.VMEM((2 * half, packed_width), BF16),
             pltpu.VMEM((2 * half, ends_total), F32),
         ],
-    )(area_size, near, far, dual, factor, factor_ends)
-
-
-def second_kernel(area_size, base, near, far, factor_ends, second, keep, send, spread):
+    )(area_size, on_chip(near), on_chip(far), dual, factor, *factor_ends)
+
+
+def second_kernel(
+    area_size, base, near, far, ends_low, ends_high, second, keep, send, spread
+):
     half = near.shape[0]
     spread[:half] = near[...]
     spread[half:] = far[...]
-    here = factor_ends[...]
+    here = jnp.concatenate([ends_low[...], ends_high[...]], axis=1)
     start = lax.axis_index("scen") * here.shape[0]
     live = start + lax.broadcasted_iota(jnp.int32, base.shape, 1) < area_size[lax.axis_index("area")]
     rows = jnp.where(live, base[...] - dot_nt(spread[...], here), 0.0).astype(BF16)
@@ -131,14 +140,14 @@
 
 def second_product(area_size, base, near, far, factor_ends):
     half, ends_total = near.shape
-    shape = out((half, ends_total), F32)
+    shape = pltpu.VMEM((half, ends_total), F32)
     return pl.pallas_call(
         second_kernel,
-        out_shape=(out(base.shape, BF16), shape, shape),
-        in_specs=[SCALARS, WHOLE, WHOLE, WHOLE, WHOLE],
+        out_shape=(pltpu.VMEM(base.shape, BF16), shape, shape),
+        in_specs=[SCALARS, WHOLE, WHOLE, WHOLE, WHOLE, WHOLE],
         out_specs=(WHOLE, WHOLE, WHOLE),
         scratch_shapes=[pltpu.VMEM((2 * half, ends_total), BF16)],
-    )(area_size, base, near, far, factor_ends)
+    )(area_size, *map(on_chip, (base, near, far, *factor_ends)))
 
 
 def angles_kernel(first_bus, area_size, second, factor, keep, send):
@@ -184,8 +193,10 @@
     pair = jnp.concatenate([packed, other], axis=0)
     pair_far = swap(pair, "scen", 1)
 
-    pick = (jnp.arange(width)[:, None] == buses[None, :]).astype(BF16)
-    factor_ends = dot_nn(factor, pick).astype(BF16)
+    factor_ends = []
+    for chosen in jnp.split(buses, 2):
+        pick = (jnp.arange(width)[:, None] == chosen[None, :]).astype(BF16)
+        factor_ends.append(dot_nn(factor, pick).astype(BF16))
     slots = jnp.arange(ends_total)
     mate = ((slots // CAP * CAP + peers % CAP)[None, :] == slots[:, None]).astype(BF16)
 
@@ -211,9 +222,7 @@
     first_rows, last_rows = slice(0, columns), slice(columns, pair_rows)
     other = swap(with_low(keep, last_rows), "scen", 2).astype(F32)
     q = keep + jnp.concatenate([other[last_rows] + other[pair_rows:], other[first_rows]], axis=0)
-    moved = exchange(with_low(q, first_rows))
-    moved = jnp.concatenate([moved[first_rows] + moved[pair_rows:], moved[last_rows]], axis=0)
-    consensus = (q + moved) / DENOM
+    consensus = (q + exchange(q.astype(BF16))) / DENOM
     spread = q - 2.0 * PENALTY * consensus
     spread_pair = spread.astype(BF16)
     spread_far = swap(spread_pair, "scen", 1)

time: 89.5 us -> 80.5 us (0.90)
  waiting for transfers between devices: 27.7 us -> 19.8 us
  matrix products: 8.9 us -> 13.8 us
  other arithmetic: 6.64 us -> 3.76 us
  Pallas kernels: 19 us -> 16.6 us
  starting transfers between devices: 24.5 us -> 23.5 us
    ppermute x17, waiting for transfers between devices: 27.7 us -> 19.8 us  [swap(): return lax.ppermute(x, axis, [(i, i ^ bit) for i in range(n)])]
    dot_general x3 -> x4, matrix products: 8.9 us -> 13.8 us  [dot_nn(): return jnp.dot(a, b, preferred_element_type=F32)]
    pallas_call x2, Pallas kernels: 10.1 us -> 7.63 us  [the longest x1 6.32 us: base_product(): pl.pallas_call(base_kernel, grid=(rows // block,), out_shape=(pltpu.VMEM(...]
    ppermute x17, starting transfers between devices: 24.5 us -> 23.5 us  [swap(): return lax.ppermute(x, axis, [(i, i ^ bit) for i in range(n)])]
    concatenate x1, other arithmetic: 1 us -> 0.04 us  [shards(): pair = jnp.concatenate([packed, other], axis=0)]
    convert_element_type x3 -> x2, other arithmetic: 0.98 us -> 0.05 us  [halves(): high = x.astype(BF16)]
    add x1, other arithmetic: 0.92 us -> 0.02 us  [shards(): keep = keep + far]
  transfers between devices with their start and end apart: 17 -> 17, of which waited for: 11 -> 10; matrix products, arithmetic and copies ran while one was open for 13% -> 21% of each run, Pallas kernels for 8% -> 9%
where the time goes in v3:
time: 80.5 us; the launch traced here: 80.1 us
  starting transfers between devices  23.5 us (29%)
  waiting for transfers between devices  19.8 us (25%)
  Pallas kernels  16.6 us (21%)
  matrix products  13.8 us (17%)
  other arithmetic  3.76 us (5%)
  local copies, waits for them, and re-layouts  1.88 us (2%)
  between operations  0.88 us (1%)
    ppermute x17, starting transfers between devices, swap(): return lax.ppermute(x, axis, [(i, i ^ bit) for i in range(n)])  23.5 us
    ppermute x17, waiting for transfers between devices, swap(): return lax.ppermute(x, axis, [(i, i ^ bit) for i in range(n)])  19.8 us
    dot_general x4, matrix products, dot_nn(): return jnp.dot(a, b, preferred_element_type=F32)  13.8 us
    pallas_call x2, Pallas kernels, angles_product(): pl.pallas_call(functools.partial(angles_kernel, part * size), grid=(steps...  7.11 us
    pallas_call x1, Pallas kernels, base_product(): pl.pallas_call(base_kernel, grid=(rows // block,), out_shape=(pltpu.VMEM(...  6.32 us
    pallas_call x1, Pallas kernels, packed_side(): pl.pallas_call(plain_kernel, out_shape=out((injection.shape[0], injection...  1.83 us
  transfers between devices with their start and end apart: 17, of which 10 were waited for; matrix products, arithmetic and copies ran while one was open for 21% of the time, Pallas kernels for 9%

profile of v3, /device:TPU:0, one launch (start us, length us, event | category | flops | bytes accessed | tf_op | source)
XLA Modules:
  0.0 80.1 jit_solution(16139754795726525551)
XLA Ops:
  0.6 1.8 %shard_map.85 = bf16[32,4608]{1,0:T(8,128)(2,1)} custom-call(s32[8]{0:T(128)} %area_size.9, f32[32,4096]{1,0:T(8,128)} %bitcast.23, f32[32,512]{1,0:T(8,128)} %bitcast.24), custom_call_target="tpu_custom_call" | custom-call | tf_op jit(solution)/shard_map/pallas_call | solution.py:57
  2.5 0.0 copy-start.5
  2.5 3.0 %collective-permute-start = (bf16[32,4608]{1,0:T(8,128)(2,1)}, bf16[32,4608]{1,0:T(8,128)(2,1)S(1)}, u32[]{:S(2)}, u32[]{:S(2)}) collective-permute-start(bf16[32,4608]{1,0:T(8,128)(2,1)} %shard_map.85), channel_id=1, source_target_pairs={{0,2},{1,3},{2,0},{3,1},{4,6},{5,7},{6,4},{7,5},{8,10},{9,11},{10,... | collective-permute-start | bytes 884744 | tf_op jit(solution)/shard_map/ppermute | solution.py:33
  5.5 0.8 fusion.28
  6.2 6.6 %fusion.6.ends_low = bf16[1024,256]{1,0:T(8,128)(2,1)} fusion(s32[256]{0:T(256)S(1)} %bitcast.29, bf16[1,1024,4096]{2,1,0:T(8,128)(2,1)} %param.7), kind=kOutput, calls=%fused_computation.8 | convolution fusion | flops 2148794368 | bytes 8913920 | tf_op jit(solution)/shard_map/dot_general | solution.py:28
  12.8 0.0 collective-permute-done
  12.8 0.0 copy-done.5
  12.9 0.1 collective-permute-start.1
  12.9 6.6 %fusion.7.ends_high = bf16[1024,256]{1,0:T(8,128)(2,1)} fusion(s32[256]{0:T(256)S(1)} %bitcast.28, bf16[1,1024,4096]{2,1,0:T(8,128)(2,1)} %param.7), kind=kOutput, calls=%fused_computation.9 | convolution fusion | flops 2148794368 | bytes 8913920 | tf_op jit(solution)/shard_map/dot_general | solution.py:28
  19.5 0.0 copy-start
  19.5 0.0 copy-start.1
  19.5 0.0 collective-permute-done.1.far
  19.5 6.3 %shard_map.86 = (f32[128,1024]{1,0:T(8,128)S(1)}, f32[64,512]{1,0:T(8,128)S(1)}, f32[64,512]{1,0:T(8,128)S(1)}) custom-call(s32[8]{0:T(128)} %area_size.9, bf16[64,4608]{1,0:T(8,128)(2,1)S(1)} %pad_maximum_fusion.near, bf16[64,4608]{1,0:T(8,128)(2,1)S(1)} %collective-permute-done.1.far, f32[32,512]{1,0:T(8,128)} %bitcast.25, bf16[1024,4096]{1,0:T(8,128)(2,1)} %bitcast.20, ...), custom_call_target="tpu_custom_call" | custom-call | tf_op jit(solution)/shard_map/pallas_call | solution.py:100
  25.9 0.0 copy-start.3
  25.9 0.6 collective-permute-start.2
  26.4 1.0 %collective-permute-done.2 = f32[64,512]{1,0:T(8,128)S(1)} collective-permute-done((f32[64,512]{1,0:T(8,128)S(1)}, f32[64,512]{1,0:T(8,128)S(1)}, u32[]{:S(2)}, u32[]{:S(2)}) %collective-permute-start.2) | collective-permute-done | bytes 131104 | tf_op jit(solution)/shard_map/ppermute | solution.py:33
  27.5 1.7 %collective-permute-start.3 = (bf16[96,512]{1,0:T(8,128)(2,1)S(1)}, bf16[96,512]{1,0:T(8,128)(2,1)S(1)}, u32[]{:S(2)}, u32[]{:S(2)}) collective-permute-start(bf16[96,512]{1,0:T(8,128)(2,1)S(1)} %pad_maximum_fusion.1), channel_id=1, source_target_pairs={{0,2},{1,3},{2,0},{3,1},{4,6},{5,7},{6,4},{7,5},{8,10},{9,11},{10,... | collective-permute-start | bytes 294920 | tf_op jit(solution)/shard_map/ppermute | solution.py:33
  29.1 0.7 fusion.21
  29.9 2.7 %collective-permute-done.3 = bf16[96,512]{1,0:T(8,128)(2,1)S(1)} collective-permute-done((bf16[96,512]{1,0:T(8,128)(2,1)S(1)}, bf16[96,512]{1,0:T(8,128)(2,1)S(1)}, u32[]{:S(2)}, u32[]{:S(2)}) %collective-permute-start.3) | collective-permute-done | bytes 98336 | tf_op jit(solution)/shard_map/ppermute | solution.py:33
  32.7 1.6 %collective-permute-start.4 = (bf16[64,512]{1,0:T(8,128)(2,1)S(1)}, bf16[64,512]{1,0:T(8,128)(2,1)S(1)}, u32[]{:S(2)}, u32[]{:S(2)}) collective-permute-start(bf16[64,512]{1,0:T(8,128)(2,1)S(1)} %get-tuple-element.30), channel_id=1, source_target_pairs={{0,4},{4,0},{8,12},{12,8},{16,20},{20,16},{24,28},{28,24},{1,5},{5... | collective-permute-start | bytes 196616 | tf_op jit(solution)/shard_map/ppermute | solution.py:33
  34.4 2.7 %collective-permute-done.4 = bf16[64,512]{1,0:T(8,128)(2,1)S(1)} collective-permute-done((bf16[64,512]{1,0:T(8,128)(2,1)S(1)}, bf16[64,512]{1,0:T(8,128)(2,1)S(1)}, u32[]{:S(2)}, u32[]{:S(2)}) %collective-permute-start.4) | collective-permute-done | bytes 65568 | tf_op jit(solution)/shard_map/ppermute | solution.py:33
  37.0 1.7 %collective-permute-start.5 = (bf16[64,512]{1,0:T(8,128)(2,1)S(1)}, bf16[64,512]{1,0:T(8,128)(2,1)S(1)}, u32[]{:S(2)}, u32[]{:S(2)}) collective-permute-start(bf16[64,512]{1,0:T(8,128)(2,1)S(1)} %broadcast_select_fusion.1), channel_id=1, source_target_pairs={{0,8},{4,12},{8,0},{12,4},{16,24},{20,28},{24,16},{28,20},{1,9},{5... | collective-permute-start | bytes 196616 | tf_op jit(solution)/shard_map/ppermute | solution.py:33
  38.8 2.6 %collective-permute-done.5 = bf16[64,512]{1,0:T(8,128)(2,1)S(1)} collective-permute-done((bf16[64,512]{1,0:T(8,128)(2,1)S(1)}, bf16[64,512]{1,0:T(8,128)(2,1)S(1)}, u32[]{:S(2)}, u32[]{:S(2)}) %collective-permute-start.5) | collective-permute-done | bytes 65568 | tf_op jit(solution)/shard_map/ppermute | solution.py:33
  41.4 3.0 %collective-permute-start.6 = (bf16[64,512]{1,0:T(8,128)(2,1)S(1)}, bf16[64,512]{1,0:T(8,128)(2,1)S(1)}, u32[]{:S(2)}, u32[]{:S(2)}) collective-permute-start(bf16[64,512]{1,0:T(8,128)(2,1)S(1)} %broadcast_select_fusion.3), channel_id=1, source_target_pairs={{0,16},{4,20},{8,24},{12,28},{16,0},{20,4},{24,8},{28,12},{1,17},{... | collective-permute-start | bytes 196616 | tf_op jit(solution)/shard_map/ppermute | solution.py:33
  44.3 2.3 %collective-permute-done.6 = bf16[64,512]{1,0:T(8,128)(2,1)S(1)} collective-permute-done((bf16[64,512]{1,0:T(8,128)(2,1)S(1)}, bf16[64,512]{1,0:T(8,128)(2,1)S(1)}, u32[]{:S(2)}, u32[]{:S(2)}) %collective-permute-start.6) | collective-permute-done | bytes 65568 | tf_op jit(solution)/shard_map/ppermute | solution.py:33
  46.6 0.3 subtract_convert_fusion
  46.9 0.1 collective-permute-start.7
  47.0 1.2 %collective-permute-done.7.far = bf16[64,512]{1,0:T(8,128)(2,1)S(1)} collective-permute-done((bf16[64,512]{1,0:T(8,128)(2,1)S(1)}, bf16[64,512]{1,0:T(8,128)(2,1)S(1)}, u32[]{:S(2)}, u32[]{:S(2)}) %collective-permute-start.7) | collective-permute-done | bytes 65568 | tf_op jit(solution)/shard_map/ppermute | solution.py:33
  48.2 0.0 copy-done.3
  48.2 0.0 copy-done
  48.3 0.0 copy-done.1
  48.3 0.0 copy-start.4
  48.3 1.0 %copy-done.4 = f32[128,1024]{1,0:T(8,128)S(1)} copy-done((f32[128,1024]{1,0:T(8,128)S(1)}, f32[128,1024]{1,0:T(8,128)}, u32[]{:S(2)}) %copy-start.4) | copy-done | bytes 524312
  49.3 1.3 %shard_map.87 = (bf16[128,1024]{1,0:T(8,128)(2,1)S(1)}, f32[64,512]{1,0:T(8,128)S(1)}, f32[64,512]{1,0:T(8,128)S(1)}) custom-call(s32[8]{0:T(128)} %area_size.9, f32[128,1024]{1,0:T(8,128)S(1)} %copy-done.4, bf16[64,512]{1,0:T(8,128)(2,1)S(1)} %get-tuple-element.40.near, bf16[64,512]{1,0:T(8,128)(2,1)S(1)} %collective-permute-done.7.far, ...), custom_call_target="tpu_custom_call" | custom-call | tf_op jit(solution)/shard_map/pallas_call | solution.py:144
  50.6 0.0 copy-start.2
  50.6 0.2 collective-permute-start.12
  50.8 1.2 %collective-permute-done.12 = f32[64,512]{1,0:T(8,128)S(1)} collective-permute-done((f32[64,512]{1,0:T(8,128)S(1)}, f32[64,512]{1,0:T(8,128)S(1)}, u32[]{:S(2)}, u32[]{:S(2)}) %collective-permute-start.12) | collective-permute-done | bytes 131104 | tf_op jit(solution)/shard_map/ppermute | solution.py:33
  52.1 1.7 %collective-permute-start.13 = (bf16[64,512]{1,0:T(8,128)(2,1)S(1)}, bf16[64,512]{1,0:T(8,128)(2,1)S(1)}, u32[]{:S(2)}, u32[]{:S(2)}) collective-permute-start(bf16[64,512]{1,0:T(8,128)(2,1)S(1)} %pad_maximum_fusion.2), channel_id=1, source_target_pairs={{0,2},{1,3},{2,0},{3,1},{4,6},{5,7},{6,4},{7,5},{8,10},{9,11},{10,... | collective-permute-start | bytes 196616 | tf_op jit(solution)/shard_map/ppermute | solution.py:33
  53.8 2.7 %collective-permute-done.13 = bf16[64,512]{1,0:T(8,128)(2,1)S(1)} collective-permute-done((bf16[64,512]{1,0:T(8,128)(2,1)S(1)}, bf16[64,512]{1,0:T(8,128)(2,1)S(1)}, u32[]{:S(2)}, u32[]{:S(2)}) %collective-permute-start.13) | collective-permute-done | bytes 65568 | tf_op jit(solution)/shard_map/ppermute | solution.py:33
  56.5 1.6 %collective-permute-start.14 = (bf16[64,512]{1,0:T(8,128)(2,1)S(1)}, bf16[64,512]{1,0:T(8,128)(2,1)S(1)}, u32[]{:S(2)}, u32[]{:S(2)}) collective-permute-start(bf16[64,512]{1,0:T(8,128)(2,1)S(1)} %pad_maximum_fusion.3), channel_id=1, source_target_pairs={{0,4},{4,0},{8,12},{12,8},{16,20},{20,16},{24,28},{28,24},{1,5},{5... | collective-permute-start | bytes 196616 | tf_op jit(solution)/shard_map/ppermute | solution.py:33
  58.1 0.0 copy-done.2
  58.1 3.5 %shard_map.88 = (f32[64,2048]{1,0:T(8,128)}, bf16[64,2048]{1,0:T(8,128)(2,1)}) custom-call(s32[8]{0:T(128)} %area_size.9, bf16[128,1024]{1,0:T(8,128)(2,1)} %copy-done.2, bf16[1024,4096]{1,0:T(8,128)(2,1)} %bitcast.21), custom_call_target="tpu_custom_call" | custom-call | tf_op jit(solution)/shard_map/pallas_call | solution.py:170
  61.7 0.0 copy-start.6
  61.7 0.0 collective-permute-start.8
  61.7 3.6 %shard_map.89 = (f32[64,2048]{1,0:T(8,128)}, bf16[64,2048]{1,0:T(8,128)(2,1)}) custom-call(s32[8]{0:T(128)} %area_size.9, bf16[128,1024]{1,0:T(8,128)(2,1)} %copy-done.2, bf16[1024,4096]{1,0:T(8,128)(2,1)} %bitcast.22), custom_call_target="tpu_custom_call" | custom-call | tf_op jit(solution)/shard_map/pallas_call | solution.py:170
  65.3 0.4 collective-permute-start.10
  65.7 0.0 collective-permute-done.14
  65.7 1.6 %collective-permute-start.15 = (bf16[64,512]{1,0:T(8,128)(2,1)S(1)}, bf16[64,512]{1,0:T(8,128)(2,1)S(1)}, u32[]{:S(2)}, u32[]{:S(2)}) collective-permute-start(bf16[64,512]{1,0:T(8,128)(2,1)S(1)} %broadcast_select_fusion), channel_id=1, source_target_pairs={{0,8},{4,12},{8,0},{12,4},{16,24},{20,28},{24,16},{28,20},{1,9},{5... | collective-permute-start | bytes 196616 | tf_op jit(solution)/shard_map/ppermute | solution.py:33
  67.4 0.0 collective-permute-done.8
  67.4 0.0 copy-done.6
  67.4 1.6 %collective-permute-start.9 = (bf16[32,2048]{1,0:T(8,128)(2,1)S(1)}, bf16[32,2048]{1,0:T(8,128)(2,1)S(1)}, u32[]{:S(2)}, u32[]{:S(2)}) collective-permute-start(bf16[32,2048]{1,0:T(8,128)(2,1)S(1)} %slice.131), channel_id=1, source_target_pairs={{0,2},{1,3},{2,0},{3,1},{4,6},{5,7},{6,4},{7,5},{8,10},{9,11},{10,... | collective-permute-start | bytes 393224 | tf_op jit(solution)/shard_map/ppermute | solution.py:33
  69.0 1.0 %collective-permute-done.15 = bf16[64,512]{1,0:T(8,128)(2,1)S(1)} collective-permute-done((bf16[64,512]{1,0:T(8,128)(2,1)S(1)}, bf16[64,512]{1,0:T(8,128)(2,1)S(1)}, u32[]{:S(2)}, u32[]{:S(2)}) %collective-permute-start.15) | collective-permute-done | bytes 65568 | tf_op jit(solution)/shard_map/ppermute | solution.py:33
  70.1 3.0 %collective-permute-start.16 = (bf16[64,512]{1,0:T(8,128)(2,1)S(1)}, bf16[64,512]{1,0:T(8,128)(2,1)S(1)}, u32[]{:S(2)}, u32[]{:S(2)}) collective-permute-start(bf16[64,512]{1,0:T(8,128)(2,1)S(1)} %broadcast_select_fusion.2), channel_id=1, source_target_pairs={{0,16},{4,20},{8,24},{12,28},{16,0},{20,4},{24,8},{28,12},{1,17},{... | collective-permute-start | bytes 196616 | tf_op jit(solution)/shard_map/ppermute | solution.py:33
  73.1 0.0 collective-permute-done.10
  73.1 1.1 %convert_add_fusion = f32[64,2048]{1,0:T(8,128)S(1)} fusion(f32[64,2048]{1,0:T(8,128)} %get-tuple-element.19, bf16[64,2048]{1,0:T(8,128)(2,1)S(1)} %collective-permute-done.10), kind=kLoop, calls=%fused_computation.15 | loop fusion | flops 262144 | bytes 1310720 | tf_op jit(solution)/shard_map/add | solution.py:248
  74.2 1.6 %collective-permute-start.11 = (bf16[32,2048]{1,0:T(8,128)(2,1)S(1)}, bf16[32,2048]{1,0:T(8,128)(2,1)S(1)}, u32[]{:S(2)}, u32[]{:S(2)}) collective-permute-start(bf16[32,2048]{1,0:T(8,128)(2,1)S(1)} %slice.130), channel_id=1, source_target_pairs={{0,2},{1,3},{2,0},{3,1},{4,6},{5,7},{6,4},{7,5},{8,10},{9,11},{10,... | collective-permute-start | bytes 393224 | tf_op jit(solution)/shard_map/ppermute | solution.py:33
  75.8 0.0 collective-permute-done.16
  75.8 0.3 fusion.8
  76.1 0.0 collective-permute-done.9
  76.1 0.7 multiply_bitcast_fusion
  76.8 2.4 %collective-permute-done.11 = bf16[32,2048]{1,0:T(8,128)(2,1)S(1)} collective-permute-done((bf16[32,2048]{1,0:T(8,128)(2,1)S(1)}, bf16[32,2048]{1,0:T(8,128)(2,1)S(1)}, u32[]{:S(2)}, u32[]{:S(2)}) %collective-permute-start.11) | collective-permute-done | bytes 131104 | tf_op jit(solution)/shard_map/ppermute | solution.py:33
  79.3 0.8 %maximum_bitcast_fusion = f32[1,32,4096]{2,1,0:T(8,128)} fusion(f32[32,2048]{1,0:T(8,128)S(1)} %slice_add_fusion, f32[32,2048]{1,0:T(8,128)S(1)} %slice_add_fusion.1), kind=kLoop, calls=%fused_computation.14 | loop fusion | flops 131072 | bytes 1048576 | tf_op jit(solution)/shard_map/broadcast_in_dim | solution.py:251
  (25 shorter events, 0.4 us)
Async XLA Ops:
  2.5 10.4 %copy-start.5 = (bf16[32,4608]{1,0:T(8,128)(2,1)S(1)}, bf16[32,4608]{1,0:T(8,128)(2,1)}, u32[]{:S(2)}) copy-start(bf16[32,4608]{1,0:T(8,128)(2,1)} %shard_map.85) | copy-start | bytes 884740
  2.5 10.4 %collective-permute-start = (bf16[32,4608]{1,0:T(8,128)(2,1)}, bf16[32,4608]{1,0:T(8,128)(2,1)S(1)}, u32[]{:S(2)}, u32[]{:S(2)}) collective-permute-start(bf16[32,4608]{1,0:T(8,128)(2,1)} %shard_map.85), channel_id=1, source_target_pairs={{0,2},{1,3},{2,0},{3,1},{4,6},{5,7},{6,4},{7,5},{8,10},{9,11},{10,... | collective-permute-start | bytes 884744 | tf_op jit(solution)/shard_map/ppermute | solution.py:33
  12.9 6.7 %collective-permute-start.1 = (bf16[64,4608]{1,0:T(8,128)(2,1)S(1)}, bf16[64,4608]{1,0:T(8,128)(2,1)S(1)}, u32[]{:S(2)}, u32[]{:S(2)}) collective-permute-start(bf16[64,4608]{1,0:T(8,128)(2,1)S(1)} %pad_maximum_fusion.near), channel_id=1, source_target_pairs={{0,1},{1,0},{2,3},{3,2},{4,5},{5,4},{6,7},{7,6},{8,9},{9,8},{10,11... | collective-permute-start | bytes 1769480 | tf_op jit(solution)/shard_map/ppermute | solution.py:33
  19.5 28.7 %copy-start = (bf16[1024,256]{1,0:T(8,128)(2,1)S(1)}, bf16[1024,256]{1,0:T(8,128)(2,1)}, u32[]{:S(2)}) copy-start(bf16[1024,256]{1,0:T(8,128)(2,1)} %fusion.6.ends_low) | copy-start | bytes 1572868
  19.5 28.7 %copy-start.1 = (bf16[1024,256]{1,0:T(8,128)(2,1)S(1)}, bf16[1024,256]{1,0:T(8,128)(2,1)}, u32[]{:S(2)}) copy-start(bf16[1024,256]{1,0:T(8,128)(2,1)} %fusion.7.ends_high) | copy-start | bytes 1572868
  25.9 22.4 %copy-start.3 = (f32[128,1024]{1,0:T(8,128)}, f32[128,1024]{1,0:T(8,128)S(1)}, u32[]{:S(2)}) copy-start(f32[128,1024]{1,0:T(8,128)S(1)} %get-tuple-element.13.base) | copy-start | bytes 1572868
  25.9 1.5 %collective-permute-start.2 = (f32[64,512]{1,0:T(8,128)S(1)}, f32[64,512]{1,0:T(8,128)S(1)}, u32[]{:S(2)}, u32[]{:S(2)}) collective-permute-start(f32[64,512]{1,0:T(8,128)S(1)} %get-tuple-element.15), channel_id=1, source_target_pairs={{0,1},{1,0},{2,3},{3,2},{4,5},{5,4},{6,7},{7,6},{8,9},{9,8},{10,11... | collective-permute-start | bytes 393224 | tf_op jit(solution)/shard_map/ppermute | solution.py:33
  27.5 5.1 %collective-permute-start.3 = (bf16[96,512]{1,0:T(8,128)(2,1)S(1)}, bf16[96,512]{1,0:T(8,128)(2,1)S(1)}, u32[]{:S(2)}, u32[]{:S(2)}) collective-permute-start(bf16[96,512]{1,0:T(8,128)(2,1)S(1)} %pad_maximum_fusion.1), channel_id=1, source_target_pairs={{0,2},{1,3},{2,0},{3,1},{4,6},{5,7},{6,4},{7,5},{8,10},{9,11},{10,... | collective-permute-start | bytes 294920 | tf_op jit(solution)/shard_map/ppermute | solution.py:33
  32.7 4.3 %collective-permute-start.4 = (bf16[64,512]{1,0:T(8,128)(2,1)S(1)}, bf16[64,512]{1,0:T(8,128)(2,1)S(1)}, u32[]{:S(2)}, u32[]{:S(2)}) collective-permute-start(bf16[64,512]{1,0:T(8,128)(2,1)S(1)} %get-tuple-element.30), channel_id=1, source_target_pairs={{0,4},{4,0},{8,12},{12,8},{16,20},{20,16},{24,28},{28,24},{1,5},{5... | collective-permute-start | bytes 196616 | tf_op jit(solution)/shard_map/ppermute | solution.py:33
  37.0 4.3 %collective-permute-start.5 = (bf16[64,512]{1,0:T(8,128)(2,1)S(1)}, bf16[64,512]{1,0:T(8,128)(2,1)S(1)}, u32[]{:S(2)}, u32[]{:S(2)}) collective-permute-start(bf16[64,512]{1,0:T(8,128)(2,1)S(1)} %broadcast_select_fusion.1), channel_id=1, source_target_pairs={{0,8},{4,12},{8,0},{12,4},{16,24},{20,28},{24,16},{28,20},{1,9},{5... | collective-permute-start | bytes 196616 | tf_op jit(solution)/shard_map/ppermute | solution.py:33
  41.4 5.2 %collective-permute-start.6 = (bf16[64,512]{1,0:T(8,128)(2,1)S(1)}, bf16[64,512]{1,0:T(8,128)(2,1)S(1)}, u32[]{:S(2)}, u32[]{:S(2)}) collective-permute-start(bf16[64,512]{1,0:T(8,128)(2,1)S(1)} %broadcast_select_fusion.3), channel_id=1, source_target_pairs={{0,16},{4,20},{8,24},{12,28},{16,0},{20,4},{24,8},{28,12},{1,17},{... | collective-permute-start | bytes 196616 | tf_op jit(solution)/shard_map/ppermute | solution.py:33
  46.9 1.3 %collective-permute-start.7 = (bf16[64,512]{1,0:T(8,128)(2,1)S(1)}, bf16[64,512]{1,0:T(8,128)(2,1)S(1)}, u32[]{:S(2)}, u32[]{:S(2)}) collective-permute-start(bf16[64,512]{1,0:T(8,128)(2,1)S(1)} %get-tuple-element.40.near), channel_id=1, source_target_pairs={{0,1},{1,0},{2,3},{3,2},{4,5},{5,4},{6,7},{7,6},{8,9},{9,8},{10,11... | collective-permute-start | bytes 196616 | tf_op jit(solution)/shard_map/ppermute | solution.py:33
  48.3 1.0 %copy-start.4 = (f32[128,1024]{1,0:T(8,128)S(1)}, f32[128,1024]{1,0:T(8,128)}, u32[]{:S(2)}) copy-start(f32[128,1024]{1,0:T(8,128)} %copy-done.3) | copy-start | bytes 1572868
  50.6 7.5 %copy-start.2 = (bf16[128,1024]{1,0:T(8,128)(2,1)}, bf16[128,1024]{1,0:T(8,128)(2,1)S(1)}, u32[]{:S(2)}) copy-start(bf16[128,1024]{1,0:T(8,128)(2,1)S(1)} %get-tuple-element.16.second) | copy-start | bytes 786436
  50.6 1.4 %collective-permute-start.12 = (f32[64,512]{1,0:T(8,128)S(1)}, f32[64,512]{1,0:T(8,128)S(1)}, u32[]{:S(2)}, u32[]{:S(2)}) collective-permute-start(f32[64,512]{1,0:T(8,128)S(1)} %get-tuple-element.22), channel_id=1, source_target_pairs={{0,1},{1,0},{2,3},{3,2},{4,5},{5,4},{6,7},{7,6},{8,9},{9,8},{10,11... | collective-permute-start | bytes 393224 | tf_op jit(solution)/shard_map/ppermute | solution.py:33
  52.1 4.3 %collective-permute-start.13 = (bf16[64,512]{1,0:T(8,128)(2,1)S(1)}, bf16[64,512]{1,0:T(8,128)(2,1)S(1)}, u32[]{:S(2)}, u32[]{:S(2)}) collective-permute-start(bf16[64,512]{1,0:T(8,128)(2,1)S(1)} %pad_maximum_fusion.2), channel_id=1, source_target_pairs={{0,2},{1,3},{2,0},{3,1},{4,6},{5,7},{6,4},{7,5},{8,10},{9,11},{10,... | collective-permute-start | bytes 196616 | tf_op jit(solution)/shard_map/ppermute | solution.py:33
  56.5 9.2 %collective-permute-start.14 = (bf16[64,512]{1,0:T(8,128)(2,1)S(1)}, bf16[64,512]{1,0:T(8,128)(2,1)S(1)}, u32[]{:S(2)}, u32[]{:S(2)}) collective-permute-start(bf16[64,512]{1,0:T(8,128)(2,1)S(1)} %pad_maximum_fusion.3), channel_id=1, source_target_pairs={{0,4},{4,0},{8,12},{12,8},{16,20},{20,16},{24,28},{28,24},{1,5},{5... | collective-permute-start | bytes 196616 | tf_op jit(solution)/shard_map/ppermute | solution.py:33
  61.7 5.7 %copy-start.6 = (f32[64,2048]{1,0:T(8,128)S(1)}, f32[64,2048]{1,0:T(8,128)}, u32[]{:S(2)}) copy-start(f32[64,2048]{1,0:T(8,128)} %get-tuple-element.17) | copy-start | bytes 1572868
  61.7 5.7 %collective-permute-start.8 = (bf16[64,2048]{1,0:T(8,128)(2,1)}, bf16[64,2048]{1,0:T(8,128)(2,1)S(1)}, u32[]{:S(2)}, u32[]{:S(2)}) collective-permute-start(bf16[64,2048]{1,0:T(8,128)(2,1)} %get-tuple-element.18), channel_id=1, source_target_pairs={{0,1},{1,0},{2,3},{3,2},{4,5},{5,4},{6,7},{7,6},{8,9},{9,8},{10,11... | collective-permute-start | bytes 786440 | tf_op jit(solution)/shard_map/ppermute | solution.py:33
  65.3 7.8 %collective-permute-start.10 = (bf16[64,2048]{1,0:T(8,128)(2,1)}, bf16[64,2048]{1,0:T(8,128)(2,1)S(1)}, u32[]{:S(2)}, u32[]{:S(2)}) collective-permute-start(bf16[64,2048]{1,0:T(8,128)(2,1)} %get-tuple-element.20), channel_id=1, source_target_pairs={{0,1},{1,0},{2,3},{3,2},{4,5},{5,4},{6,7},{7,6},{8,9},{9,8},{10,11... | collective-permute-start | bytes 786440 | tf_op jit(solution)/shard_map/ppermute | solution.py:33
  65.7 4.3 %collective-permute-start.15 = (bf16[64,512]{1,0:T(8,128)(2,1)S(1)}, bf16[64,512]{1,0:T(8,128)(2,1)S(1)}, u32[]{:S(2)}, u32[]{:S(2)}) collective-permute-start(bf16[64,512]{1,0:T(8,128)(2,1)S(1)} %broadcast_select_fusion), channel_id=1, source_target_pairs={{0,8},{4,12},{8,0},{12,4},{16,24},{20,28},{24,16},{28,20},{1,9},{5... | collective-permute-start | bytes 196616 | tf_op jit(solution)/shard_map/ppermute | solution.py:33
  67.4 8.7 %collective-permute-start.9 = (bf16[32,2048]{1,0:T(8,128)(2,1)S(1)}, bf16[32,2048]{1,0:T(8,128)(2,1)S(1)}, u32[]{:S(2)}, u32[]{:S(2)}) collective-permute-start(bf16[32,2048]{1,0:T(8,128)(2,1)S(1)} %slice.131), channel_id=1, source_target_pairs={{0,2},{1,3},{2,0},{3,1},{4,6},{5,7},{6,4},{7,5},{8,10},{9,11},{10,... | collective-permute-start | bytes 393224 | tf_op jit(solution)/shard_map/ppermute | solution.py:33
  70.1 5.7 %collective-permute-start.16 = (bf16[64,512]{1,0:T(8,128)(2,1)S(1)}, bf16[64,512]{1,0:T(8,128)(2,1)S(1)}, u32[]{:S(2)}, u32[]{:S(2)}) collective-permute-start(bf16[64,512]{1,0:T(8,128)(2,1)S(1)} %broadcast_select_fusion.2), channel_id=1, source_target_pairs={{0,16},{4,20},{8,24},{12,28},{16,0},{20,4},{24,8},{28,12},{1,17},{... | collective-permute-start | bytes 196616 | tf_op jit(solution)/shard_map/ppermute | solution.py:33
  74.2 5.0 %collective-permute-start.11 = (bf16[32,2048]{1,0:T(8,128)(2,1)S(1)}, bf16[32,2048]{1,0:T(8,128)(2,1)S(1)}, u32[]{:S(2)}, u32[]{:S(2)}) collective-permute-start(bf16[32,2048]{1,0:T(8,128)(2,1)S(1)} %slice.130), channel_id=1, source_target_pairs={{0,2},{1,3},{2,0},{3,1},{4,6},{5,7},{6,4},{7,5},{8,10},{9,11},{10,... | collective-permute-start | bytes 393224 | tf_op jit(solution)/shard_map/ppermute | solution.py:33

commit v4 on v2

--- a/solution.py
+++ b/solution.py
@@ -38,8 +38,12 @@
     return high, (x - high.astype(F32)).astype(BF16)
 
 
-def out(shape, dtype):
-    return jax.ShapeDtypeStruct(shape, dtype)
+def room(mebibytes):
+    return pltpu.CompilerParams(vmem_limit_bytes=mebibytes * 2**20)
+
+
+def on_chip(x):
+    return pltpu.with_memory_space_constraint(x, pltpu.VMEM)
 
 
 def plain_kernel(area_size, injection, dual, packed):
@@ -52,9 +56,10 @@
 def packed_side(area_size, injection, dual):
     return pl.pallas_call(
         plain_kernel,
-        out_shape=out((injection.shape[0], injection.shape[1] + dual.shape[1]), BF16),
+        out_shape=pltpu.VMEM((injection.shape[0], injection.shape[1] + dual.shape[1]), BF16),
         in_specs=[SCALARS, WHOLE, WHOLE],
         out_specs=WHOLE,
+        compiler_params=room(4),
     )(area_size, injection, dual)
 
 
@@ -69,7 +74,7 @@
         side[half:] = far[...]
         partial[...] = jnp.zeros_like(partial)
 
-    here = factor_ends[...]
+    here = factor_ends[pl.ds(pl.multiple_of(step * block, block), block), :]
     value = dot_nt(side[:, :width], factor[...])
     start = lax.axis_index("scen") * (pl.num_programs(0) * block) + step * block
     live = start + lax.broadcasted_iota(jnp.int32, value.shape, 1) < area_size[lax.axis_index("area")]
@@ -88,16 +93,16 @@
 def base_product(area_size, near, far, dual, factor, factor_ends):
     rows, width = factor.shape
     half, packed_width = near.shape
-    ends_total = factor_ends.shape[1]
+    ends_total = dual.shape[1]
     block = 512
     fixed = pl.BlockSpec((half, ends_total), lambda i: (0, 0))
     return pl.pallas_call(
         base_kernel,
         grid=(rows // block,),
         out_shape=(
-            out((2 * half, rows), F32),
-            out((half, ends_total), F32),
-            out((half, ends_total), F32),
+            pltpu.VMEM((2 * half, rows), F32),
+            pltpu.VMEM((half, ends_total), F32),
+            pltpu.VMEM((half, ends_total), F32),
         ),
         in_specs=[
             SCALARS,
@@ -105,14 +110,15 @@
             WHOLE,
             WHOLE,
             pl.BlockSpec((block, width), lambda i: (i, 0)),
-            pl.BlockSpec((block, ends_total), lambda i: (i, 0)),
+            WHOLE,
         ],
         out_specs=(pl.BlockSpec((2 * half, block), lambda i: (0, i)), fixed, fixed),
         scratch_shapes=[
             pltpu.VMEM((2 * half, packed_width), BF16),
             pltpu.VMEM((2 * half, ends_total), F32),
         ],
-    )(area_size, near, far, dual, factor, factor_ends)
+        compiler_params=room(24),
+    )(area_size, on_chip(near), on_chip(far), dual, factor, on_chip(factor_ends))
 
 
 def second_kernel(area_size, base, near, far, factor_ends, second, keep, send, spread):
@@ -131,14 +137,15 @@
 
 def second_product(area_size, base, near, far, factor_ends):
     half, ends_total = near.shape
-    shape = out((half, ends_total), F32)
+    shape = pltpu.VMEM((half, ends_total), F32)
     return pl.pallas_call(
         second_kernel,
-        out_shape=(out(base.shape, BF16), shape, shape),
+        out_shape=(pltpu.VMEM(base.shape, BF16), shape, shape),
         in_specs=[SCALARS, WHOLE, WHOLE, WHOLE, WHOLE],
         out_specs=(WHOLE, WHOLE, WHOLE),
         scratch_shapes=[pltpu.VMEM((2 * half, ends_total), BF16)],
-    )(area_size, base, near, far, factor_ends)
+        compiler_params=room(8),
+    )(area_size, *map(on_chip, (base, near, far, factor_ends)))
 
 
 def angles_kernel(first_bus, area_size, second, factor, keep, send):
@@ -161,10 +168,11 @@
     return pl.pallas_call(
         functools.partial(angles_kernel, part * size),
         grid=(steps,),
-        out_shape=(out((half, size), F32), out((half, size), BF16)),
+        out_shape=(pltpu.VMEM((half, size), F32), pltpu.VMEM((half, size), BF16)),
         in_specs=[SCALARS, WHOLE, pl.BlockSpec((rows, depth), lambda i: (0, part * steps + i))],
         out_specs=(spec, spec),
-    )(area_size, second, factor)
+        compiler_params=room(14),
+    )(area_size, on_chip(second), factor)
 
 
 def shards(injection, kkt_factor, dual_price, area_size, bnd_bus, peer_end):
@@ -211,9 +219,7 @@
     first_rows, last_rows = slice(0, columns), slice(columns, pair_rows)
     other = swap(with_low(keep, last_rows), "scen", 2).astype(F32)
     q = keep + jnp.concatenate([other[last_rows] + other[pair_rows:], other[first_rows]], axis=0)
-    moved = exchange(with_low(q, first_rows))
-    moved = jnp.concatenate([moved[first_rows] + moved[pair_rows:], moved[last_rows]], axis=0)
-    consensus = (q + moved) / DENOM
+    consensus = (q + exchange(q.astype(BF16))) / DENOM
     spread = q - 2.0 * PENALTY * consensus
     spread_pair = spread.astype(BF16)
     spread_far = swap(spread_pair, "scen", 1)

time: 89.5 us -> 74.8 us (0.84)
  Pallas kernels: 19 us -> 9.62 us
  other arithmetic: 6.64 us -> 2.75 us
  waiting for transfers between devices: 27.7 us -> 26.3 us
  local copies, waits for them, and re-layouts: 1.49 us -> 2.59 us
  matrix products: 8.9 us -> 7.91 us
    pallas_call x3, Pallas kernels: 11.9 us -> 6.25 us  [the longest x1 4.47 us: base_product(): pl.pallas_call(base_kernel, grid=(rows // block,), out_shape=(pltpu.VMEM(...]
    pallas_call x2, Pallas kernels: 7.15 us -> 3.36 us  [angles_product(): pl.pallas_call(functools.partial(angles_kernel, part * size), grid=(steps...]
    ppermute x17, waiting for transfers between devices: 27.7 us -> 26.3 us  [swap(): return lax.ppermute(x, axis, [(i, i ^ bit) for i in range(n)])]
    unnamed x10 -> x14, local copies, waits for them, and re-layouts: 1.45 us -> 2.55 us
    add x2, other arithmetic: 1.15 us -> 0.11 us  [shards(): keep = keep + swap(send, 'scen', 1).astype(F32)]
    dot_general x3, matrix products: 8.9 us -> 7.91 us  [dot_nn(): return jnp.dot(a, b, preferred_element_type=F32)]
    concatenate x1, other arithmetic: 1 us -> 0.04 us  [shards(): pair = jnp.concatenate([packed, other], axis=0)]
    convert_element_type x3 -> x2, other arithmetic: 0.98 us -> 0.05 us  [halves(): high = x.astype(BF16)]
  transfers between devices with their start and end apart: 17 -> 17, of which waited for: 11 -> 12; matrix products, arithmetic and copies ran while one was open for 13% -> 12% of each run, Pallas kernels for 8% -> 5%
where the time goes in v4:
time: 74.8 us; the launch traced here: 74.4 us
  waiting for transfers between devices  26.3 us (35%)
  starting transfers between devices  24.3 us (32%)
  Pallas kernels  9.62 us (13%)
  matrix products  7.91 us (11%)
  other arithmetic  2.75 us (4%)
  local copies, waits for them, and re-layouts  2.59 us (3%)
  between operations  0.95 us (1%)
    ppermute x17, waiting for transfers between devices, swap(): return lax.ppermute(x, axis, [(i, i ^ bit) for i in range(n)])  26.3 us
    ppermute x17, starting transfers between devices, swap(): return lax.ppermute(x, axis, [(i, i ^ bit) for i in range(n)])  24.3 us
    dot_general x3, matrix products, dot_nn(): return jnp.dot(a, b, preferred_element_type=F32)  7.91 us
    pallas_call x1, Pallas kernels, base_product(): pl.pallas_call(base_kernel, grid=(rows // block,), out_shape=(pltpu.VMEM(...  4.47 us
    pallas_call x2, Pallas kernels, angles_product(): pl.pallas_call(functools.partial(angles_kernel, part * size), grid=(steps...  3.36 us
    unnamed x14, local copies, waits for them, and re-layouts  2.55 us
    broadcast_in_dim x2, other arithmetic, shards(): return (angles_here[None], dual_last[None], consensus_last[None])  1.51 us
  transfers between devices with their start and end apart: 17, of which 12 were waited for; matrix products, arithmetic and copies ran while one was open for 12% of the time, Pallas kernels for 5%

profile of v4, /device:TPU:0, one launch (start us, length us, event | category | flops | bytes accessed | tf_op | source)
XLA Modules:
  0.0 74.4 jit_solution(15487338458727327625)
XLA Ops:
  0.6 0.0 copy-start
  0.6 1.0 %copy-done = f32[1,32,4096]{2,1,0:T(8,128)S(1)} copy-done((f32[1,32,4096]{2,1,0:T(8,128)S(1)}, f32[1,32,4096]{2,1,0:T(8,128)}, u32[]{:S(2)}) %copy-start) | copy-done | bytes 524312
  1.7 0.0 copy-start.1
  1.7 0.8 %copy-done.1 = f32[1,32,512]{2,1,0:T(8,128)S(1)} copy-done((f32[1,32,512]{2,1,0:T(8,128)S(1)}, f32[1,32,512]{2,1,0:T(8,128)}, u32[]{:S(2)}) %copy-start.1) | copy-done | bytes 65560
  2.5 0.0 copy-start.3
  2.5 0.7 copy-done.3
  3.2 0.6 shard_map.85
  3.8 3.1 %collective-permute-start = (bf16[32,4608]{1,0:T(8,128)(2,1)S(1)}, bf16[32,4608]{1,0:T(8,128)(2,1)S(1)}, u32[]{:S(2)}, u32[]{:S(2)}) collective-permute-start(bf16[32,4608]{1,0:T(8,128)(2,1)S(1)} %shard_map.85), channel_id=1, source_target_pairs={{0,2},{1,3},{2,0},{3,1},{4,6},{5,7},{6,4},{7,5},{8,10},{9,11},{10,... | collective-permute-start | bytes 884744 | tf_op jit(solution)/shard_map/ppermute | solution.py:33
  6.8 0.8 %fusion.17 = (s32[1,512]{1,0:T(1,128)S(1)}, s32[1,512]{1,0:T(1,128)S(1)}, s32[1,512]{1,0:T(1,128)S(1)}) fusion(s32[]{:T(128)S(6)} %axis_index.15, s32[8,512]{1,0:T(8,128)} %param.11, s32[]{:T(128)S(6)} %select_n.49, s32[8,512]{1,0:T(8,128)} %param.10), kind=kLoop, calls=%fused_computation.62 | loop fusion | flops 17408 | bytes 10248 | tf_op jit(solution)/shard_map/xor | solution.py:188
  7.6 6.2 %collective-permute-done = bf16[32,4608]{1,0:T(8,128)(2,1)S(1)} collective-permute-done((bf16[32,4608]{1,0:T(8,128)(2,1)S(1)}, bf16[32,4608]{1,0:T(8,128)(2,1)S(1)}, u32[]{:S(2)}, u32[]{:S(2)}) %collective-permute-start) | collective-permute-done | bytes 294944 | tf_op jit(solution)/shard_map/ppermute | solution.py:33
  13.8 0.0 slice-start
  13.9 0.1 collective-permute-start.1
  14.0 0.0 slice-start.1
  14.0 0.0 copy-start.2
  14.0 0.0 copy-start.4
  14.0 7.3 %fusion.3.factor_ends = bf16[1024,512]{1,0:T(8,128)(2,1)S(1)} fusion(s32[512]{0:T(512)S(1)} %bitcast.25, bf16[1,1024,4096]{2,1,0:T(8,128)(2,1)} %param.7), kind=kOutput, calls=%fused_computation.4 | convolution fusion | flops 4297588736 | bytes 9439232 | tf_op jit(solution)/shard_map/dot_general | solution.py:28
  21.3 0.0 collective-permute-done.1.far
  21.3 0.0 slice-done
  21.3 0.0 slice-done.1
  21.4 0.0 copy-done.2
  21.4 0.0 copy-done.4
  21.4 4.5 %shard_map.86 = (f32[128,1024]{1,0:T(8,128)S(1)}, f32[64,512]{1,0:T(8,128)S(1)}, f32[64,512]{1,0:T(8,128)S(1)}) custom-call(s32[8]{0:T(128)S(1)} %copy-done.4, bf16[64,4608]{1,0:T(8,128)(2,1)S(1)} %pad_maximum_fusion.near, bf16[64,4608]{1,0:T(8,128)(2,1)S(1)} %collective-permute-done.1.far, f32[32,512]{1,0:T(8,128)S(1)} %bitcast.22, ...), custom_call_target="tpu_custom_call" | custom-call | tf_op jit(solution)/shard_map/pallas_call | solution.py:99
  25.9 0.5 collective-permute-start.2
  26.4 1.0 %collective-permute-done.2 = f32[64,512]{1,0:T(8,128)S(1)} collective-permute-done((f32[64,512]{1,0:T(8,128)S(1)}, f32[64,512]{1,0:T(8,128)S(1)}, u32[]{:S(2)}, u32[]{:S(2)}) %collective-permute-start.2) | collective-permute-done | bytes 131104 | tf_op jit(solution)/shard_map/ppermute | solution.py:33
  27.4 1.8 %collective-permute-start.3 = (bf16[96,512]{1,0:T(8,128)(2,1)S(1)}, bf16[96,512]{1,0:T(8,128)(2,1)S(1)}, u32[]{:S(2)}, u32[]{:S(2)}) collective-permute-start(bf16[96,512]{1,0:T(8,128)(2,1)S(1)} %pad_maximum_fusion.1), channel_id=1, source_target_pairs={{0,2},{1,3},{2,0},{3,1},{4,6},{5,7},{6,4},{7,5},{8,10},{9,11},{10,... | collective-permute-start | bytes 294920 | tf_op jit(solution)/shard_map/ppermute | solution.py:33
  29.2 3.3 %collective-permute-done.3 = bf16[96,512]{1,0:T(8,128)(2,1)S(1)} collective-permute-done((bf16[96,512]{1,0:T(8,128)(2,1)S(1)}, bf16[96,512]{1,0:T(8,128)(2,1)S(1)}, u32[]{:S(2)}, u32[]{:S(2)}) %collective-permute-start.3) | collective-permute-done | bytes 98336 | tf_op jit(solution)/shard_map/ppermute | solution.py:33
  32.6 1.8 %collective-permute-start.4 = (bf16[64,512]{1,0:T(8,128)(2,1)S(1)}, bf16[64,512]{1,0:T(8,128)(2,1)S(1)}, u32[]{:S(2)}, u32[]{:S(2)}) collective-permute-start(bf16[64,512]{1,0:T(8,128)(2,1)S(1)} %get-tuple-element.30), channel_id=1, source_target_pairs={{0,4},{4,0},{8,12},{12,8},{16,20},{20,16},{24,28},{28,24},{1,5},{5... | collective-permute-start | bytes 196616 | tf_op jit(solution)/shard_map/ppermute | solution.py:33
  34.4 2.5 %collective-permute-done.4 = bf16[64,512]{1,0:T(8,128)(2,1)S(1)} collective-permute-done((bf16[64,512]{1,0:T(8,128)(2,1)S(1)}, bf16[64,512]{1,0:T(8,128)(2,1)S(1)}, u32[]{:S(2)}, u32[]{:S(2)}) %collective-permute-start.4) | collective-permute-done | bytes 65568 | tf_op jit(solution)/shard_map/ppermute | solution.py:33
  37.0 1.9 %collective-permute-start.5 = (bf16[64,512]{1,0:T(8,128)(2,1)S(1)}, bf16[64,512]{1,0:T(8,128)(2,1)S(1)}, u32[]{:S(2)}, u32[]{:S(2)}) collective-permute-start(bf16[64,512]{1,0:T(8,128)(2,1)S(1)} %broadcast_select_fusion.1), channel_id=1, source_target_pairs={{0,8},{4,12},{8,0},{12,4},{16,24},{20,28},{24,16},{28,20},{1,9},{5... | collective-permute-start | bytes 196616 | tf_op jit(solution)/shard_map/ppermute | solution.py:33
  38.8 2.5 %collective-permute-done.5 = bf16[64,512]{1,0:T(8,128)(2,1)S(1)} collective-permute-done((bf16[64,512]{1,0:T(8,128)(2,1)S(1)}, bf16[64,512]{1,0:T(8,128)(2,1)S(1)}, u32[]{:S(2)}, u32[]{:S(2)}) %collective-permute-start.5) | collective-permute-done | bytes 65568 | tf_op jit(solution)/shard_map/ppermute | solution.py:33
  41.3 3.1 %collective-permute-start.6 = (bf16[64,512]{1,0:T(8,128)(2,1)S(1)}, bf16[64,512]{1,0:T(8,128)(2,1)S(1)}, u32[]{:S(2)}, u32[]{:S(2)}) collective-permute-start(bf16[64,512]{1,0:T(8,128)(2,1)S(1)} %broadcast_select_fusion.3), channel_id=1, source_target_pairs={{0,16},{4,20},{8,24},{12,28},{16,0},{20,4},{24,8},{28,12},{1,17},{... | collective-permute-start | bytes 196616 | tf_op jit(solution)/shard_map/ppermute | solution.py:33
  44.4 2.2 %collective-permute-done.6 = bf16[64,512]{1,0:T(8,128)(2,1)S(1)} collective-permute-done((bf16[64,512]{1,0:T(8,128)(2,1)S(1)}, bf16[64,512]{1,0:T(8,128)(2,1)S(1)}, u32[]{:S(2)}, u32[]{:S(2)}) %collective-permute-start.6) | collective-permute-done | bytes 65568 | tf_op jit(solution)/shard_map/ppermute | solution.py:33
  46.7 0.3 subtract_convert_fusion
  47.0 0.1 collective-permute-start.7
  47.1 1.2 %collective-permute-done.7.far = bf16[64,512]{1,0:T(8,128)(2,1)S(1)} collective-permute-done((bf16[64,512]{1,0:T(8,128)(2,1)S(1)}, bf16[64,512]{1,0:T(8,128)(2,1)S(1)}, u32[]{:S(2)}, u32[]{:S(2)}) %collective-permute-start.7) | collective-permute-done | bytes 65568 | tf_op jit(solution)/shard_map/ppermute | solution.py:33
  48.3 1.2 %shard_map.87 = (bf16[128,1024]{1,0:T(8,128)(2,1)S(1)}, f32[64,512]{1,0:T(8,128)S(1)}, f32[64,512]{1,0:T(8,128)S(1)}) custom-call(s32[8]{0:T(128)S(1)} %copy-done.4, f32[128,1024]{1,0:T(8,128)S(1)} %get-tuple-element.13.base, bf16[64,512]{1,0:T(8,128)(2,1)S(1)} %get-tuple-element.38.near, bf16[64,512]{1,0:T(8,128)(2,1)S(1)} %collective-permute-done.7.far, ...), custom_call_target="tpu_custom_call" | custom-call | tf_op jit(solution)/shard_map/pallas_call | solution.py:141
  49.5 0.2 collective-permute-start.12
  49.7 1.2 %collective-permute-done.12 = f32[64,512]{1,0:T(8,128)S(1)} collective-permute-done((f32[64,512]{1,0:T(8,128)S(1)}, f32[64,512]{1,0:T(8,128)S(1)}, u32[]{:S(2)}, u32[]{:S(2)}) %collective-permute-start.12) | collective-permute-done | bytes 131104 | tf_op jit(solution)/shard_map/ppermute | solution.py:33
  51.0 1.7 %collective-permute-start.13 = (bf16[64,512]{1,0:T(8,128)(2,1)S(1)}, bf16[64,512]{1,0:T(8,128)(2,1)S(1)}, u32[]{:S(2)}, u32[]{:S(2)}) collective-permute-start(bf16[64,512]{1,0:T(8,128)(2,1)S(1)} %pad_maximum_fusion.2), channel_id=1, source_target_pairs={{0,2},{1,3},{2,0},{3,1},{4,6},{5,7},{6,4},{7,5},{8,10},{9,11},{10,... | collective-permute-start | bytes 196616 | tf_op jit(solution)/shard_map/ppermute | solution.py:33
  52.7 2.7 %collective-permute-done.13 = bf16[64,512]{1,0:T(8,128)(2,1)S(1)} collective-permute-done((bf16[64,512]{1,0:T(8,128)(2,1)S(1)}, bf16[64,512]{1,0:T(8,128)(2,1)S(1)}, u32[]{:S(2)}, u32[]{:S(2)}) %collective-permute-start.13) | collective-permute-done | bytes 65568 | tf_op jit(solution)/shard_map/ppermute | solution.py:33
  55.4 1.6 %collective-permute-start.14 = (bf16[64,512]{1,0:T(8,128)(2,1)S(1)}, bf16[64,512]{1,0:T(8,128)(2,1)S(1)}, u32[]{:S(2)}, u32[]{:S(2)}) collective-permute-start(bf16[64,512]{1,0:T(8,128)(2,1)S(1)} %pad_maximum_fusion.3), channel_id=1, source_target_pairs={{0,4},{4,0},{8,12},{12,8},{16,20},{20,16},{24,28},{28,24},{1,5},{5... | collective-permute-start | bytes 196616 | tf_op jit(solution)/shard_map/ppermute | solution.py:33
  57.0 1.7 %shard_map.89 = (f32[64,2048]{1,0:T(8,128)S(1)}, bf16[64,2048]{1,0:T(8,128)(2,1)S(1)}) custom-call(s32[8]{0:T(128)S(1)} %copy-done.4, bf16[128,1024]{1,0:T(8,128)(2,1)S(1)} %get-tuple-element.16.second, bf16[1024,4096]{1,0:T(8,128)(2,1)S(1)} %bitcast.18), custom_call_target="tpu_custom_call" | custom-call | tf_op jit(solution)/shard_map/pallas_call | solution.py:168
  58.7 0.1 collective-permute-start.10
  58.8 1.7 %shard_map.88 = (f32[64,2048]{1,0:T(8,128)S(1)}, bf16[64,2048]{1,0:T(8,128)(2,1)S(1)}) custom-call(s32[8]{0:T(128)S(1)} %copy-done.4, bf16[128,1024]{1,0:T(8,128)(2,1)S(1)} %get-tuple-element.16.second, bf16[1024,4096]{1,0:T(8,128)(2,1)S(1)} %bitcast.19), custom_call_target="tpu_custom_call" | custom-call | tf_op jit(solution)/shard_map/pallas_call | solution.py:168
  60.5 0.5 collective-permute-start.8
  61.0 0.0 collective-permute-done.14
  61.1 1.7 %collective-permute-start.15 = (bf16[64,512]{1,0:T(8,128)(2,1)S(1)}, bf16[64,512]{1,0:T(8,128)(2,1)S(1)}, u32[]{:S(2)}, u32[]{:S(2)}) collective-permute-start(bf16[64,512]{1,0:T(8,128)(2,1)S(1)} %broadcast_select_fusion), channel_id=1, source_target_pairs={{0,8},{4,12},{8,0},{12,4},{16,24},{20,28},{24,16},{28,20},{1,9},{5... | collective-permute-start | bytes 196616 | tf_op jit(solution)/shard_map/ppermute | solution.py:33
  62.7 0.0 collective-permute-done.10
  62.8 1.6 %collective-permute-start.11 = (bf16[32,2048]{1,0:T(8,128)(2,1)S(1)}, bf16[32,2048]{1,0:T(8,128)(2,1)S(1)}, u32[]{:S(2)}, u32[]{:S(2)}) collective-permute-start(bf16[32,2048]{1,0:T(8,128)(2,1)S(1)} %slice.128), channel_id=1, source_target_pairs={{0,2},{1,3},{2,0},{3,1},{4,6},{5,7},{6,4},{7,5},{8,10},{9,11},{10,... | collective-permute-start | bytes 393224 | tf_op jit(solution)/shard_map/ppermute | solution.py:33
  64.4 1.0 %collective-permute-done.15 = bf16[64,512]{1,0:T(8,128)(2,1)S(1)} collective-permute-done((bf16[64,512]{1,0:T(8,128)(2,1)S(1)}, bf16[64,512]{1,0:T(8,128)(2,1)S(1)}, u32[]{:S(2)}, u32[]{:S(2)}) %collective-permute-start.15) | collective-permute-done | bytes 65568 | tf_op jit(solution)/shard_map/ppermute | solution.py:33
  65.4 3.0 %collective-permute-start.16 = (bf16[64,512]{1,0:T(8,128)(2,1)S(1)}, bf16[64,512]{1,0:T(8,128)(2,1)S(1)}, u32[]{:S(2)}, u32[]{:S(2)}) collective-permute-start(bf16[64,512]{1,0:T(8,128)(2,1)S(1)} %broadcast_select_fusion.2), channel_id=1, source_target_pairs={{0,16},{4,20},{8,24},{12,28},{16,0},{20,4},{24,8},{28,12},{1,17},{... | collective-permute-start | bytes 196616 | tf_op jit(solution)/shard_map/ppermute | solution.py:33
  68.4 0.0 collective-permute-done.8
  68.4 0.1 convert_add_fusion.1
  68.5 1.6 %collective-permute-start.9 = (bf16[32,2048]{1,0:T(8,128)(2,1)S(1)}, bf16[32,2048]{1,0:T(8,128)(2,1)S(1)}, u32[]{:S(2)}, u32[]{:S(2)}) collective-permute-start(bf16[32,2048]{1,0:T(8,128)(2,1)S(1)} %slice.129), channel_id=1, source_target_pairs={{0,2},{1,3},{2,0},{3,1},{4,6},{5,7},{6,4},{7,5},{8,10},{9,11},{10,... | collective-permute-start | bytes 393224 | tf_op jit(solution)/shard_map/ppermute | solution.py:33
  70.1 0.8 %collective-permute-done.16 = bf16[64,512]{1,0:T(8,128)(2,1)S(1)} collective-permute-done((bf16[64,512]{1,0:T(8,128)(2,1)S(1)}, bf16[64,512]{1,0:T(8,128)(2,1)S(1)}, u32[]{:S(2)}, u32[]{:S(2)}) %collective-permute-start.16) | collective-permute-done | bytes 65568 | tf_op jit(solution)/shard_map/ppermute | solution.py:33
  70.9 0.3 fusion.4
  71.2 0.0 collective-permute-done.11
  71.3 0.7 multiply_bitcast_fusion
  72.0 1.6 %collective-permute-done.9 = bf16[32,2048]{1,0:T(8,128)(2,1)S(1)} collective-permute-done((bf16[32,2048]{1,0:T(8,128)(2,1)S(1)}, bf16[32,2048]{1,0:T(8,128)(2,1)S(1)}, u32[]{:S(2)}, u32[]{:S(2)}) %collective-permute-start.9) | collective-permute-done | bytes 131104 | tf_op jit(solution)/shard_map/ppermute | solution.py:33
  73.6 0.8 %maximum_bitcast_fusion = f32[1,32,4096]{2,1,0:T(8,128)} fusion(f32[32,2048]{1,0:T(8,128)S(1)} %slice_add_fusion, f32[32,2048]{1,0:T(8,128)S(1)} %slice_add_fusion.1), kind=kLoop, calls=%fused_computation.9 | loop fusion | flops 131072 | bytes 1048576 | tf_op jit(solution)/shard_map/broadcast_in_dim | solution.py:248
  (26 shorter events, 0.5 us)
Async XLA Ops:
  0.6 1.0 %copy-start = (f32[1,32,4096]{2,1,0:T(8,128)S(1)}, f32[1,32,4096]{2,1,0:T(8,128)}, u32[]{:S(2)}) copy-start(f32[1,32,4096]{2,1,0:T(8,128)} %param.6) | copy-start | bytes 1572868
  1.7 0.8 %copy-start.1 = (f32[1,32,512]{2,1,0:T(8,128)S(1)}, f32[1,32,512]{2,1,0:T(8,128)}, u32[]{:S(2)}) copy-start(f32[1,32,512]{2,1,0:T(8,128)} %param.8) | copy-start | bytes 196612
  2.5 0.7 copy-start.3
  3.8 10.1 %collective-permute-start = (bf16[32,4608]{1,0:T(8,128)(2,1)S(1)}, bf16[32,4608]{1,0:T(8,128)(2,1)S(1)}, u32[]{:S(2)}, u32[]{:S(2)}) collective-permute-start(bf16[32,4608]{1,0:T(8,128)(2,1)S(1)} %shard_map.85), channel_id=1, source_target_pairs={{0,2},{1,3},{2,0},{3,1},{4,6},{5,7},{6,4},{7,5},{8,10},{9,11},{10,... | collective-permute-start | bytes 884744 | tf_op jit(solution)/shard_map/ppermute | solution.py:33
  13.8 7.5 %slice-start = ((s8[8388608]{0:T(1024)(128)(4,1)}), s8[4194304]{0:T(1024)(128)(4,1)S(1)}, s32[]{:S(2)}) async-start(s8[8388608]{0:T(1024)(128)(4,1)} %bitcast.15), calls=%async_computation | async-start | bytes 8388608
  13.9 7.4 %collective-permute-start.1 = (bf16[64,4608]{1,0:T(8,128)(2,1)S(1)}, bf16[64,4608]{1,0:T(8,128)(2,1)S(1)}, u32[]{:S(2)}, u32[]{:S(2)}) collective-permute-start(bf16[64,4608]{1,0:T(8,128)(2,1)S(1)} %pad_maximum_fusion.near), channel_id=1, source_target_pairs={{0,1},{1,0},{2,3},{3,2},{4,5},{5,4},{6,7},{7,6},{8,9},{9,8},{10,11... | collective-permute-start | bytes 1769480 | tf_op jit(solution)/shard_map/ppermute | solution.py:33
  14.0 7.4 %slice-start.1 = ((s8[8388608]{0:T(1024)(128)(4,1)}), s8[4194304]{0:T(1024)(128)(4,1)S(1)}, s32[]{:S(2)}) async-start(s8[8388608]{0:T(1024)(128)(4,1)} %bitcast.15), calls=%async_computation.1 | async-start | bytes 8388608
  14.0 7.4 %copy-start.2 = (f32[1,32,512]{2,1,0:T(8,128)S(1)}, f32[1,32,512]{2,1,0:T(8,128)}, u32[]{:S(2)}) copy-start(f32[1,32,512]{2,1,0:T(8,128)} %param.8) | copy-start | bytes 196612
  14.0 7.4 %copy-start.4 = (s32[8]{0:T(128)S(1)}, s32[8]{0:T(128)}, u32[]{:S(2)}) copy-start(s32[8]{0:T(128)} %area_size.9) | copy-start | bytes 100
  25.9 1.5 %collective-permute-start.2 = (f32[64,512]{1,0:T(8,128)S(1)}, f32[64,512]{1,0:T(8,128)S(1)}, u32[]{:S(2)}, u32[]{:S(2)}) collective-permute-start(f32[64,512]{1,0:T(8,128)S(1)} %get-tuple-element.15), channel_id=1, source_target_pairs={{0,1},{1,0},{2,3},{3,2},{4,5},{5,4},{6,7},{7,6},{8,9},{9,8},{10,11... | collective-permute-start | bytes 393224 | tf_op jit(solution)/shard_map/ppermute | solution.py:33
  27.4 5.1 %collective-permute-start.3 = (bf16[96,512]{1,0:T(8,128)(2,1)S(1)}, bf16[96,512]{1,0:T(8,128)(2,1)S(1)}, u32[]{:S(2)}, u32[]{:S(2)}) collective-permute-start(bf16[96,512]{1,0:T(8,128)(2,1)S(1)} %pad_maximum_fusion.1), channel_id=1, source_target_pairs={{0,2},{1,3},{2,0},{3,1},{4,6},{5,7},{6,4},{7,5},{8,10},{9,11},{10,... | collective-permute-start | bytes 294920 | tf_op jit(solution)/shard_map/ppermute | solution.py:33
  32.6 4.3 %collective-permute-start.4 = (bf16[64,512]{1,0:T(8,128)(2,1)S(1)}, bf16[64,512]{1,0:T(8,128)(2,1)S(1)}, u32[]{:S(2)}, u32[]{:S(2)}) collective-permute-start(bf16[64,512]{1,0:T(8,128)(2,1)S(1)} %get-tuple-element.30), channel_id=1, source_target_pairs={{0,4},{4,0},{8,12},{12,8},{16,20},{20,16},{24,28},{28,24},{1,5},{5... | collective-permute-start | bytes 196616 | tf_op jit(solution)/shard_map/ppermute | solution.py:33
  37.0 4.3 %collective-permute-start.5 = (bf16[64,512]{1,0:T(8,128)(2,1)S(1)}, bf16[64,512]{1,0:T(8,128)(2,1)S(1)}, u32[]{:S(2)}, u32[]{:S(2)}) collective-permute-start(bf16[64,512]{1,0:T(8,128)(2,1)S(1)} %broadcast_select_fusion.1), channel_id=1, source_target_pairs={{0,8},{4,12},{8,0},{12,4},{16,24},{20,28},{24,16},{28,20},{1,9},{5... | collective-permute-start | bytes 196616 | tf_op jit(solution)/shard_map/ppermute | solution.py:33
  41.3 5.4 %collective-permute-start.6 = (bf16[64,512]{1,0:T(8,128)(2,1)S(1)}, bf16[64,512]{1,0:T(8,128)(2,1)S(1)}, u32[]{:S(2)}, u32[]{:S(2)}) collective-permute-start(bf16[64,512]{1,0:T(8,128)(2,1)S(1)} %broadcast_select_fusion.3), channel_id=1, source_target_pairs={{0,16},{4,20},{8,24},{12,28},{16,0},{20,4},{24,8},{28,12},{1,17},{... | collective-permute-start | bytes 196616 | tf_op jit(solution)/shard_map/ppermute | solution.py:33
  47.0 1.3 %collective-permute-start.7 = (bf16[64,512]{1,0:T(8,128)(2,1)S(1)}, bf16[64,512]{1,0:T(8,128)(2,1)S(1)}, u32[]{:S(2)}, u32[]{:S(2)}) collective-permute-start(bf16[64,512]{1,0:T(8,128)(2,1)S(1)} %get-tuple-element.38.near), channel_id=1, source_target_pairs={{0,1},{1,0},{2,3},{3,2},{4,5},{5,4},{6,7},{7,6},{8,9},{9,8},{10,11... | collective-permute-start | bytes 196616 | tf_op jit(solution)/shard_map/ppermute | solution.py:33
  49.5 1.4 %collective-permute-start.12 = (f32[64,512]{1,0:T(8,128)S(1)}, f32[64,512]{1,0:T(8,128)S(1)}, u32[]{:S(2)}, u32[]{:S(2)}) collective-permute-start(f32[64,512]{1,0:T(8,128)S(1)} %get-tuple-element.22), channel_id=1, source_target_pairs={{0,1},{1,0},{2,3},{3,2},{4,5},{5,4},{6,7},{7,6},{8,9},{9,8},{10,11... | collective-permute-start | bytes 393224 | tf_op jit(solution)/shard_map/ppermute | solution.py:33
  51.0 4.3 %collective-permute-start.13 = (bf16[64,512]{1,0:T(8,128)(2,1)S(1)}, bf16[64,512]{1,0:T(8,128)(2,1)S(1)}, u32[]{:S(2)}, u32[]{:S(2)}) collective-permute-start(bf16[64,512]{1,0:T(8,128)(2,1)S(1)} %pad_maximum_fusion.2), channel_id=1, source_target_pairs={{0,2},{1,3},{2,0},{3,1},{4,6},{5,7},{6,4},{7,5},{8,10},{9,11},{10,... | collective-permute-start | bytes 196616 | tf_op jit(solution)/shard_map/ppermute | solution.py:33
  55.4 5.7 %collective-permute-start.14 = (bf16[64,512]{1,0:T(8,128)(2,1)S(1)}, bf16[64,512]{1,0:T(8,128)(2,1)S(1)}, u32[]{:S(2)}, u32[]{:S(2)}) collective-permute-start(bf16[64,512]{1,0:T(8,128)(2,1)S(1)} %pad_maximum_fusion.3), channel_id=1, source_target_pairs={{0,4},{4,0},{8,12},{12,8},{16,20},{20,16},{24,28},{28,24},{1,5},{5... | collective-permute-start | bytes 196616 | tf_op jit(solution)/shard_map/ppermute | solution.py:33
  58.7 4.0 %collective-permute-start.10 = (bf16[64,2048]{1,0:T(8,128)(2,1)S(1)}, bf16[64,2048]{1,0:T(8,128)(2,1)S(1)}, u32[]{:S(2)}, u32[]{:S(2)}) collective-permute-start(bf16[64,2048]{1,0:T(8,128)(2,1)S(1)} %get-tuple-element.20), channel_id=1, source_target_pairs={{0,1},{1,0},{2,3},{3,2},{4,5},{5,4},{6,7},{7,6},{8,9},{9,8},{10,11... | collective-permute-start | bytes 786440 | tf_op jit(solution)/shard_map/ppermute | solution.py:33
  60.5 7.9 %collective-permute-start.8 = (bf16[64,2048]{1,0:T(8,128)(2,1)S(1)}, bf16[64,2048]{1,0:T(8,128)(2,1)S(1)}, u32[]{:S(2)}, u32[]{:S(2)}) collective-permute-start(bf16[64,2048]{1,0:T(8,128)(2,1)S(1)} %get-tuple-element.18), channel_id=1, source_target_pairs={{0,1},{1,0},{2,3},{3,2},{4,5},{5,4},{6,7},{7,6},{8,9},{9,8},{10,11... | collective-permute-start | bytes 786440 | tf_op jit(solution)/shard_map/ppermute | solution.py:33
  61.1 4.3 %collective-permute-start.15 = (bf16[64,512]{1,0:T(8,128)(2,1)S(1)}, bf16[64,512]{1,0:T(8,128)(2,1)S(1)}, u32[]{:S(2)}, u32[]{:S(2)}) collective-permute-start(bf16[64,512]{1,0:T(8,128)(2,1)S(1)} %broadcast_select_fusion), channel_id=1, source_target_pairs={{0,8},{4,12},{8,0},{12,4},{16,24},{20,28},{24,16},{28,20},{1,9},{5... | collective-permute-start | bytes 196616 | tf_op jit(solution)/shard_map/ppermute | solution.py:33
  62.8 8.4 %collective-permute-start.11 = (bf16[32,2048]{1,0:T(8,128)(2,1)S(1)}, bf16[32,2048]{1,0:T(8,128)(2,1)S(1)}, u32[]{:S(2)}, u32[]{:S(2)}) collective-permute-start(bf16[32,2048]{1,0:T(8,128)(2,1)S(1)} %slice.128), channel_id=1, source_target_pairs={{0,2},{1,3},{2,0},{3,1},{4,6},{5,7},{6,4},{7,5},{8,10},{9,11},{10,... | collective-permute-start | bytes 393224 | tf_op jit(solution)/shard_map/ppermute | solution.py:33
  65.4 5.5 %collective-permute-start.16 = (bf16[64,512]{1,0:T(8,128)(2,1)S(1)}, bf16[64,512]{1,0:T(8,128)(2,1)S(1)}, u32[]{:S(2)}, u32[]{:S(2)}) collective-permute-start(bf16[64,512]{1,0:T(8,128)(2,1)S(1)} %broadcast_select_fusion.2), channel_id=1, source_target_pairs={{0,16},{4,20},{8,24},{12,28},{16,0},{20,4},{24,8},{28,12},{1,17},{... | collective-permute-start | bytes 196616 | tf_op jit(solution)/shard_map/ppermute | solution.py:33
  68.5 5.0 %collective-permute-start.9 = (bf16[32,2048]{1,0:T(8,128)(2,1)S(1)}, bf16[32,2048]{1,0:T(8,128)(2,1)S(1)}, u32[]{:S(2)}, u32[]{:S(2)}) collective-permute-start(bf16[32,2048]{1,0:T(8,128)(2,1)S(1)} %slice.129), channel_id=1, source_target_pairs={{0,2},{1,3},{2,0},{3,1},{4,6},{5,7},{6,4},{7,5},{8,10},{9,11},{10,... | collective-permute-start | bytes 393224 | tf_op jit(solution)/shard_map/ppermute | solution.py:33

commit v5 on v4

--- a/solution.py
+++ b/solution.py
@@ -42,6 +42,10 @@
     return pltpu.CompilerParams(vmem_limit_bytes=mebibytes * 2**20)
 
 
+def off_chip(x):
+    return pltpu.with_memory_space_constraint(x, pltpu.HBM)
+
+
 def on_chip(x):
     return pltpu.with_memory_space_constraint(x, pltpu.VMEM)
 
@@ -60,77 +64,77 @@
         in_specs=[SCALARS, WHOLE, WHOLE],
         out_specs=WHOLE,
         compiler_params=room(4),
-    )(area_size, injection, dual)
-
-
-def base_kernel(area_size, near, far, dual, factor, factor_ends, base, keep, send, side, partial):
-    step = pl.program_id(0)
+    )(area_size, off_chip(injection), off_chip(dual))
+
+
+def base_kernel(
+    area_size, near, far, dual, factor, ends_top, ends_bottom, base, keep, send, side, partial
+):
     half = near.shape[0]
-    block, width = factor.shape
-
-    @pl.when(step == 0)
-    def _():
-        side[:half] = near[...]
-        side[half:] = far[...]
-        partial[...] = jnp.zeros_like(partial)
-
-    here = factor_ends[pl.ds(pl.multiple_of(step * block, block), block), :]
-    value = dot_nt(side[:, :width], factor[...])
-    start = lax.axis_index("scen") * (pl.num_programs(0) * block) + step * block
-    live = start + lax.broadcasted_iota(jnp.int32, value.shape, 1) < area_size[lax.axis_index("area")]
-    base[...] = value
-    first = jnp.where(live, value - dot_nt(side[:, width:], here), 0.0).astype(BF16)
-    partial[...] += dot_nn(first, here)
-
-    @pl.when(step == pl.num_programs(0) - 1)
-    def _():
-        count = dual.shape[0]
-        keep[:count] = PENALTY * partial[:count] + dual[...]
-        keep[count:] = PENALTY * partial[count:half]
-        send[...] = PENALTY * partial[half:]
+    count = dual.shape[0]
+    rows, width = factor.shape
+    block = rows // 2
+    side[:half] = near[...]
+    side[half:] = far[...]
+    for part, ends in enumerate((ends_top, ends_bottom)):
+        here = slice(part * block, (part + 1) * block)
+        value = dot_nt(side[:, :width], factor[here, :])
+        base[:, here] = value
+        start = lax.axis_index("scen") * rows + part * block
+        live = start + lax.broadcasted_iota(jnp.int32, value.shape, 1) < area_size[
+            lax.axis_index("area")
+        ]
+        first = value - dot_nt(side[:, width:], ends[...])
+        ends_part = dot_nn(jnp.where(live, first, 0.0).astype(BF16), ends[...])
+        if part:
+            ends_part = ends_part + partial[...]
+        partial[...] = ends_part
+    keep[:count] = PENALTY * partial[:count] + dual[...]
+    keep[count:] = PENALTY * partial[count:half]
+    send[...] = PENALTY * partial[half:]
 
 
 def base_product(area_size, near, far, dual, factor, factor_ends):
-    rows, width = factor.shape
+    rows = factor.shape[0]
     half, packed_width = near.shape
     ends_total = dual.shape[1]
-    block = 512
-    fixed = pl.BlockSpec((half, ends_total), lambda i: (0, 0))
     return pl.pallas_call(
         base_kernel,
-        grid=(rows // block,),
         out_shape=(
             pltpu.VMEM((2 * half, rows), F32),
             pltpu.VMEM((half, ends_total), F32),
             pltpu.VMEM((half, ends_total), F32),
         ),
-        in_specs=[
-            SCALARS,
-            WHOLE,
-            WHOLE,
-            WHOLE,
-            pl.BlockSpec((block, width), lambda i: (i, 0)),
-            WHOLE,
-        ],
-        out_specs=(pl.BlockSpec((2 * half, block), lambda i: (0, i)), fixed, fixed),
+        in_specs=[SCALARS] + [WHOLE] * 6,
+        out_specs=(WHOLE, WHOLE, WHOLE),
         scratch_shapes=[
             pltpu.VMEM((2 * half, packed_width), BF16),
             pltpu.VMEM((2 * half, ends_total), F32),
         ],
         compiler_params=room(24),
-    )(area_size, on_chip(near), on_chip(far), dual, factor, on_chip(factor_ends))
-
-
-def second_kernel(area_size, base, near, far, factor_ends, second, keep, send, spread):
+    )(area_size, *map(on_chip, (near, far, dual, factor, *factor_ends)))
+
+
+def second_kernel(
+    area_size, base, near, far, ends_top, ends_bottom, second, keep, send, spread
+):
     half = near.shape[0]
     spread[:half] = near[...]
     spread[half:] = far[...]
-    here = factor_ends[...]
-    start = lax.axis_index("scen") * here.shape[0]
-    live = start + lax.broadcasted_iota(jnp.int32, base.shape, 1) < area_size[lax.axis_index("area")]
-    rows = jnp.where(live, base[...] - dot_nt(spread[...], here), 0.0).astype(BF16)
-    second[...] = rows
-    partial = PENALTY * dot_nn(rows, here)
+    rows = base.shape[1]
+    block = rows // 2
+    partial = None
+    for part, ends in enumerate((ends_top, ends_bottom)):
+        here = slice(part * block, (part + 1) * block)
+        value = base[:, here] - dot_nt(spread[...], ends[...])
+        start = lax.axis_index("scen") * rows + part * block
+        live = start + lax.broadcasted_iota(jnp.int32, value.shape, 1) < area_size[
+            lax.axis_index("area")
+        ]
+        value = jnp.where(live, value, 0.0).astype(BF16)
+        second[:, here] = value
+        ends_part = PENALTY * dot_nn(value, ends[...])
+        partial = ends_part if partial is None else partial + ends_part
     keep[...] = partial[:half]
     send[...] = partial[half:]
 
@@ -141,38 +145,36 @@
     return pl.pallas_call(
         second_kernel,
         out_shape=(pltpu.VMEM(base.shape, BF16), shape, shape),
-        in_specs=[SCALARS, WHOLE, WHOLE, WHOLE, WHOLE],
+        in_specs=[SCALARS] + [WHOLE] * 5,
         out_specs=(WHOLE, WHOLE, WHOLE),
         scratch_shapes=[pltpu.VMEM((2 * half, ends_total), BF16)],
         compiler_params=room(8),
-    )(area_size, *map(on_chip, (base, near, far, factor_ends)))
+    )(area_size, *map(on_chip, (base, near, far, *factor_ends)))
 
 
 def angles_kernel(first_bus, area_size, second, factor, keep, send):
-    half, depth = keep.shape
-    value = dot_nn(second[...], factor[...])
-    start = first_bus + pl.program_id(0) * depth
-    live = start + lax.broadcasted_iota(jnp.int32, value.shape, 1) < area_size[lax.axis_index("area")]
-    value = jnp.where(live, value, 0.0)
-    keep[...] = value[:half]
-    send[...] = value[half:].astype(BF16)
+    half, size = keep.shape
+    depth = 512
+    for start in range(0, size, depth):
+        here = slice(start, start + depth)
+        buses = slice(first_bus + start, first_bus + start + depth)
+        value = dot_nn(second[...], factor[:, buses])
+        bus = buses.start + lax.broadcasted_iota(jnp.int32, value.shape, 1)
+        value = jnp.where(bus < area_size[lax.axis_index("area")], value, 0.0)
+        keep[:, here] = value[:half]
+        send[:, here] = value[half:].astype(BF16)
 
 
 def angles_product(area_size, second, factor, parts, part):
-    rows, width = factor.shape
     half = second.shape[0] // 2
-    depth = 1024
-    size = width // parts
-    steps = size // depth
-    spec = pl.BlockSpec((half, depth), lambda i: (0, i))
+    size = factor.shape[1] // parts
     return pl.pallas_call(
         functools.partial(angles_kernel, part * size),
-        grid=(steps,),
         out_shape=(pltpu.VMEM((half, size), F32), pltpu.VMEM((half, size), BF16)),
-        in_specs=[SCALARS, WHOLE, pl.BlockSpec((rows, depth), lambda i: (0, part * steps + i))],
-        out_specs=(spec, spec),
+        in_specs=[SCALARS, WHOLE, WHOLE],
+        out_specs=(WHOLE, WHOLE),
         compiler_params=room(14),
-    )(area_size, on_chip(second), factor)
+    )(area_size, on_chip(second), on_chip(factor))
 
 
 def shards(injection, kkt_factor, dual_price, area_size, bnd_bus, peer_end):
@@ -193,7 +195,9 @@
     pair_far = swap(pair, "scen", 1)
 
     pick = (jnp.arange(width)[:, None] == buses[None, :]).astype(BF16)
-    factor_ends = dot_nn(factor, pick).astype(BF16)
+    factor_ends = []
+    for rows in jnp.split(factor, 2, axis=0):
+        factor_ends.append(dot_nn(rows, pick).astype(BF16))
     slots = jnp.arange(ends_total)
     mate = ((slots // CAP * CAP + peers % CAP)[None, :] == slots[:, None]).astype(BF16)
 
@@ -203,10 +207,10 @@
 
     def exchange(q):
         moved = q
-        bit = 1
-        while bit < areas_all:
-            moved = jnp.where((offset & bit)[None, :] != 0, swap(moved, "area", bit), moved)
-            bit *= 2
+        for hop in range(areas_all.bit_length() - 1):
+            bit = 1 << hop
+            other = swap(moved, "area", bit)
+            moved = jnp.where((offset & bit)[None, :] != 0, other, moved)
         return dot_nn(moved, mate)
 
     def with_low(x, low_rows):
@@ -242,10 +246,13 @@
 
     pieces = []
     for keep, send in products:
-        keep = keep + swap(send, "scen", 1).astype(F32)
-        pieces.append(keep[:columns] + swap(keep[columns:].astype(BF16), "scen", 2).astype(F32))
-    angles_here = jnp.concatenate(pieces, axis=1)
-    return (angles_here[None], dual_last[None], consensus_last[None])
+        other = swap(send, "scen", 1)
+        keep = keep + other.astype(F32)
+        sent = keep[columns:].astype(BF16)
+        other = swap(sent, "scen", 2)
+        pieces.append(keep[:columns] + other.astype(F32))
+    angles_here = jnp.concatenate(pieces, axis=1)[None]
+    return (angles_here, dual_last[None], consensus_last[None])
 
 
 def solution(mesh):

time: 74.8 us -> 67.5 us (0.902)
  waiting for transfers between devices: 26.3 us -> 21.5 us
  local copies, waits for them, and re-layouts: 2.59 us -> 0.71 us
    ppermute x17, waiting for transfers between devices: 26.3 us -> 21.5 us  [swap(): return lax.ppermute(x, axis, [(i, i ^ bit) for i in range(n)])]
    unnamed x14 -> x8, local copies, waits for them, and re-layouts: 2.55 us -> 0.67 us
    pallas_call x3, Pallas kernels: 7.83 us -> 6.62 us  [the longest x1 4.05 us: base_product(): pl.pallas_call(base_kernel, out_shape=(pltpu.VMEM((2 * half, rows), F32),...]
    dot_general x3 -> x4, matrix products: 7.91 us -> 7.88 us  [dot_nn(): return jnp.dot(a, b, preferred_element_type=F32)]
  transfers between devices with their start and end apart: 17 -> 17, of which waited for: 12 -> 12; matrix products, arithmetic and copies ran while one was open for 12% -> 14% of each run, Pallas kernels for 5% -> 4%
where the time goes in v5:
time: 67.5 us; the launch traced here: 67.2 us
  starting transfers between devices  24.3 us (36%)
  waiting for transfers between devices  21.5 us (32%)
  Pallas kernels  9.08 us (13%)
  matrix products  7.88 us (12%)
  other arithmetic  2.74 us (4%)
  between operations  0.95 us (1%)
  local copies, waits for them, and re-layouts  0.71 us (1%)
    ppermute x17, starting transfers between devices, swap(): return lax.ppermute(x, axis, [(i, i ^ bit) for i in range(n)])  24.3 us
    ppermute x17, waiting for transfers between devices, swap(): return lax.ppermute(x, axis, [(i, i ^ bit) for i in range(n)])  21.5 us
    dot_general x4, matrix products, dot_nn(): return jnp.dot(a, b, preferred_element_type=F32)  7.88 us
    pallas_call x1, Pallas kernels, base_product(): pl.pallas_call(base_kernel, out_shape=(pltpu.VMEM((2 * half, rows), F32),...  4.05 us
    pallas_call x2, Pallas kernels, angles_product(): pl.pallas_call(functools.partial(angles_kernel, part * size), out_shape=(...  2.57 us
    pallas_call x1, Pallas kernels, second_product(): pl.pallas_call(second_kernel, out_shape=(pltpu.VMEM(base.shape, BF16), sh...  1.35 us
  transfers between devices with their start and end apart: 17, of which 12 were waited for; matrix products, arithmetic and copies ran while one was open for 14% of the time, Pallas kernels for 4%

profile of v5, /device:TPU:0, one launch (start us, length us, event | category | flops | bytes accessed | tf_op | source)
XLA Modules:
  0.0 67.2 jit_solution(15050631659245646684)
XLA Ops:
  0.6 0.0 copy-start.2
  0.6 0.6 copy-done.2
  1.3 1.1 %shard_map.85 = bf16[32,4608]{1,0:T(8,128)(2,1)S(1)} custom-call(s32[8]{0:T(128)S(1)} %copy-done.2, f32[32,4096]{1,0:T(8,128)} %bitcast.34, f32[32,512]{1,0:T(8,128)} %bitcast.32), custom_call_target="tpu_custom_call" | custom-call | tf_op jit(solution)/shard_map/pallas_call | solution.py:61
  2.4 3.1 %collective-permute-start = (bf16[32,4608]{1,0:T(8,128)(2,1)S(1)}, bf16[32,4608]{1,0:T(8,128)(2,1)S(1)}, u32[]{:S(2)}, u32[]{:S(2)}) collective-permute-start(bf16[32,4608]{1,0:T(8,128)(2,1)S(1)} %shard_map.85), channel_id=1, source_target_pairs={{0,2},{1,3},{2,0},{3,1},{4,6},{5,7},{6,4},{7,5},{8,10},{9,11},{10,... | collective-permute-start | bytes 884744 | tf_op jit(solution)/shard_map/ppermute | solution.py:33
  5.5 0.8 %fusion.33 = (s32[1,512]{1,0:T(1,128)S(1)}, s32[1,512]{1,0:T(1,128)S(1)}, s32[1,512]{1,0:T(1,128)S(1)}) fusion(s32[]{:T(128)S(6)} %axis_index.15, s32[8,512]{1,0:T(8,128)} %param.11, s32[]{:T(128)S(6)} %select_n.49, s32[8,512]{1,0:T(8,128)} %param.10), kind=kLoop, calls=%fused_computation.70 | loop fusion | flops 17408 | bytes 10248 | tf_op jit(solution)/shard_map/xor | solution.py:190
  6.2 0.0 copy-start
  6.2 4.8 %fusion.14.ends_bottom = bf16[512,512]{1,0:T(8,128)(2,1)S(1)} fusion(bf16[1,1024,4096]{2,1,0:T(8,128)(2,1)} %param.7, s32[512]{0:T(512)S(1)} %bitcast.37), kind=kOutput, calls=%fused_computation.11 | convolution fusion | flops 2149842944 | bytes 4720640 | tf_op jit(solution)/shard_map/dot_general | solution.py:28
  11.1 1.4 %collective-permute-done = bf16[32,4608]{1,0:T(8,128)(2,1)S(1)} collective-permute-done((bf16[32,4608]{1,0:T(8,128)(2,1)S(1)}, bf16[32,4608]{1,0:T(8,128)(2,1)S(1)}, u32[]{:S(2)}, u32[]{:S(2)}) %collective-permute-start) | collective-permute-done | bytes 294944 | tf_op jit(solution)/shard_map/ppermute | solution.py:33
  12.5 0.0 copy-start.1
  12.5 0.0 copy-start.3
  12.5 0.1 collective-permute-start.1
  12.6 0.0 copy-done
  12.6 2.5 %fusion.17.ends_top = bf16[512,512]{1,0:T(8,128)(2,1)S(1)} fusion(bf16[1,1024,4096]{2,1,0:T(8,128)(2,1)S(1)} %copy-done, s32[512]{0:T(512)S(1)} %bitcast.38), kind=kOutput, calls=%fused_computation.12 | convolution fusion | flops 2149842944 | bytes 4720640 | tf_op jit(solution)/shard_map/dot_general | solution.py:28
  15.1 0.0 collective-permute-done.1.far
  15.1 0.0 copy-done.1
  15.1 0.0 copy-done.3
  15.1 4.1 %shard_map.86 = (f32[128,1024]{1,0:T(8,128)S(1)}, f32[64,512]{1,0:T(8,128)S(1)}, f32[64,512]{1,0:T(8,128)S(1)}) custom-call(s32[8]{0:T(128)S(1)} %copy-done.3, bf16[64,4608]{1,0:T(8,128)(2,1)S(1)} %pad_maximum_fusion.near, bf16[64,4608]{1,0:T(8,128)(2,1)S(1)} %collective-permute-done.1.far, f32[32,512]{1,0:T(8,128)S(1)} %bitcast.33, ...), custom_call_target="tpu_custom_call" | custom-call | tf_op jit(solution)/shard_map/pallas_call | solution.py:101
  19.2 0.6 collective-permute-start.2
  19.8 1.0 %collective-permute-done.2 = f32[64,512]{1,0:T(8,128)S(1)} collective-permute-done((f32[64,512]{1,0:T(8,128)S(1)}, f32[64,512]{1,0:T(8,128)S(1)}, u32[]{:S(2)}, u32[]{:S(2)}) %collective-permute-start.2) | collective-permute-done | bytes 131104 | tf_op jit(solution)/shard_map/ppermute | solution.py:33
  20.8 1.8 %collective-permute-start.3 = (bf16[96,512]{1,0:T(8,128)(2,1)S(1)}, bf16[96,512]{1,0:T(8,128)(2,1)S(1)}, u32[]{:S(2)}, u32[]{:S(2)}) collective-permute-start(bf16[96,512]{1,0:T(8,128)(2,1)S(1)} %pad_maximum_fusion.1), channel_id=1, source_target_pairs={{0,2},{1,3},{2,0},{3,1},{4,6},{5,7},{6,4},{7,5},{8,10},{9,11},{10,... | collective-permute-start | bytes 294920 | tf_op jit(solution)/shard_map/ppermute | solution.py:33
  22.6 3.3 %collective-permute-done.3 = bf16[96,512]{1,0:T(8,128)(2,1)S(1)} collective-permute-done((bf16[96,512]{1,0:T(8,128)(2,1)S(1)}, bf16[96,512]{1,0:T(8,128)(2,1)S(1)}, u32[]{:S(2)}, u32[]{:S(2)}) %collective-permute-start.3) | collective-permute-done | bytes 98336 | tf_op jit(solution)/shard_map/ppermute | solution.py:33
  26.0 1.8 %collective-permute-start.4 = (bf16[64,512]{1,0:T(8,128)(2,1)S(1)}, bf16[64,512]{1,0:T(8,128)(2,1)S(1)}, u32[]{:S(2)}, u32[]{:S(2)}) collective-permute-start(bf16[64,512]{1,0:T(8,128)(2,1)S(1)} %get-tuple-element.30), channel_id=1, source_target_pairs={{0,4},{4,0},{8,12},{12,8},{16,20},{20,16},{24,28},{28,24},{1,5},{5... | collective-permute-start | bytes 196616 | tf_op jit(solution)/shard_map/ppermute | solution.py:33
  27.8 2.5 %collective-permute-done.4 = bf16[64,512]{1,0:T(8,128)(2,1)S(1)} collective-permute-done((bf16[64,512]{1,0:T(8,128)(2,1)S(1)}, bf16[64,512]{1,0:T(8,128)(2,1)S(1)}, u32[]{:S(2)}, u32[]{:S(2)}) %collective-permute-start.4) | collective-permute-done | bytes 65568 | tf_op jit(solution)/shard_map/ppermute | solution.py:33
  30.4 1.9 %collective-permute-start.5 = (bf16[64,512]{1,0:T(8,128)(2,1)S(1)}, bf16[64,512]{1,0:T(8,128)(2,1)S(1)}, u32[]{:S(2)}, u32[]{:S(2)}) collective-permute-start(bf16[64,512]{1,0:T(8,128)(2,1)S(1)} %broadcast_select_fusion.1), channel_id=1, source_target_pairs={{0,8},{4,12},{8,0},{12,4},{16,24},{20,28},{24,16},{28,20},{1,9},{5... | collective-permute-start | bytes 196616 | tf_op jit(solution)/shard_map/ppermute | solution.py:33
  32.2 2.5 %collective-permute-done.5 = bf16[64,512]{1,0:T(8,128)(2,1)S(1)} collective-permute-done((bf16[64,512]{1,0:T(8,128)(2,1)S(1)}, bf16[64,512]{1,0:T(8,128)(2,1)S(1)}, u32[]{:S(2)}, u32[]{:S(2)}) %collective-permute-start.5) | collective-permute-done | bytes 65568 | tf_op jit(solution)/shard_map/ppermute | solution.py:33
  34.7 3.1 %collective-permute-start.6 = (bf16[64,512]{1,0:T(8,128)(2,1)S(1)}, bf16[64,512]{1,0:T(8,128)(2,1)S(1)}, u32[]{:S(2)}, u32[]{:S(2)}) collective-permute-start(bf16[64,512]{1,0:T(8,128)(2,1)S(1)} %broadcast_select_fusion.3), channel_id=1, source_target_pairs={{0,16},{4,20},{8,24},{12,28},{16,0},{20,4},{24,8},{28,12},{1,17},{... | collective-permute-start | bytes 196616 | tf_op jit(solution)/shard_map/ppermute | solution.py:33
  37.8 2.2 %collective-permute-done.6 = bf16[64,512]{1,0:T(8,128)(2,1)S(1)} collective-permute-done((bf16[64,512]{1,0:T(8,128)(2,1)S(1)}, bf16[64,512]{1,0:T(8,128)(2,1)S(1)}, u32[]{:S(2)}, u32[]{:S(2)}) %collective-permute-start.6) | collective-permute-done | bytes 65568 | tf_op jit(solution)/shard_map/ppermute | solution.py:33
  40.0 0.3 subtract_convert_fusion
  40.4 0.1 collective-permute-start.7
  40.4 1.2 %collective-permute-done.7.far = bf16[64,512]{1,0:T(8,128)(2,1)S(1)} collective-permute-done((bf16[64,512]{1,0:T(8,128)(2,1)S(1)}, bf16[64,512]{1,0:T(8,128)(2,1)S(1)}, u32[]{:S(2)}, u32[]{:S(2)}) %collective-permute-start.7) | collective-permute-done | bytes 65568 | tf_op jit(solution)/shard_map/ppermute | solution.py:33
  41.7 1.4 %shard_map.87 = (bf16[128,1024]{1,0:T(8,128)(2,1)S(1)}, f32[64,512]{1,0:T(8,128)S(1)}, f32[64,512]{1,0:T(8,128)S(1)}) custom-call(s32[8]{0:T(128)S(1)} %copy-done.3, f32[128,1024]{1,0:T(8,128)S(1)} %get-tuple-element.13.base, bf16[64,512]{1,0:T(8,128)(2,1)S(1)} %get-tuple-element.38.near, bf16[64,512]{1,0:T(8,128)(2,1)S(1)} %collective-permute-done.7.far, ...), custom_call_target="tpu_custom_call" | custom-call | tf_op jit(solution)/shard_map/pallas_call | solution.py:145
  43.0 0.2 collective-permute-start.12
  43.3 1.2 %collective-permute-done.12 = f32[64,512]{1,0:T(8,128)S(1)} collective-permute-done((f32[64,512]{1,0:T(8,128)S(1)}, f32[64,512]{1,0:T(8,128)S(1)}, u32[]{:S(2)}, u32[]{:S(2)}) %collective-permute-start.12) | collective-permute-done | bytes 131104 | tf_op jit(solution)/shard_map/ppermute | solution.py:33
  44.5 1.7 %collective-permute-start.13 = (bf16[64,512]{1,0:T(8,128)(2,1)S(1)}, bf16[64,512]{1,0:T(8,128)(2,1)S(1)}, u32[]{:S(2)}, u32[]{:S(2)}) collective-permute-start(bf16[64,512]{1,0:T(8,128)(2,1)S(1)} %pad_maximum_fusion.2), channel_id=1, source_target_pairs={{0,2},{1,3},{2,0},{3,1},{4,6},{5,7},{6,4},{7,5},{8,10},{9,11},{10,... | collective-permute-start | bytes 196616 | tf_op jit(solution)/shard_map/ppermute | solution.py:33
  46.2 2.6 %collective-permute-done.13 = bf16[64,512]{1,0:T(8,128)(2,1)S(1)} collective-permute-done((bf16[64,512]{1,0:T(8,128)(2,1)S(1)}, bf16[64,512]{1,0:T(8,128)(2,1)S(1)}, u32[]{:S(2)}, u32[]{:S(2)}) %collective-permute-start.13) | collective-permute-done | bytes 65568 | tf_op jit(solution)/shard_map/ppermute | solution.py:33
  48.9 1.7 %collective-permute-start.14 = (bf16[64,512]{1,0:T(8,128)(2,1)S(1)}, bf16[64,512]{1,0:T(8,128)(2,1)S(1)}, u32[]{:S(2)}, u32[]{:S(2)}) collective-permute-start(bf16[64,512]{1,0:T(8,128)(2,1)S(1)} %pad_maximum_fusion.3), channel_id=1, source_target_pairs={{0,4},{4,0},{8,12},{12,8},{16,20},{20,16},{24,28},{28,24},{1,5},{5... | collective-permute-start | bytes 196616 | tf_op jit(solution)/shard_map/ppermute | solution.py:33
  50.6 1.3 %shard_map.89 = (f32[64,2048]{1,0:T(8,128)S(1)}, bf16[64,2048]{1,0:T(8,128)(2,1)S(1)}) custom-call(s32[8]{0:T(128)S(1)} %copy-done.3, bf16[128,1024]{1,0:T(8,128)(2,1)S(1)} %get-tuple-element.16.second, bf16[1024,4096]{1,0:T(8,128)(2,1)S(1)} %bitcast.30), custom_call_target="tpu_custom_call" | custom-call | tf_op jit(solution)/shard_map/pallas_call | solution.py:171
  51.9 0.1 collective-permute-start.10
  52.0 1.3 %shard_map.88 = (f32[64,2048]{1,0:T(8,128)S(1)}, bf16[64,2048]{1,0:T(8,128)(2,1)S(1)}) custom-call(s32[8]{0:T(128)S(1)} %copy-done.3, bf16[128,1024]{1,0:T(8,128)(2,1)S(1)} %get-tuple-element.16.second, bf16[1024,4096]{1,0:T(8,128)(2,1)S(1)} %bitcast.31), custom_call_target="tpu_custom_call" | custom-call | tf_op jit(solution)/shard_map/pallas_call | solution.py:171
  53.2 0.6 collective-permute-start.8
  53.8 0.0 collective-permute-done.14
  53.8 1.6 %collective-permute-start.15 = (bf16[64,512]{1,0:T(8,128)(2,1)S(1)}, bf16[64,512]{1,0:T(8,128)(2,1)S(1)}, u32[]{:S(2)}, u32[]{:S(2)}) collective-permute-start(bf16[64,512]{1,0:T(8,128)(2,1)S(1)} %broadcast_select_fusion), channel_id=1, source_target_pairs={{0,8},{4,12},{8,0},{12,4},{16,24},{20,28},{24,16},{28,20},{1,9},{5... | collective-permute-start | bytes 196616 | tf_op jit(solution)/shard_map/ppermute | solution.py:33
  55.5 0.0 collective-permute-done.10
  55.6 1.6 %collective-permute-start.11 = (bf16[32,2048]{1,0:T(8,128)(2,1)S(1)}, bf16[32,2048]{1,0:T(8,128)(2,1)S(1)}, u32[]{:S(2)}, u32[]{:S(2)}) collective-permute-start(bf16[32,2048]{1,0:T(8,128)(2,1)S(1)} %slice.130), channel_id=1, source_target_pairs={{0,2},{1,3},{2,0},{3,1},{4,6},{5,7},{6,4},{7,5},{8,10},{9,11},{10,... | collective-permute-start | bytes 393224 | tf_op jit(solution)/shard_map/ppermute | solution.py:33
  57.1 1.0 %collective-permute-done.15 = bf16[64,512]{1,0:T(8,128)(2,1)S(1)} collective-permute-done((bf16[64,512]{1,0:T(8,128)(2,1)S(1)}, bf16[64,512]{1,0:T(8,128)(2,1)S(1)}, u32[]{:S(2)}, u32[]{:S(2)}) %collective-permute-start.15) | collective-permute-done | bytes 65568 | tf_op jit(solution)/shard_map/ppermute | solution.py:33
  58.2 3.0 %collective-permute-start.16 = (bf16[64,512]{1,0:T(8,128)(2,1)S(1)}, bf16[64,512]{1,0:T(8,128)(2,1)S(1)}, u32[]{:S(2)}, u32[]{:S(2)}) collective-permute-start(bf16[64,512]{1,0:T(8,128)(2,1)S(1)} %broadcast_select_fusion.2), channel_id=1, source_target_pairs={{0,16},{4,20},{8,24},{12,28},{16,0},{20,4},{24,8},{28,12},{1,17},{... | collective-permute-start | bytes 196616 | tf_op jit(solution)/shard_map/ppermute | solution.py:33
  61.2 0.0 collective-permute-done.8
  61.2 0.1 convert_add_fusion.1
  61.3 1.6 %collective-permute-start.9 = (bf16[32,2048]{1,0:T(8,128)(2,1)S(1)}, bf16[32,2048]{1,0:T(8,128)(2,1)S(1)}, u32[]{:S(2)}, u32[]{:S(2)}) collective-permute-start(bf16[32,2048]{1,0:T(8,128)(2,1)S(1)} %slice.131), channel_id=1, source_target_pairs={{0,2},{1,3},{2,0},{3,1},{4,6},{5,7},{6,4},{7,5},{8,10},{9,11},{10,... | collective-permute-start | bytes 393224 | tf_op jit(solution)/shard_map/ppermute | solution.py:33
  62.8 0.8 %collective-permute-done.16 = bf16[64,512]{1,0:T(8,128)(2,1)S(1)} collective-permute-done((bf16[64,512]{1,0:T(8,128)(2,1)S(1)}, bf16[64,512]{1,0:T(8,128)(2,1)S(1)}, u32[]{:S(2)}, u32[]{:S(2)}) %collective-permute-start.16) | collective-permute-done | bytes 65568 | tf_op jit(solution)/shard_map/ppermute | solution.py:33
  63.7 0.3 fusion.20
  64.0 0.0 collective-permute-done.11
  64.0 0.7 %multiply_bitcast_fusion = (f32[1,32,512]{2,1,0:T(8,128)}, f32[1,32,512]{2,1,0:T(8,128)}) fusion(f32[64,512]{1,0:T(8,128)S(1)} %get-tuple-element.39, f32[32,512]{1,0:T(8,128)S(1)} %get-tuple-element.27, f32[64,512]{1,0:T(8,128)S(1)} %fusion.20), kind=kLoop, calls=%fused_computation.42 | loop fusion | flops 131072 | bytes 393216 | tf_op jit(solution)/shard_map/broadcast_in_dim | solution.py:255
  64.7 1.6 %collective-permute-done.9 = bf16[32,2048]{1,0:T(8,128)(2,1)S(1)} collective-permute-done((bf16[32,2048]{1,0:T(8,128)(2,1)S(1)}, bf16[32,2048]{1,0:T(8,128)(2,1)S(1)}, u32[]{:S(2)}, u32[]{:S(2)}) %collective-permute-start.9) | collective-permute-done | bytes 131104 | tf_op jit(solution)/shard_map/ppermute | solution.py:33
  66.3 0.8 %maximum_bitcast_fusion = f32[1,32,4096]{2,1,0:T(8,128)} fusion(f32[32,2048]{1,0:T(8,128)S(1)} %slice_add_fusion, f32[32,2048]{1,0:T(8,128)S(1)} %slice_add_fusion.1), kind=kLoop, calls=%fused_computation.17 | loop fusion | flops 131072 | bytes 1048576 | tf_op jit(solution)/shard_map/broadcast_in_dim | solution.py:254
  (25 shorter events, 0.5 us)
Async XLA Ops:
  0.6 0.7 copy-start.2
  2.4 10.1 %collective-permute-start = (bf16[32,4608]{1,0:T(8,128)(2,1)S(1)}, bf16[32,4608]{1,0:T(8,128)(2,1)S(1)}, u32[]{:S(2)}, u32[]{:S(2)}) collective-permute-start(bf16[32,4608]{1,0:T(8,128)(2,1)S(1)} %shard_map.85), channel_id=1, source_target_pairs={{0,2},{1,3},{2,0},{3,1},{4,6},{5,7},{6,4},{7,5},{8,10},{9,11},{10,... | collective-permute-start | bytes 884744 | tf_op jit(solution)/shard_map/ppermute | solution.py:33
  6.2 6.4 %copy-start = (bf16[1,1024,4096]{2,1,0:T(8,128)(2,1)S(1)}, bf16[1,1024,4096]{2,1,0:T(8,128)(2,1)}, u32[]{:S(2)}) copy-start(bf16[1,1024,4096]{2,1,0:T(8,128)(2,1)} %param.7) | copy-start | bytes 25165828
  12.5 2.6 %copy-start.1 = (f32[1,32,512]{2,1,0:T(8,128)S(1)}, f32[1,32,512]{2,1,0:T(8,128)}, u32[]{:S(2)}) copy-start(f32[1,32,512]{2,1,0:T(8,128)} %param.8) | copy-start | bytes 196612
  12.5 2.6 %copy-start.3 = (s32[8]{0:T(128)S(1)}, s32[8]{0:T(128)}, u32[]{:S(2)}) copy-start(s32[8]{0:T(128)} %area_size.9) | copy-start | bytes 100
  12.5 2.6 %collective-permute-start.1 = (bf16[64,4608]{1,0:T(8,128)(2,1)S(1)}, bf16[64,4608]{1,0:T(8,128)(2,1)S(1)}, u32[]{:S(2)}, u32[]{:S(2)}) collective-permute-start(bf16[64,4608]{1,0:T(8,128)(2,1)S(1)} %pad_maximum_fusion.near), channel_id=1, source_target_pairs={{0,1},{1,0},{2,3},{3,2},{4,5},{5,4},{6,7},{7,6},{8,9},{9,8},{10,11... | collective-permute-start | bytes 1769480 | tf_op jit(solution)/shard_map/ppermute | solution.py:33
  19.2 1.5 %collective-permute-start.2 = (f32[64,512]{1,0:T(8,128)S(1)}, f32[64,512]{1,0:T(8,128)S(1)}, u32[]{:S(2)}, u32[]{:S(2)}) collective-permute-start(f32[64,512]{1,0:T(8,128)S(1)} %get-tuple-element.15), channel_id=1, source_target_pairs={{0,1},{1,0},{2,3},{3,2},{4,5},{5,4},{6,7},{7,6},{8,9},{9,8},{10,11... | collective-permute-start | bytes 393224 | tf_op jit(solution)/shard_map/ppermute | solution.py:33
  20.8 5.1 %collective-permute-start.3 = (bf16[96,512]{1,0:T(8,128)(2,1)S(1)}, bf16[96,512]{1,0:T(8,128)(2,1)S(1)}, u32[]{:S(2)}, u32[]{:S(2)}) collective-permute-start(bf16[96,512]{1,0:T(8,128)(2,1)S(1)} %pad_maximum_fusion.1), channel_id=1, source_target_pairs={{0,2},{1,3},{2,0},{3,1},{4,6},{5,7},{6,4},{7,5},{8,10},{9,11},{10,... | collective-permute-start | bytes 294920 | tf_op jit(solution)/shard_map/ppermute | solution.py:33
  26.0 4.3 %collective-permute-start.4 = (bf16[64,512]{1,0:T(8,128)(2,1)S(1)}, bf16[64,512]{1,0:T(8,128)(2,1)S(1)}, u32[]{:S(2)}, u32[]{:S(2)}) collective-permute-start(bf16[64,512]{1,0:T(8,128)(2,1)S(1)} %get-tuple-element.30), channel_id=1, source_target_pairs={{0,4},{4,0},{8,12},{12,8},{16,20},{20,16},{24,28},{28,24},{1,5},{5... | collective-permute-start | bytes 196616 | tf_op jit(solution)/shard_map/ppermute | solution.py:33
  30.4 4.3 %collective-permute-start.5 = (bf16[64,512]{1,0:T(8,128)(2,1)S(1)}, bf16[64,512]{1,0:T(8,128)(2,1)S(1)}, u32[]{:S(2)}, u32[]{:S(2)}) collective-permute-start(bf16[64,512]{1,0:T(8,128)(2,1)S(1)} %broadcast_select_fusion.1), channel_id=1, source_target_pairs={{0,8},{4,12},{8,0},{12,4},{16,24},{20,28},{24,16},{28,20},{1,9},{5... | collective-permute-start | bytes 196616 | tf_op jit(solution)/shard_map/ppermute | solution.py:33
  34.7 5.3 %collective-permute-start.6 = (bf16[64,512]{1,0:T(8,128)(2,1)S(1)}, bf16[64,512]{1,0:T(8,128)(2,1)S(1)}, u32[]{:S(2)}, u32[]{:S(2)}) collective-permute-start(bf16[64,512]{1,0:T(8,128)(2,1)S(1)} %broadcast_select_fusion.3), channel_id=1, source_target_pairs={{0,16},{4,20},{8,24},{12,28},{16,0},{20,4},{24,8},{28,12},{1,17},{... | collective-permute-start | bytes 196616 | tf_op jit(solution)/shard_map/ppermute | solution.py:33
  40.4 1.3 %collective-permute-start.7 = (bf16[64,512]{1,0:T(8,128)(2,1)S(1)}, bf16[64,512]{1,0:T(8,128)(2,1)S(1)}, u32[]{:S(2)}, u32[]{:S(2)}) collective-permute-start(bf16[64,512]{1,0:T(8,128)(2,1)S(1)} %get-tuple-element.38.near), channel_id=1, source_target_pairs={{0,1},{1,0},{2,3},{3,2},{4,5},{5,4},{6,7},{7,6},{8,9},{9,8},{10,11... | collective-permute-start | bytes 196616 | tf_op jit(solution)/shard_map/ppermute | solution.py:33
  43.0 1.4 %collective-permute-start.12 = (f32[64,512]{1,0:T(8,128)S(1)}, f32[64,512]{1,0:T(8,128)S(1)}, u32[]{:S(2)}, u32[]{:S(2)}) collective-permute-start(f32[64,512]{1,0:T(8,128)S(1)} %get-tuple-element.22), channel_id=1, source_target_pairs={{0,1},{1,0},{2,3},{3,2},{4,5},{5,4},{6,7},{7,6},{8,9},{9,8},{10,11... | collective-permute-start | bytes 393224 | tf_op jit(solution)/shard_map/ppermute | solution.py:33
  44.5 4.3 %collective-permute-start.13 = (bf16[64,512]{1,0:T(8,128)(2,1)S(1)}, bf16[64,512]{1,0:T(8,128)(2,1)S(1)}, u32[]{:S(2)}, u32[]{:S(2)}) collective-permute-start(bf16[64,512]{1,0:T(8,128)(2,1)S(1)} %pad_maximum_fusion.2), channel_id=1, source_target_pairs={{0,2},{1,3},{2,0},{3,1},{4,6},{5,7},{6,4},{7,5},{8,10},{9,11},{10,... | collective-permute-start | bytes 196616 | tf_op jit(solution)/shard_map/ppermute | solution.py:33
  48.9 4.9 %collective-permute-start.14 = (bf16[64,512]{1,0:T(8,128)(2,1)S(1)}, bf16[64,512]{1,0:T(8,128)(2,1)S(1)}, u32[]{:S(2)}, u32[]{:S(2)}) collective-permute-start(bf16[64,512]{1,0:T(8,128)(2,1)S(1)} %pad_maximum_fusion.3), channel_id=1, source_target_pairs={{0,4},{4,0},{8,12},{12,8},{16,20},{20,16},{24,28},{28,24},{1,5},{5... | collective-permute-start | bytes 196616 | tf_op jit(solution)/shard_map/ppermute | solution.py:33
  51.9 3.6 %collective-permute-start.10 = (bf16[64,2048]{1,0:T(8,128)(2,1)S(1)}, bf16[64,2048]{1,0:T(8,128)(2,1)S(1)}, u32[]{:S(2)}, u32[]{:S(2)}) collective-permute-start(bf16[64,2048]{1,0:T(8,128)(2,1)S(1)} %get-tuple-element.20), channel_id=1, source_target_pairs={{0,1},{1,0},{2,3},{3,2},{4,5},{5,4},{6,7},{7,6},{8,9},{9,8},{10,11... | collective-permute-start | bytes 786440 | tf_op jit(solution)/shard_map/ppermute | solution.py:33
  53.2 7.9 %collective-permute-start.8 = (bf16[64,2048]{1,0:T(8,128)(2,1)S(1)}, bf16[64,2048]{1,0:T(8,128)(2,1)S(1)}, u32[]{:S(2)}, u32[]{:S(2)}) collective-permute-start(bf16[64,2048]{1,0:T(8,128)(2,1)S(1)} %get-tuple-element.18), channel_id=1, source_target_pairs={{0,1},{1,0},{2,3},{3,2},{4,5},{5,4},{6,7},{7,6},{8,9},{9,8},{10,11... | collective-permute-start | bytes 786440 | tf_op jit(solution)/shard_map/ppermute | solution.py:33
  53.8 4.3 %collective-permute-start.15 = (bf16[64,512]{1,0:T(8,128)(2,1)S(1)}, bf16[64,512]{1,0:T(8,128)(2,1)S(1)}, u32[]{:S(2)}, u32[]{:S(2)}) collective-permute-start(bf16[64,512]{1,0:T(8,128)(2,1)S(1)} %broadcast_select_fusion), channel_id=1, source_target_pairs={{0,8},{4,12},{8,0},{12,4},{16,24},{20,28},{24,16},{28,20},{1,9},{5... | collective-permute-start | bytes 196616 | tf_op jit(solution)/shard_map/ppermute | solution.py:33
  55.6 8.4 %collective-permute-start.11 = (bf16[32,2048]{1,0:T(8,128)(2,1)S(1)}, bf16[32,2048]{1,0:T(8,128)(2,1)S(1)}, u32[]{:S(2)}, u32[]{:S(2)}) collective-permute-start(bf16[32,2048]{1,0:T(8,128)(2,1)S(1)} %slice.130), channel_id=1, source_target_pairs={{0,2},{1,3},{2,0},{3,1},{4,6},{5,7},{6,4},{7,5},{8,10},{9,11},{10,... | collective-permute-start | bytes 393224 | tf_op jit(solution)/shard_map/ppermute | solution.py:33
  58.2 5.5 %collective-permute-start.16 = (bf16[64,512]{1,0:T(8,128)(2,1)S(1)}, bf16[64,512]{1,0:T(8,128)(2,1)S(1)}, u32[]{:S(2)}, u32[]{:S(2)}) collective-permute-start(bf16[64,512]{1,0:T(8,128)(2,1)S(1)} %broadcast_select_fusion.2), channel_id=1, source_target_pairs={{0,16},{4,20},{8,24},{12,28},{16,0},{20,4},{24,8},{28,12},{1,17},{... | collective-permute-start | bytes 196616 | tf_op jit(solution)/shard_map/ppermute | solution.py:33
  61.3 5.0 %collective-permute-start.9 = (bf16[32,2048]{1,0:T(8,128)(2,1)S(1)}, bf16[32,2048]{1,0:T(8,128)(2,1)S(1)}, u32[]{:S(2)}, u32[]{:S(2)}) collective-permute-start(bf16[32,2048]{1,0:T(8,128)(2,1)S(1)} %slice.131), channel_id=1, source_target_pairs={{0,2},{1,3},{2,0},{3,1},{4,6},{5,7},{6,4},{7,5},{8,10},{9,11},{10,... | collective-permute-start | bytes 393224 | tf_op jit(solution)/shard_map/ppermute | solution.py:33
